TPU v7x, 32 devices: a whole 2x2x4 slice. The times are simulated.
32 devices in a mesh: ens: 2 (over x), lat: 16 (over z, y, core).
Axes of the slice: x: 2, y: 2, z: 4, core: 2. Of those that a mesh axis runs over, the one named last changes fastest.
Arguments:
- state: bfloat16 [256, 1440, 128], P(('ens', 'lat')), parts along dimension 0, may hold values from -6 to 6
- inner_weight: bfloat16 [2, 1152, 512], replicated, may hold values from -0.1875 to 0.1875
- outer_weight: bfloat16 [2, 512, 128], replicated, may hold values from -0.25 to 0.25
- surface_proj: bfloat16 [2, 128, 4], replicated, may hold values from -0.5 to 0.5
- forcing_in: bfloat16 [2, 4, 512], replicated, may hold values from -3 to 3
- margin_rows: int32 [2, 64, 3], replicated, may hold values from 0 to 63, as said below
- margin_weights: float32 [2, 64, 3], replicated, may hold values from 0.2 to 1
- wet_mask: int32 [64, 1440], replicated, may hold values 0 or 1
Outputs:
- next_state: bfloat16 [256, 1440, 128], P(('ens', 'lat')), parts along dimension 0
There are 2 independent parts, one for each index of `ens`. A program takes and returns all parts, laid end to end along the dimension named above; an argument that names none is the same for every part. Nothing has to cross between parts.
Inputs may be any that keep to these rules, and one draw needn't show every extreme that they name: `margin_rows`: every entry of row r of either component lies between ((r) // 8 - 1) * 8 and ((r) // 8 + 2) * 8 - 1 (within 0 to 63); r + k * 8 with k = -1 is reached by the first row of each block of 8 rows and k = 1 plus 8 - 1 by the last, unless the component ends there.
All inputs are finite; a program needn't handle non-finite values.
Results may differ from a plain program's by a relative error of at most 0.0085.
Values may be sent and summed in bfloat16 or wider, within the bound.
No kernel may reach another device: no remote copies, remote signals or barrier semaphores. Data moves between devices by JAX's collectives and lax.ppermute only.
A program may use at most 128 MiB of HBM per device.

v0:
```python
import jax
import jax.numpy as jnp
from jax import lax
from jax.sharding import PartitionSpec as P


def passed_along(block, axis, distance):
    devices = range(lax.axis_size(axis))
    route = [((i - distance) % len(devices), i) for i in devices]
    return lax.ppermute(block, axis, route)


def padded_2(block, sides, width):
    for axis, dim in sides:
        count = lax.axis_size(axis)
        forward = [(i, i + 1) for i in range(count - 1)]
        forward.append((count - 1, 0))
        backward = [(target, source) for source, target in forward]
        low = lax.ppermute(
            lax.slice_in_dim(block, block.shape[dim] - width, None, axis=dim), axis, forward
        )
        high = lax.ppermute(lax.slice_in_dim(block, 0, width, axis=dim), axis, backward)
        block = jnp.concatenate([low, block, high], axis=dim)
    return block


def shards(
    state,
    inner_weight,
    outer_weight,
    surface_proj,
    forcing_in,
    margin_rows,
    margin_weights,
    wet_mask,
):
    half_axis = lax.axis_size("lat") // 2
    quarter = half_axis // 2
    row_count = state.shape[0]
    lon_cells = state.shape[1]
    flux_count = surface_proj.shape[2]
    device_index = lax.axis_index("lat")
    moved_index = (device_index + quarter) % (2 * half_axis)
    component = moved_index // half_axis
    position = moved_index % half_axis
    inner = lax.dynamic_index_in_dim(inner_weight, component, 0, keepdims=False)
    outer = lax.dynamic_index_in_dim(outer_weight, component, 0, keepdims=False)
    projection = lax.dynamic_index_in_dim(surface_proj, component, 0, keepdims=False)
    forcing_map = lax.dynamic_index_in_dim(forcing_in, component, 0, keepdims=False)
    table_all = lax.dynamic_index_in_dim(margin_rows, component, 0, keepdims=False)
    fraction_all = lax.dynamic_index_in_dim(margin_weights, component, 0, keepdims=False)
    margin_table = lax.dynamic_slice_in_dim(table_all, position * row_count, row_count, 0)
    fractions = lax.dynamic_slice_in_dim(fraction_all, position * row_count, row_count, 0)
    wet_rows = lax.dynamic_slice_in_dim(wet_mask, position * row_count, row_count, 0).astype(
        jnp.float32
    )
    wet_factor = jnp.where(component == 1, wet_rows, jnp.ones_like(wet_rows))
    surface = jnp.einsum("rlc,cf->rfl", state, projection, preferred_element_type=jnp.float32)
    surface = (surface * wet_factor[:, None, :]).astype(jnp.bfloat16)
    surface = surface.reshape(row_count, flux_count * lon_cells)
    pieces_list = []
    for offset in (1, 0, -1):
        pieces_list.append(passed_along(surface, "lat", half_axis + offset))
    window = jnp.concatenate(pieces_list, axis=0)
    local_rows = margin_table - (position - 1) * row_count
    picked = jnp.take(window, local_rows, axis=0)
    forcing = jnp.einsum("rk,rkx->rx", fractions, picked.astype(jnp.float32))
    forcing = forcing.reshape(row_count, flux_count, lon_cells)
    padded = padded_2(state, (("lat", 0),), 1)
    south_keep = jnp.where(position == 0, 0.0, 1.0).astype(jnp.bfloat16)
    north_keep = jnp.where(position == half_axis - 1, 0.0, 1.0).astype(jnp.bfloat16)
    padded = jnp.concatenate(
        [padded[:1] * south_keep, padded[1:-1], padded[-1:] * north_keep], axis=0
    )
    taps_list = []
    for row_shift in range(3):
        block_rows = padded[row_shift : row_shift + row_count]
        for lon_shift in range(3):
            taps_list.append(jnp.roll(block_rows, 1 - lon_shift, axis=1))
    patches = jnp.concatenate(taps_list, axis=-1)
    pre_act = jnp.einsum("rlk,kh->rlh", patches, inner, preferred_element_type=jnp.float32)
    pre_act = pre_act + jnp.einsum("rfl,fh->rlh", forcing, forcing_map.astype(jnp.float32))
    hidden = jax.nn.silu(pre_act).astype(jnp.bfloat16)
    update = jnp.einsum("rlh,hc->rlc", hidden, outer, preferred_element_type=jnp.float32)
    result = (state.astype(jnp.float32) + update) * wet_factor[:, :, None]
    return result.astype(jnp.bfloat16)


def solution(mesh):
    placed = (P(("ens", "lat"), None, None), P(), P(), P(), P(), P(), P(), P())
    return jax.shard_map(
        shards, mesh=mesh, in_specs=placed, out_specs=P(("ens", "lat"), None, None), check_vma=False
    )
```

profile of v0, /device:TPU:1, one launch (start us, length us, event | category | flops | bytes accessed | tf_op | source)
XLA Modules:
  0.0 90.1 jit_solution(8991803836357413821)
XLA Ops:
  0.0 0.0 copy-start
  0.0 0.0 copy-start.3
  0.0 0.0 copy-start.4
  0.1 1.0 %convert_select_fusion = f32[8,1440]{1,0:T(8,128)S(1)} fusion(s32[64,1440]{1,0:T(8,128)} %param.15, s32[]{:T(128)S(6)} %select_n.80, pred[]{:T(512)S(6)} %eq.14), kind=kLoop, calls=%fused_computation.46 | loop fusion | flops 23040 | bytes 92165 | tf_op jit(solution)/shard_map/jit(_where)/select_n | solution.py:57
  1.0 2.8 %fusion.17 = bf16[8,4,1440]{2,1,0:T(4,128)(2,1)S(1)} fusion(bf16[8,1440,128]{2,1,0:T(8,128)(2,1)} %param.8, f32[8,1440]{1,0:T(8,128)S(1)} %convert_select_fusion, bf16[2,128,4]{1,2,0:T(4,128)(2,1)} %param.11, s32[]{:T(128)S(6)} %select_n.78), kind=kOutput, calls=%fused_computation.33 | convolution fusion | flops 11888640 | bytes 3088388 | tf_op jit(solution)/shard_map/rlc,cf->rfl/dot_general | solution.py:58
  3.8 0.2 reshape.39
  4.0 4.7 %collective-permute-start.2 = (bf16[8,5760]{1,0:T(8,128)(2,1)S(1)}, bf16[8,5760]{1,0:T(8,128)(2,1)S(1)}, u32[]{:S(2)}, u32[]{:S(2)}) collective-permute-start(bf16[8,5760]{1,0:T(8,128)(2,1)S(1)} %reshape.39), channel_id=1, source_target_pairs={{7,0},{8,1},{9,2},{10,3},{11,4},{12,5},{13,6},{14,7},{15,8},{0,9},... | collective-permute-start | bytes 276488 | tf_op jit(solution)/shard_map/ppermute | solution.py:10
  8.7 0.1 collective-permute-start.3
  8.8 1.4 %collective-permute-start.4 = (bf16[8,5760]{1,0:T(8,128)(2,1)S(1)}, bf16[8,5760]{1,0:T(8,128)(2,1)S(1)}, u32[]{:S(2)}, u32[]{:S(2)}) collective-permute-start(bf16[8,5760]{1,0:T(8,128)(2,1)S(1)} %reshape.39), channel_id=1, source_target_pairs={{9,0},{10,1},{11,2},{12,3},{13,4},{14,5},{15,6},{0,7},{1,8},{2,9},... | collective-permute-start | bytes 276488 | tf_op jit(solution)/shard_map/ppermute | solution.py:10
  10.1 2.0 %fusion.37 = (bf16[1,1440,128]{2,1,0:T(8,128)(2,1)}, bf16[1,1440,128]{2,1,0:T(8,128)(2,1)}) fusion(bf16[8,1440,128]{2,1,0:T(8,128)(2,1)} %param.8), kind=kLoop, calls=%fused_computation.64 | loop fusion | bytes 1474560 | tf_op jit(solution)/shard_map/slice | solution.py:22
  12.2 0.4 collective-permute-start.1
  12.6 2.0 %collective-permute-start = (bf16[1,1440,128]{2,1,0:T(8,128)(2,1)}, bf16[1,1440,128]{2,1,0:T(8,128)(2,1)S(1)}, u32[]{:S(2)}, u32[]{:S(2)}) collective-permute-start(bf16[1,1440,128]{2,1,0:T(8,128)(2,1)} %get-tuple-element.16), channel_id=1, source_target_pairs={{0,1},{1,2},{2,3},{3,4},{4,5},{5,6},{6,7},{7,8},{8,9},{9,10},{10,1... | collective-permute-start | bytes 1105928 | tf_op jit(solution)/shard_map/ppermute | solution.py:19
  14.6 0.7 fusion.38
  15.4 0.0 copy-done.3
  15.4 0.1 compare_select_fusion
  15.5 0.1 copy.12
  15.5 0.1 reshape.43
  15.6 0.1 copy.11
  15.7 0.0 copy-done.4
  15.7 0.1 constant_dynamic-slice_fusion.2
  15.8 0.1 copy.15
  15.9 0.0 collective-permute-done.2
  15.9 3.7 %collective-permute-done.3 = bf16[8,5760]{1,0:T(8,128)(2,1)S(1)} collective-permute-done((bf16[8,5760]{1,0:T(8,128)(2,1)S(1)}, bf16[8,5760]{1,0:T(8,128)(2,1)S(1)}, u32[]{:S(2)}, u32[]{:S(2)}) %collective-permute-start.3) | collective-permute-done | bytes 92192 | tf_op jit(solution)/shard_map/ppermute | solution.py:10
  19.6 4.8 %collective-permute-done.4 = bf16[8,5760]{1,0:T(8,128)(2,1)S(1)} collective-permute-done((bf16[8,5760]{1,0:T(8,128)(2,1)S(1)}, bf16[8,5760]{1,0:T(8,128)(2,1)S(1)}, u32[]{:S(2)}, u32[]{:S(2)}) %collective-permute-start.4) | collective-permute-done | bytes 92192 | tf_op jit(solution)/shard_map/ppermute | solution.py:10
  24.4 0.7 gather_fusion
  25.2 0.9 reshape.42
  26.0 1.4 %fusion.20 = bf16[8,1,5760]{2,1,0:T(2,128)(2,1)S(1)} fusion(f32[8,3,1]{1,2,0:T(1,128)S(1)} %bitcast.44, bf16[8,3,5760]{2,1,0:T(4,128)(2,1)} %reshape.42, pred[8,3]{1,0:T(8,128)(4,1)S(1)} %copy.11), kind=kOutput, calls=%fused_computation.36 | convolution fusion | flops 414720 | bytes 368760 | tf_op jit(solution)/shard_map/rk,rkx->rx/dot_general | solution.py:67
  27.5 0.1 reshape.40
  27.6 0.0 copy-done.2
  27.6 0.0 copy-start.1
  27.6 9.5 %fusion.26 = f32[8,1440,512]{2,1,0:T(8,128)} fusion(bf16[8,4,1440]{2,1,0:T(4,128)(2,1)S(1)} %reshape.40, bf16[2,4,512]{2,1,0:T(4,128)(2,1)S(1)} %copy-done.2, s32[]{:T(128)S(6)} %select_n.78), kind=kOutput, calls=%fused_computation.51 | convolution fusion | flops 47185920 | bytes 23695364 | tf_op jit(solution)/shard_map/rfl,fh->rlh/dot_general | solution.py:82
  37.1 0.0 collective-permute-done.1
  37.1 1.0 %broadcast_multiply_fusion = bf16[1,1440,128]{2,1,0:T(8,128)(2,1)S(1)} fusion(bf16[1,1440,128]{2,1,0:T(8,128)(2,1)} %collective-permute-done.1, bf16[]{:T(256)S(6)} %select_n.76), kind=kLoop, calls=%fused_computation.42 | loop fusion | flops 184320 | bytes 737282 | tf_op jit(solution)/shard_map/mul | solution.py:73
  38.2 0.0 collective-permute-done
  38.2 0.0 copy-done.1
  38.2 2.6 %fusion = (bf16[8,1439,128]{2,1,0:T(8,128)(2,1)S(1)}, bf16[8,1439,128]{2,1,0:T(8,128)(2,1)S(1)}, bf16[8,1439,128]{2,1,0:T(8,128)(2,1)S(1)}, bf16[8,1439,128]{2,1...) fusion(bf16[1,1440,128]{2,1,0:T(8,128)(2,1)S(1)} %broadcast_multiply_fusion, ...), kind=kLoop, calls=%fused_computation.9 | loop fusion | flops 5894144 | bytes 27267072 | tf_op jit(solution)/shard_map/concatenate | solution.py:72
  40.8 2.6 %fusion.15 = bf16[8,1440,1152]{2,1,0:T(8,128)(2,1)} fusion(bf16[8,1440,128]{2,1,0:T(8,128)(2,1)S(1)} %copy-done.1, bf16[1,1440,128]{2,1,0:T(8,128)(2,1)S(1)} %broadcast_multiply_fusion.1, bf16[8,1439,128]{2,1,0:T(8,128)(2,1)S(1)} %get-tuple-element.13), kind=kLoop, calls=%fused_computation.28 | loop fusion | flops 8847359 | bytes 9213952
  43.5 1.9 %fusion.7 = bf16[8,1440,1152]{2,1,0:T(8,128)(2,1)} fusion(bf16[8,1440,1152]{2,1,0:T(8,128)(2,1)} %fusion.15, bf16[1,1440,128]{2,1,0:T(8,128)(2,1)S(1)} %broadcast_multiply_fusion.1, bf16[8,1440,128]{2,1,0:T(8,128)(2,1)S(1)} %copy-done.1), kind=kLoop, calls=%fused_computation.16 | loop fusion | flops 5898240 | bytes 6266880
  45.4 2.0 %fusion.13 = bf16[8,1440,1152]{2,1,0:T(8,128)(2,1)} fusion(bf16[8,1440,1152]{2,1,0:T(8,128)(2,1)} %fusion.7, bf16[8,1440,128]{2,1,0:T(8,128)(2,1)S(1)} %copy-done.1, bf16[1,1440,128]{2,1,0:T(8,128)(2,1)S(1)} %broadcast_multiply_fusion.1, bf16[8,1439,128]{2,1,0:T(8,128)(2,1)S(1)} %get-tuple-element.14), kind=kLoop, calls=%fused_computation.25 | loop fusion | flops 8847360 | bytes 9213952
  47.4 2.5 %maximum_dynamic-update-slice_fusion.1 = bf16[8,1440,1152]{2,1,0:T(8,128)(2,1)} fusion(bf16[8,1440,1152]{2,1,0:T(8,128)(2,1)} %fusion.13, bf16[8,1439,128]{2,1,0:T(8,128)(2,1)S(1)} %get-tuple-element.12, bf16[8,1,128]{2,1,0:T(2,128)(2,1)S(1)} %get-tuple-element.18), kind=kLoop, calls=%fused_computation.30 | loop fusion | flops 5898240 | bytes 5898240
  49.9 1.8 %constant_dynamic-update-slice_fusion = bf16[8,1440,1152]{2,1,0:T(8,128)(2,1)} fusion(bf16[8,1440,1152]{2,1,0:T(8,128)(2,1)} %maximum_dynamic-update-slice_fusion.1, bf16[8,1440,128]{2,1,0:T(8,128)(2,1)S(1)} %copy-done.1), kind=kLoop, calls=%fused_computation.47 | loop fusion | bytes 5898240
  51.7 1.9 %maximum_dynamic-update-slice_fusion = bf16[8,1440,1152]{2,1,0:T(8,128)(2,1)} fusion(bf16[8,1440,1152]{2,1,0:T(8,128)(2,1)} %constant_dynamic-update-slice_fusion, bf16[8,1,128]{2,1,0:T(2,128)(2,1)S(1)} %get-tuple-element.17, bf16[8,1439,128]{2,1,0:T(8,128)(2,1)S(1)} %get-tuple-element.11), kind=kLoop, calls=%fused_computation.29 | loop fusion | flops 5898240 | bytes 5898240
  53.7 2.5 %fusion.11 = bf16[8,1440,1152]{2,1,0:T(8,128)(2,1)} fusion(bf16[8,1440,1152]{2,1,0:T(8,128)(2,1)} %maximum_dynamic-update-slice_fusion, bf16[1,1440,128]{2,1,0:T(8,128)(2,1)S(1)} %broadcast_multiply_fusion, bf16[8,1440,128]{2,1,0:T(8,128)(2,1)S(1)} %copy-done.1, bf16[8,1439,128]{2,1,0:T(8,128)(2,1)S(1)} %get-tuple-element.8), kind=kLoop, calls=%fused_computation.22 | loop fusion | flops 8847360 | bytes 9213952
  56.1 2.0 %fusion.3 = bf16[8,1440,1152]{2,1,0:T(8,128)(2,1)} fusion(bf16[8,1440,1152]{2,1,0:T(8,128)(2,1)} %fusion.11, bf16[1,1440,128]{2,1,0:T(8,128)(2,1)S(1)} %broadcast_multiply_fusion, bf16[8,1440,128]{2,1,0:T(8,128)(2,1)S(1)} %copy-done.1), kind=kLoop, calls=%fused_computation.12 | loop fusion | flops 5898240 | bytes 6266880
  58.1 2.0 %fusion.9 = bf16[8,1440,1152]{2,1,0:T(8,128)(2,1)} fusion(bf16[8,1440,1152]{2,1,0:T(8,128)(2,1)} %fusion.3, bf16[1,1440,128]{2,1,0:T(8,128)(2,1)S(1)} %broadcast_multiply_fusion, bf16[8,1440,128]{2,1,0:T(8,128)(2,1)S(1)} %copy-done.1, bf16[8,1439,128]{2,1,0:T(8,128)(2,1)S(1)} %get-tuple-element.7), kind=kLoop, calls=%fused_computation.19 | loop fusion | flops 8847360 | bytes 9213952 | tf_op jit(solution)/shard_map/concatenate | solution.py:80
  60.0 0.0 copy-done
  60.0 0.0 copy-done.5
  60.0 30.0 %multiply_convert_fusion.1 = bf16[8,1440,128]{2,1,0:T(8,128)(2,1)} fusion(bf16[8,1440,128]{2,1,0:T(8,128)(2,1)} %param.8, f32[8,1440]{1,0:T(8,128)S(1)} %convert_select_fusion, bf16[2,512,128]{2,1,0:T(8,128)(2,1)S(1)} %copy-done.5, s32[]{:T(128)S(6)} %select_n.78, f32[8,1440,512]{2,1,0:T(8,128)} %fusion.26, bf16[8,1440,1152]{2,1,0:T(8,128)(2,1)} %fusion.9, ...), kind=kOutput, calls=%fused_computation.2 | convolution fusion | flops 15140782080 | bytes 57394176 | tf_op jit(solution)/shard_map/rlh,hc->rlc/dot_general | solution.py:84
  (7 shorter events, 0.1 us)
Async XLA Ops:
  0.0 60.0 %copy-start = (bf16[2,1152,512]{2,1,0:T(8,128)(2,1)S(1)}, bf16[2,1152,512]{2,1,0:T(8,128)(2,1)}, u32[]{:S(2)}) copy-start(bf16[2,1152,512]{2,1,0:T(8,128)(2,1)} %param.9) | copy-start | bytes 7077892
  0.0 15.4 %copy-start.3 = (s32[2,64,3]{1,0,2:T(2,128)S(1)}, s32[2,64,3]{1,0,2:T(2,128)}, u32[]{:S(2)}) copy-start(s32[2,64,3]{1,0,2:T(2,128)} %param.13) | copy-start | bytes 4612
  0.0 15.7 %copy-start.4 = (f32[2,64,3]{1,0,2:T(2,128)S(1)}, f32[2,64,3]{1,0,2:T(2,128)}, u32[]{:S(2)}) copy-start(f32[2,64,3]{1,0,2:T(2,128)} %param.14) | copy-start | bytes 4612
  4.0 11.9 %collective-permute-start.2 = (bf16[8,5760]{1,0:T(8,128)(2,1)S(1)}, bf16[8,5760]{1,0:T(8,128)(2,1)S(1)}, u32[]{:S(2)}, u32[]{:S(2)}) collective-permute-start(bf16[8,5760]{1,0:T(8,128)(2,1)S(1)} %reshape.39), channel_id=1, source_target_pairs={{7,0},{8,1},{9,2},{10,3},{11,4},{12,5},{13,6},{14,7},{15,8},{0,9},... | collective-permute-start | bytes 276488 | tf_op jit(solution)/shard_map/ppermute | solution.py:10
  8.7 10.9 %collective-permute-start.3 = (bf16[8,5760]{1,0:T(8,128)(2,1)S(1)}, bf16[8,5760]{1,0:T(8,128)(2,1)S(1)}, u32[]{:S(2)}, u32[]{:S(2)}) collective-permute-start(bf16[8,5760]{1,0:T(8,128)(2,1)S(1)} %reshape.39), channel_id=1, source_target_pairs={{8,0},{9,1},{10,2},{11,3},{12,4},{13,5},{14,6},{15,7},{0,8},{1,9},... | collective-permute-start | bytes 276488 | tf_op jit(solution)/shard_map/ppermute | solution.py:10
  8.8 15.6 %collective-permute-start.4 = (bf16[8,5760]{1,0:T(8,128)(2,1)S(1)}, bf16[8,5760]{1,0:T(8,128)(2,1)S(1)}, u32[]{:S(2)}, u32[]{:S(2)}) collective-permute-start(bf16[8,5760]{1,0:T(8,128)(2,1)S(1)} %reshape.39), channel_id=1, source_target_pairs={{9,0},{10,1},{11,2},{12,3},{13,4},{14,5},{15,6},{0,7},{1,8},{2,9},... | collective-permute-start | bytes 276488 | tf_op jit(solution)/shard_map/ppermute | solution.py:10
  12.2 15.5 %copy-start.2 = (bf16[2,4,512]{2,1,0:T(4,128)(2,1)S(1)}, bf16[2,4,512]{2,1,0:T(4,128)(2,1)}, u32[]{:S(2)}) copy-start(bf16[2,4,512]{2,1,0:T(4,128)(2,1)} %param.12) | copy-start | bytes 24580
  12.2 25.0 %collective-permute-start.1 = (bf16[1,1440,128]{2,1,0:T(8,128)(2,1)}, bf16[1,1440,128]{2,1,0:T(8,128)(2,1)}, u32[]{:S(2)}, u32[]{:S(2)}) collective-permute-start(bf16[1,1440,128]{2,1,0:T(8,128)(2,1)} %get-tuple-element.15), channel_id=1, source_target_pairs={{1,0},{2,1},{3,2},{4,3},{5,4},{6,5},{7,6},{8,7},{9,8},{10,9},{11,1... | collective-permute-start | bytes 1105928 | tf_op jit(solution)/shard_map/ppermute | solution.py:22
  12.6 25.6 %collective-permute-start = (bf16[1,1440,128]{2,1,0:T(8,128)(2,1)}, bf16[1,1440,128]{2,1,0:T(8,128)(2,1)S(1)}, u32[]{:S(2)}, u32[]{:S(2)}) collective-permute-start(bf16[1,1440,128]{2,1,0:T(8,128)(2,1)} %get-tuple-element.16), channel_id=1, source_target_pairs={{0,1},{1,2},{2,3},{3,4},{4,5},{5,6},{6,7},{7,8},{8,9},{9,10},{10,1... | collective-permute-start | bytes 1105928 | tf_op jit(solution)/shard_map/ppermute | solution.py:19
  27.6 10.6 %copy-start.1 = (bf16[8,1440,128]{2,1,0:T(8,128)(2,1)S(1)}, bf16[8,1440,128]{2,1,0:T(8,128)(2,1)}, u32[]{:S(2)}) copy-start(bf16[8,1440,128]{2,1,0:T(8,128)(2,1)} %param.8) | copy-start | bytes 8847364
  58.1 2.0 %copy-start.5 = (bf16[2,512,128]{2,1,0:T(8,128)(2,1)S(1)}, bf16[2,512,128]{2,1,0:T(8,128)(2,1)}, u32[]{:S(2)}) copy-start(bf16[2,512,128]{2,1,0:T(8,128)(2,1)} %param.10) | copy-start | bytes 786436
where the time goes:
time: 90.4 us; the launch traced here: 90.1 us
  matrix products  43.7 us (48%)
  other arithmetic  22.1 us (24%)
  starting transfers between devices  8.54 us (9%)
  waiting for transfers between devices  8.49 us (9%)
  local copies, waits for them, and re-layouts  7.01 us (8%)
    dot_general x1, matrix products, shards(): jnp.einsum('rlh,hc->rlc', hidden, outer, preferred_element_type=jnp.float32)  30 us
    unnamed x7, other arithmetic  15.4 us
    dot_general x1, matrix products, shards(): jnp.einsum('rfl,fh->rlh', forcing, forcing_map.astype(jnp.float32))  9.5 us
    ppermute x3, waiting for transfers between devices, passed_along(): return lax.ppermute(block, axis, route)  8.49 us
    ppermute x3, starting transfers between devices, passed_along(): return lax.ppermute(block, axis, route)  6.12 us
    dot_general x1, matrix products, shards(): jnp.einsum('rlc,cf->rfl', state, projection, preferred_element_type=jnp.f...  2.81 us
    concatenate x1, other arithmetic, shards(): jnp.concatenate([padded[:1] * south_keep, padded[1:-1], padded[-1:] * nor...  2.62 us
    slice x1, local copies, waits for them, and re-layouts, padded_2(): lax.slice_in_dim(block, 0, width, axis=dim)  2.03 us
  transfers between devices with their start and end apart: 5, of which 2 were waited for; matrix products, arithmetic and copies ran while one was open for 19% of the time, Pallas kernels for 0%

commit v1 on v0

v1 whole, which is shorter than its diff:
```python
import functools

import jax
import jax.numpy as jnp
from jax import lax
from jax.experimental import pallas as pl
from jax.experimental.pallas import tpu as pltpu
from jax.sharding import PartitionSpec as P

BF = jnp.bfloat16
F32 = jnp.float32
GROUPS = 4
FIRST_PAIRS = 2


def dot(a, b):
    return jnp.dot(a, b, preferred_element_type=F32)


def lane(shape):
    return lax.broadcasted_iota(jnp.int32, shape, len(shape) - 1)


def sublane(shape):
    return lax.broadcasted_iota(jnp.int32, shape, len(shape) - 2)


def limits(mib):
    return pltpu.CompilerParams(
        dimension_semantics=("arbitrary",), vmem_limit_bytes=mib << 20
    )


def surface_kernel(rows, lon, group, fluxes, where, x_ref, proj_ref, wet_ref, out_ref, acc, wetf):
    step = pl.program_id(0)
    channels = x_ref.shape[2]
    spread = (lane((fluxes, 128)) % fluxes == sublane((fluxes, 128))).astype(BF)
    tiled = dot(proj_ref[0], spread).astype(BF)

    @pl.when(step == 0)
    def _():
        acc[...] = jnp.zeros_like(acc)

    owner = lane((channels, 128)) // fluxes
    for g in range(GROUPS):
        size = min(group, lon - g * group)
        span = slice(g * group, g * group + size)
        lhs = jnp.concatenate([x_ref[0, span, :], x_ref[1, span, :]], axis=1)
        halves = [
            jnp.where(owner == g * rows + 2 * step + k, tiled, jnp.zeros_like(tiled)) for k in (0, 1)
        ]
        acc[0:size, :] += dot(lhs, jnp.concatenate(halves, axis=0))

    @pl.when(step == pl.num_programs(0) - 1)
    def _():
        wetf[...] = jnp.zeros_like(wetf)
        wetf[:, 0:lon] = wet_ref[...].astype(F32)
        mask = jnp.zeros_like(acc)
        for g in range(GROUPS):
            pick = (lane((rows, 128)) // fluxes == g * rows + sublane((rows, 128))).astype(F32)
            mask += lax.dot_general(
                wetf[:, g * group : (g + 1) * group], pick, (((0,), (0,)), ((), ())),
                preferred_element_type=F32,
            )
        mask = jnp.where(where[0] == 1, mask, jnp.ones_like(mask))
        out_ref[...] = (acc[...] * mask).astype(BF)


def surfaces(where, state, surface_proj, wet_mask, group):
    rows, lon, channels = state.shape
    fluxes = surface_proj.shape[2]
    return pl.pallas_call(
        functools.partial(surface_kernel, rows, lon, group, fluxes),
        grid_spec=pltpu.PrefetchScalarGridSpec(
            num_scalar_prefetch=1,
            grid=(rows // 2,),
            in_specs=[
                pl.BlockSpec((2, lon, channels), lambda i, s: (i, 0, 0)),
                pl.BlockSpec((1, channels, fluxes), lambda i, s: (s[0], 0, 0)),
                pl.BlockSpec((rows, lon), lambda i, s: (s[1], 0)),
            ],
            out_specs=pl.BlockSpec((group, 128), lambda i, s: (0, 0)),
            scratch_shapes=[
                pltpu.VMEM((group, 128), F32),
                pltpu.VMEM((rows, GROUPS * group), F32),
            ],
        ),
        out_shape=jax.ShapeDtypeStruct((group, 128), BF),
        compiler_params=limits(16),
        name="surface_fields",
    )(where, state, surface_proj, wet_mask)


def partial_kernel(first, pairs, lon, edges, *refs):
    if edges:
        where, d0, d1, d2, d3, w_ref, low_ref, high_ref, out_ref, up_ref, down_ref, tf, wy, wm = refs
    else:
        where, d0, d1, d2, d3, w_ref, _, out_ref, tf, wy, wm = refs
    step = pl.program_id(0)
    pair = step + first

    def tap(a, b):
        return w_ref[0, pl.ds((a * 3 + b) * 128, 128), :].astype(F32) * 0.5

    @pl.when(step == 0)
    def _():
        for k, (a, b) in enumerate(((0, 0), (0, 2), (1, 1), (2, 1))):
            wy[0, k * 128 : (k + 1) * 128, :] = tap(a, b).astype(BF)
        for k, (a, b) in enumerate(((2, 0), (2, 2), (0, 1), (1, 1))):
            wy[1, k * 128 : (k + 1) * 128, :] = tap(a, b).astype(BF)
        for k, b in enumerate((0, 2)):
            ends = tap(0, b) + tap(2, b)
            wm[0, k * 128 : (k + 1) * 128, :] = (0.5 * (ends + tap(1, b))).astype(BF)
            wm[1, k * 128 : (k + 1) * 128, :] = (0.5 * (ends - tap(1, b))).astype(BF)
        if edges:
            up_ref[0:lon, :] = high_ref[0]
            down_ref[0:lon, :] = low_ref[0]

    south = jnp.where(pair == 0, 0.0, 1.0)
    north = jnp.where(pair == pairs - 1, 0.0, 1.0)
    x1 = d1[0].astype(F32)
    x2 = d2[0].astype(F32)
    for p, t in enumerate(
        (d0[0].astype(F32) * south - x2, x1 + x2, x2 - x1, d3[0].astype(F32) * north - x1)
    ):
        tf[p, 8 : 8 + lon, :] = t
        tf[p, 7:8, :] = t[lon - 1 : lon]
        tf[p, 8 + lon : 9 + lon, :] = t[0:1]

    def sides(p):
        return [tf[p, 7 : 7 + lon, :].astype(BF), tf[p, 9 : 9 + lon, :].astype(BF)]

    own = [d1[0], d2[0]]
    m1 = dot(jnp.concatenate(sides(1), axis=1), wm[0])
    m2 = dot(jnp.concatenate(sides(2), axis=1), wm[1])
    out_ref[0] = (dot(jnp.concatenate(sides(0) + own, axis=1), wy[0]) + (m1 + m2)).astype(BF)
    out_ref[1] = (dot(jnp.concatenate(sides(3) + own, axis=1), wy[1]) + (m1 - m2)).astype(BF)


def partials(where, state, inner_weight, first, count, group, earlier=None):
    rows, lon, channels = state.shape
    depth, hidden = inner_weight.shape[1:]
    edges = earlier is None

    def row(offset):
        def index(i, s):
            return (jnp.clip(2 * (i + first) + offset, 0, rows - 1), 0, 0)

        return pl.BlockSpec((1, lon, channels), index)

    in_specs = [row(k) for k in (-1, 0, 1, 2)]
    in_specs.append(pl.BlockSpec((1, depth, hidden), lambda i, s: (s[0], 0, 0)))
    out_specs = [pl.BlockSpec((2, lon, hidden), lambda i, s: (i + first, 0, 0))]
    out_shape = [jax.ShapeDtypeStruct((rows, lon, hidden), BF)]
    operands = [state] * 4 + [inner_weight]
    aliases = {}
    if edges:
        in_specs.append(pl.BlockSpec((1, lon, channels), lambda i, s: (0, 0, 0)))
        in_specs.append(pl.BlockSpec((1, lon, channels), lambda i, s: (rows - 1, 0, 0)))
        operands += [state, state]
        for _ in range(2):
            out_specs.append(pl.BlockSpec((lon + group, channels), lambda i, s: (0, 0)))
            out_shape.append(jax.ShapeDtypeStruct((lon + group, channels), BF))
    else:
        in_specs.append(pl.BlockSpec(memory_space=pl.ANY))
        operands.append(earlier)
        aliases = {6: 0}
    return pl.pallas_call(
        functools.partial(partial_kernel, first, rows // 2, lon, edges),
        grid_spec=pltpu.PrefetchScalarGridSpec(
            num_scalar_prefetch=1,
            grid=(count,),
            in_specs=in_specs,
            out_specs=out_specs,
            scratch_shapes=[
                pltpu.VMEM((4, lon + 16, channels), F32),
                pltpu.VMEM((2, 4 * channels, hidden), BF),
                pltpu.VMEM((2, 2 * channels, hidden), BF),
            ],
        ),
        out_shape=out_shape,
        input_output_aliases=aliases,
        compiler_params=limits(52),
        cost_estimate=pl.CostEstimate(
            flops=count * 2 * lon * 6 * channels * hidden * 2,
            bytes_accessed=count * 2 * lon * (hidden + 2 * channels) * 2,
            transcendentals=0,
        ),
        name="own_rows",
    )(where, *operands)


def finish_kernel(
    rows, lon, group, fluxes, where, x_ref, near_ref, part_ref, low_ref, high_ref, mid_ref, wl_ref, wh_ref,
    f_ref, o_ref, wet_ref, table, weights, out_ref, halo, window, we, spread, wett, wetf,
):
    r = pl.program_id(0)
    parity = r % 2

    @pl.when(r == 0)
    def _():
        for e, (side, w_ref) in enumerate(((low_ref, wl_ref), (high_ref, wh_ref))):
            v = side[0:lon, :].astype(F32)
            halo[e, 8 : 8 + lon, :] = v
            halo[e, 7:8, :] = v[lon - 1 : lon]
            halo[e, 8 + lon : 9 + lon, :] = v[0:1]
            for k, b in enumerate((0, 2, 1)):
                tap = w_ref[0, b * 128 : (b + 1) * 128, :].astype(F32) * 0.5
                we[e, k * 128 : (k + 1) * 128, :] = tap.astype(BF)
        packs = [
            low_ref[lon : lon + group, :].astype(F32),
            mid_ref[...].astype(F32),
            high_ref[lon : lon + group, :].astype(F32),
        ]
        for g in range(GROUPS):
            size = min(group, lon - g * group)
            held = lane((group, 128)) // (rows * fluxes)
            total = jnp.zeros((group, 128), F32)
            for w, pack in enumerate(packs):
                shift = (rows * fluxes * (w - g)) % 128
                moved = pltpu.roll(pack, shift, 1) if shift else pack
                total = jnp.where(held == w, moved, total)
            window[g * group : g * group + size, :] = total[0:size].astype(BF)
        at = sublane((128, spread.shape[1])) % fluxes
        total = jnp.zeros(spread.shape, F32)
        for f in range(fluxes):
            total = jnp.where(at == f, f_ref[0, f : f + 1, :].astype(F32) * 0.5, total)
        spread[...] = total
        wetf[...] = jnp.zeros_like(wetf)
        wetf[0:rows, 0:lon] = jnp.where(where[0] == 1, wet_ref[...].astype(F32), 1.0)
        for c in range(wetf.shape[1] // 128):
            wett[c * 128 : (c + 1) * 128, :] = wetf[:, c * 128 : (c + 1) * 128].T

    slot = sublane(spread.shape) // fluxes
    share = jnp.zeros(spread.shape, F32)
    for m in range(table.shape[2]):
        local = table[0, r, m] - (where[1] - 1) * rows
        share += jnp.where(slot == local, weights[0, r, m], 0.0)
    we[parity, 384:512, :] = (share * spread[...]).astype(BF)

    def close(total):
        total = total + part_ref[0].astype(F32)
        act = (total + total * jnp.tanh(total)).astype(BF)
        value = x_ref[0].astype(F32) + dot(act, o_ref[0])
        pick = lane((lon, 128)) == r
        keep = jnp.max(jnp.where(pick, wett[0:lon, :], 0.0), axis=1, keepdims=True)
        out_ref[0] = jnp.where(keep > 0.5, value, 0.0).astype(BF)

    edge = jnp.logical_or(r == 0, r == rows - 1)

    @pl.when(edge)
    def _():
        lhs = [halo[parity, k : k + lon, :].astype(BF) for k in (7, 9, 8)] + [window[...]]
        close(dot(jnp.concatenate(lhs, axis=1), we[parity]))

    @pl.when(jnp.logical_not(edge))
    def _():
        close(dot(jnp.concatenate([near_ref[0], window[...]], axis=1), we[parity, 256:512, :]))


def finish(where, state, part, low, high, mid, inner_weight, forcing_in, outer_weight, wet_mask, table, weights):
    rows, lon, channels = state.shape
    hidden = inner_weight.shape[2]
    fluxes = forcing_in.shape[1]
    group = mid.shape[0]
    margins = table.shape[2]

    def near(r, s):
        return (jnp.clip(r - 1 + 2 * (r % 2), 0, rows - 1), 0, 0)

    def whole(i, s):
        return (0, 0)

    return pl.pallas_call(
        functools.partial(finish_kernel, rows, lon, group, fluxes),
        grid_spec=pltpu.PrefetchScalarGridSpec(
            num_scalar_prefetch=1,
            grid=(rows,),
            in_specs=[
                pl.BlockSpec((1, lon, channels), lambda r, s: (r, 0, 0)),
                pl.BlockSpec((1, lon, channels), near),
                pl.BlockSpec((1, lon, hidden), lambda r, s: (r, 0, 0)),
                pl.BlockSpec((lon + group, channels), whole),
                pl.BlockSpec((lon + group, channels), whole),
                pl.BlockSpec((group, channels), whole),
                pl.BlockSpec((1, 3 * channels, hidden), lambda r, s: (s[0], 0, 0)),
                pl.BlockSpec((1, 3 * channels, hidden), lambda r, s: (s[0], 2, 0)),
                pl.BlockSpec((1, fluxes, hidden), lambda r, s: (s[0], 0, 0)),
                pl.BlockSpec((1, hidden, channels), lambda r, s: (s[0], 0, 0)),
                pl.BlockSpec((rows, lon), lambda r, s: (s[1], 0)),
                pl.BlockSpec((1, rows, margins), lambda r, s: (s[0], s[1], 0), memory_space=pltpu.SMEM),
                pl.BlockSpec((1, rows, margins), lambda r, s: (s[0], s[1], 0), memory_space=pltpu.SMEM),
            ],
            out_specs=pl.BlockSpec((1, lon, channels), lambda r, s: (r, 0, 0)),
            scratch_shapes=[
                pltpu.VMEM((2, lon + 16, channels), F32),
                pltpu.VMEM((lon, 128), BF),
                pltpu.VMEM((2, 512, hidden), BF),
                pltpu.VMEM((128, hidden), F32),
                pltpu.VMEM((GROUPS * group, 128), F32),
                pltpu.VMEM((128, GROUPS * group), F32),
            ],
        ),
        out_shape=jax.ShapeDtypeStruct((rows, lon, channels), BF),
        compiler_params=limits(52),
        name="finish_rows",
    )(
        where, state, state, part, low, high, mid, inner_weight, inner_weight, forcing_in, outer_weight,
        wet_mask, table, weights,
    )


def shards(state, inner_weight, outer_weight, surface_proj, forcing_in, margin_rows, margin_weights, wet_mask):
    count = lax.axis_size("lat")
    half = count // 2
    quarter = half // 2
    lon = state.shape[1]
    group = -(-lon // (GROUPS * 128)) * 128
    moved = (lax.axis_index("lat") + quarter) % count
    where = jnp.where(lax.iota(jnp.int32, 2) == 0, moved // half, moved % half)

    def component(i):
        return ((i + quarter) % count) // half

    def beside(block, distance):
        route = [(i, (i + distance) % count) for i in range(count)]
        route = [(i, j) for i, j in route if component(i) == component(j)]
        return lax.ppermute(block, "lat", route)

    pack = surfaces(where, state, surface_proj, wet_mask, group)
    mid = lax.ppermute(pack, "lat", [(i, (i + half) % count) for i in range(count)])
    part, up, down = partials(where, state, inner_weight, 0, FIRST_PAIRS, group)
    mid, part = lax.optimization_barrier((mid, part))
    up = lax.dynamic_update_slice(up, mid, (lon, 0))
    down = lax.dynamic_update_slice(down, mid, (lon, 0))
    low = beside(up, 1)
    high = beside(down, -1)
    (part,) = partials(
        where, state, inner_weight, FIRST_PAIRS, state.shape[0] // 2 - FIRST_PAIRS, group, part
    )
    return finish(
        where, state, part, low, high, mid, inner_weight, forcing_in, outer_weight, wet_mask,
        margin_rows, margin_weights,
    )


def solution(mesh):
    placed = (P(("ens", "lat"), None, None), P(), P(), P(), P(), P(), P(), P())
    return jax.shard_map(
        shards, mesh=mesh, in_specs=placed, out_specs=P(("ens", "lat"), None, None), check_vma=False
    )
```

time: 90.4 us -> 55.2 us (0.61)
  the two profiles are of different devices: /device:TPU:1 before, /device:TPU:0 now
where the time goes in v1:
time: 55.2 us; the launch traced here: 54.7 us
  Pallas kernels  38.3 us (69%)
  starting transfers between devices  12.4 us (22%)
  local copies, waits for them, and re-layouts  3.91 us (7%)
    pallas_call x2, Pallas kernels, partials(): pl.pallas_call(functools.partial(partial_kernel, first, rows // 2, lon, e...  19.4 us
    pallas_call x1, Pallas kernels, finish(): pl.pallas_call(functools.partial(finish_kernel, rows, lon, group, fluxes)...  15.9 us
    ppermute x2, starting transfers between devices, beside(): return lax.ppermute(block, 'lat', route)  8.26 us
    ppermute x1, starting transfers between devices, shards(): lax.ppermute(pack, 'lat', [(i, (i + half) % count) for i in range(count)])  4.1 us
    unnamed x17, local copies, waits for them, and re-layouts  3.88 us
    pallas_call x1, Pallas kernels, surfaces(): pl.pallas_call(functools.partial(surface_kernel, rows, lon, group, fluxes...  3 us
  transfers between devices with their start and end apart: 3, of which 0 were waited for; matrix products, arithmetic and copies ran while one was open for 0% of the time, Pallas kernels for 35%

profile of v1, /device:TPU:0, one launch (start us, length us, event | category | flops | bytes accessed | tf_op | source)
XLA Modules:
  0.0 54.7 jit_solution(8374584719846859648)
XLA Ops:
  0.0 0.8 %copy.10.proj_ref = bf16[2,128,4]{2,1,0:T(8,128)(2,1)S(1)} copy(bf16[2,128,4]{1,2,0:T(4,128)(2,1)} %param.11) | data formatting | bytes 4096 | tf_op args[3]
  0.8 0.0 copy-start
  0.9 1.8 %copy-done = bf16[8,1440,128]{2,1,0:T(8,128)(2,1)S(1)} copy-done((bf16[8,1440,128]{2,1,0:T(8,128)(2,1)S(1)}, bf16[8,1440,128]{2,1,0:T(8,128)(2,1)}, u32[]{:S(2)}) %copy-start) | copy-done | bytes 2949144
  2.7 0.0 copy-start.1
  2.7 1.0 %copy-done.1 = s32[64,1440]{1,0:T(8,128)S(1)} copy-done((s32[64,1440]{1,0:T(8,128)S(1)}, s32[64,1440]{1,0:T(8,128)}, u32[]{:S(2)}) %copy-start.1) | copy-done | bytes 368664
  3.7 3.0 %surface_fields.1 = bf16[384,128]{1,0:T(8,128)(2,1)S(1)} custom-call(s32[2]{0:T(128)S(1)} %compare_select_fusion.where.refs_0_, bf16[8,1440,128]{2,1,0:T(8,128)(2,1)S(1)} %copy-done, bf16[2,128,4]{2,1,0:T(8,128)(2,1)S(1)} %copy.10.proj_ref, s32[64,1440]{1,0:T(8,128)S(1)} %copy-done.1), custom_call_target="tpu_custom_call" | custom-call | tf_op jit(solution)/shard_map/surface_fields/pallas_call | solution.py:72
  6.7 0.0 copy-start.5
  6.7 0.0 copy-start.6
  6.7 4.1 %collective-permute-start = (bf16[384,128]{1,0:T(8,128)(2,1)S(1)}, bf16[384,128]{1,0:T(8,128)(2,1)S(1)}, u32[]{:S(2)}, u32[]{:S(2)}) collective-permute-start(bf16[384,128]{1,0:T(8,128)(2,1)S(1)} %surface_fields.1), channel_id=1, source_target_pairs={{0,8},{1,9},{2,10},{3,11},{4,12},{5,13},{6,14},{7,15},{8,0},{9,1},... | collective-permute-start | bytes 294920 | tf_op jit(solution)/shard_map/ppermute | solution.py:331
  10.8 9.9 %own_rows.2 = (bf16[8,1440,512]{2,1,0:T(8,128)(2,1)}, bf16[1824,128]{1,0:T(8,128)(2,1)S(1)}, bf16[1824,128]{1,0:T(8,128)(2,1)S(1)}) custom-call(s32[2]{0:T(128)S(1)} %compare_select_fusion.where.refs_0_, bf16[8,1440,128]{2,1,0:T(8,128)(2,1)} %near_ref.1, bf16[8,1440,128]{2,1,0:T(8,128)(2,1)} %near_ref.1, bf16[8,1440,128]{2,1,0:T(8,128)(2,1)} %near_ref.1, ...), custom_call_target="tpu_custom_call" | custom-call | flops 4529848320 | bytes 8847360 | tf_op jit(solution)/shard_map/own_rows/pallas_call | solution.py:168
  20.7 0.0 collective-permute-done.mid_ref
  20.7 1.9 %collective-permute-start.1 = (bf16[1824,128]{1,0:T(8,128)(2,1)S(1)}, bf16[1824,128]{1,0:T(8,128)(2,1)S(1)}, u32[]{:S(2)}, u32[]{:S(2)}) collective-permute-start(bf16[1824,128]{1,0:T(8,128)(2,1)S(1)} %get-tuple-element.16), channel_id=1, source_target_pairs={{0,1},{1,2},{2,3},{4,5},{5,6},{6,7},{7,8},{8,9},{9,10},{10,11},{12... | collective-permute-start | bytes 1400840 | tf_op jit(solution)/shard_map/ppermute | solution.py:328
  22.6 6.3 %collective-permute-start.2 = (bf16[1824,128]{1,0:T(8,128)(2,1)S(1)}, bf16[1824,128]{1,0:T(8,128)(2,1)S(1)}, u32[]{:S(2)}, u32[]{:S(2)}) collective-permute-start(bf16[1824,128]{1,0:T(8,128)(2,1)S(1)} %get-tuple-element.15), channel_id=1, source_target_pairs={{0,15},{1,0},{2,1},{3,2},{5,4},{6,5},{7,6},{8,7},{9,8},{10,9},{11,... | collective-permute-start | bytes 1400840 | tf_op jit(solution)/shard_map/ppermute | solution.py:328
  29.0 0.0 copy-done.5
  29.0 0.1 copy.11.table
  29.1 0.0 copy-done.6
  29.1 0.1 copy.12.weights
  29.2 0.0 copy-start.2
  29.2 0.0 copy-start.3
  29.3 0.0 copy-start.4
  29.3 9.5 %own_rows.3.part_ref = bf16[8,1440,512]{2,1,0:T(8,128)(2,1)} custom-call(s32[2]{0:T(128)S(1)} %compare_select_fusion.where.refs_0_, bf16[8,1440,128]{2,1,0:T(8,128)(2,1)} %near_ref.1, bf16[8,1440,128]{2,1,0:T(8,128)(2,1)} %near_ref.1, bf16[8,1440,128]{2,1,0:T(8,128)(2,1)} %near_ref.1, ...), custom_call_target="tpu_custom_call", output_to_operand_aliasing={{}: (6, {})} | custom-call | flops 4529848320 | bytes 8847360 | tf_op jit(solution)/shard_map/own_rows/pallas_call | solution.py:168
  38.8 0.0 collective-permute-done.1.low_ref
  38.8 0.0 collective-permute-done.2.high_ref
  38.8 0.0 copy-done.2
  38.8 0.0 copy-done.3
  38.8 0.0 copy-done.4
  38.8 15.9 %finish_rows.1 = bf16[8,1440,128]{2,1,0:T(8,128)(2,1)} custom-call(s32[2]{0:T(128)S(1)} %compare_select_fusion.where.refs_0_, bf16[8,1440,128]{2,1,0:T(8,128)(2,1)} %near_ref.1, bf16[8,1440,128]{2,1,0:T(8,128)(2,1)} %near_ref.1, bf16[8,1440,512]{2,1,0:T(8,128)(2,1)} %own_rows.3.part_ref, bf16[1824,128]{1,0:T(8,128)(2,1)S(1)} %collective-permute-done.1.low_ref, ...), custom_call_target="tpu_custom_call" | custom-call | tf_op jit(solution)/shard_map/finish_rows/pallas_call | solution.py:274
  (2 shorter events, 0.0 us)
Async XLA Ops:
  0.8 1.8 %copy-start = (bf16[8,1440,128]{2,1,0:T(8,128)(2,1)S(1)}, bf16[8,1440,128]{2,1,0:T(8,128)(2,1)}, u32[]{:S(2)}) copy-start(bf16[8,1440,128]{2,1,0:T(8,128)(2,1)} %near_ref.1) | copy-start | bytes 8847364
  2.7 1.0 %copy-start.1 = (s32[64,1440]{1,0:T(8,128)S(1)}, s32[64,1440]{1,0:T(8,128)}, u32[]{:S(2)}) copy-start(s32[64,1440]{1,0:T(8,128)} %wet_ref.3) | copy-start | bytes 1105924
  6.7 22.3 %copy-start.5 = (s32[2,64,3]{1,0,2:T(2,128)S(1)}, s32[2,64,3]{1,0,2:T(2,128)}, u32[]{:S(2)}) copy-start(s32[2,64,3]{1,0,2:T(2,128)} %param.13) | copy-start | bytes 4612
  6.7 22.4 %copy-start.6 = (f32[2,64,3]{1,0,2:T(2,128)S(1)}, f32[2,64,3]{1,0,2:T(2,128)}, u32[]{:S(2)}) copy-start(f32[2,64,3]{1,0,2:T(2,128)} %param.14) | copy-start | bytes 4612
  6.7 14.0 %collective-permute-start = (bf16[384,128]{1,0:T(8,128)(2,1)S(1)}, bf16[384,128]{1,0:T(8,128)(2,1)S(1)}, u32[]{:S(2)}, u32[]{:S(2)}) collective-permute-start(bf16[384,128]{1,0:T(8,128)(2,1)S(1)} %surface_fields.1), channel_id=1, source_target_pairs={{0,8},{1,9},{2,10},{3,11},{4,12},{5,13},{6,14},{7,15},{8,0},{9,1},... | collective-permute-start | bytes 294920 | tf_op jit(solution)/shard_map/ppermute | solution.py:331
  20.7 18.1 %collective-permute-start.1 = (bf16[1824,128]{1,0:T(8,128)(2,1)S(1)}, bf16[1824,128]{1,0:T(8,128)(2,1)S(1)}, u32[]{:S(2)}, u32[]{:S(2)}) collective-permute-start(bf16[1824,128]{1,0:T(8,128)(2,1)S(1)} %get-tuple-element.16), channel_id=1, source_target_pairs={{0,1},{1,2},{2,3},{4,5},{5,6},{6,7},{7,8},{8,9},{9,10},{10,11},{12... | collective-permute-start | bytes 1400840 | tf_op jit(solution)/shard_map/ppermute | solution.py:328
  22.6 16.2 %collective-permute-start.2 = (bf16[1824,128]{1,0:T(8,128)(2,1)S(1)}, bf16[1824,128]{1,0:T(8,128)(2,1)S(1)}, u32[]{:S(2)}, u32[]{:S(2)}) collective-permute-start(bf16[1824,128]{1,0:T(8,128)(2,1)S(1)} %get-tuple-element.15), channel_id=1, source_target_pairs={{0,15},{1,0},{2,1},{3,2},{5,4},{6,5},{7,6},{8,7},{9,8},{10,9},{11,... | collective-permute-start | bytes 1400840 | tf_op jit(solution)/shard_map/ppermute | solution.py:328
  29.2 9.6 %copy-start.2 = (s32[64,1440]{1,0:T(8,128)S(1)}, s32[64,1440]{1,0:T(8,128)}, u32[]{:S(2)}) copy-start(s32[64,1440]{1,0:T(8,128)} %wet_ref.3) | copy-start | bytes 1105924
  29.2 9.6 %copy-start.3 = (bf16[2,512,128]{2,1,0:T(8,128)(2,1)S(1)}, bf16[2,512,128]{2,1,0:T(8,128)(2,1)}, u32[]{:S(2)}) copy-start(bf16[2,512,128]{2,1,0:T(8,128)(2,1)} %o_ref.1) | copy-start | bytes 786436
  29.3 9.6 %copy-start.4 = (bf16[2,4,512]{2,1,0:T(4,128)(2,1)S(1)}, bf16[2,4,512]{2,1,0:T(4,128)(2,1)}, u32[]{:S(2)}) copy-start(bf16[2,4,512]{2,1,0:T(4,128)(2,1)} %f_ref.1) | copy-start | bytes 24580

commit v2 on v1

v2 whole, which is shorter than its diff:
```python
import functools

import jax
import jax.numpy as jnp
from jax import lax
from jax.experimental import pallas as pl
from jax.experimental.pallas import tpu as pltpu
from jax.sharding import PartitionSpec as P

BF = jnp.bfloat16
F32 = jnp.float32
GROUPS = 4
FIRST_PAIRS = 2


def dot(a, b):
    return jnp.dot(a, b, preferred_element_type=F32)


def lane(shape):
    return lax.broadcasted_iota(jnp.int32, shape, len(shape) - 1)


def sublane(shape):
    return lax.broadcasted_iota(jnp.int32, shape, len(shape) - 2)


def limits(mib):
    return pltpu.CompilerParams(
        dimension_semantics=("arbitrary",), vmem_limit_bytes=mib << 20
    )


def surface_kernel(
    rows, lon, group, fluxes, where, x_ref, proj_ref, wet_ref, out_ref, xv_ref, up_ref, down_ref, acc, wetf
):
    step = pl.program_id(0)
    channels = x_ref.shape[2]
    spread = (lane((fluxes, 128)) % fluxes == sublane((fluxes, 128))).astype(BF)
    tiled = lax.dot_general(
        proj_ref[0], spread, (((0,), (0,)), ((), ())), preferred_element_type=F32
    ).astype(BF)
    xv_ref[2 * step] = x_ref[0]
    xv_ref[2 * step + 1] = x_ref[1]

    @pl.when(step == 0)
    def _():
        acc[...] = jnp.zeros_like(acc)
        down_ref[0:lon, :] = x_ref[0]

    owner = lane((channels, 128)) // fluxes
    for g in range(GROUPS):
        size = min(group, lon - g * group)
        span = slice(g * group, g * group + size)
        lhs = jnp.concatenate([x_ref[0, span, :], x_ref[1, span, :]], axis=1)
        halves = [
            jnp.where(owner == g * rows + 2 * step + k, tiled, jnp.zeros_like(tiled)) for k in (0, 1)
        ]
        acc[0:size, :] += dot(lhs, jnp.concatenate(halves, axis=0))

    @pl.when(step == pl.num_programs(0) - 1)
    def _():
        up_ref[0:lon, :] = x_ref[1]
        wetf[...] = jnp.zeros_like(wetf)
        wetf[:, 0:lon] = wet_ref[...].astype(F32)
        mask = jnp.zeros_like(acc)
        for g in range(GROUPS):
            pick = (lane((rows, 128)) // fluxes == g * rows + sublane((rows, 128))).astype(F32)
            mask += lax.dot_general(
                wetf[:, g * group : (g + 1) * group], pick, (((0,), (0,)), ((), ())),
                preferred_element_type=F32,
            )
        mask = jnp.where(where[0] == 1, mask, jnp.ones_like(mask))
        out_ref[...] = (acc[...] * mask).astype(BF)


def held():
    return pl.BlockSpec(memory_space=pltpu.VMEM)


def surfaces(where, state, surface_proj, wet_mask, group):
    rows, lon, channels = state.shape
    fluxes = surface_proj.shape[2]
    return pl.pallas_call(
        functools.partial(surface_kernel, rows, lon, group, fluxes),
        grid_spec=pltpu.PrefetchScalarGridSpec(
            num_scalar_prefetch=1,
            grid=(rows // 2,),
            in_specs=[
                pl.BlockSpec((2, lon, channels), lambda i, s: (i, 0, 0)),
                pl.BlockSpec((1, fluxes, channels), lambda i, s: (s[0], 0, 0)),
                pl.BlockSpec((rows, lon), lambda i, s: (s[1], 0)),
            ],
            out_specs=[held()] * 4,
            scratch_shapes=[
                pltpu.VMEM((group, 128), F32),
                pltpu.VMEM((rows, GROUPS * group), F32),
            ],
        ),
        out_shape=[
            pltpu.VMEM((group, 128), BF),
            pltpu.VMEM((rows, lon, channels), BF),
            pltpu.VMEM((lon + group, channels), BF),
            pltpu.VMEM((lon + group, channels), BF),
        ],
        compiler_params=limits(16),
        name="surface_fields",
    )(
        where,
        pltpu.with_memory_space_constraint(state, pltpu.HBM),
        jnp.swapaxes(surface_proj, 1, 2),
        pltpu.with_memory_space_constraint(wet_mask, pltpu.HBM),
    )


def partial_kernel(first, pairs, lon, *refs):
    if first == 0:
        where, x_ref, w_ref, out_ref, wy, wm, we, tf = refs
    else:
        where, x_ref, wy, wm, _, out_ref, tf = refs
    step = pl.program_id(0)
    pair = step + first

    if first == 0:

        def tap(a, b):
            return w_ref[0, pl.ds((a * 3 + b) * 128, 128), :].astype(F32) * 0.5

        @pl.when(step == 0)
        def _():
            for k, (a, b) in enumerate(((0, 0), (0, 2), (1, 1), (2, 1))):
                wy[0, k * 128 : (k + 1) * 128, :] = tap(a, b).astype(BF)
            for k, (a, b) in enumerate(((2, 0), (2, 2), (0, 1), (1, 1))):
                wy[1, k * 128 : (k + 1) * 128, :] = tap(a, b).astype(BF)
            for k, b in enumerate((0, 2)):
                ends = tap(0, b) + tap(2, b)
                wm[0, k * 128 : (k + 1) * 128, :] = (0.5 * (ends + tap(1, b))).astype(BF)
                wm[1, k * 128 : (k + 1) * 128, :] = (0.5 * (ends - tap(1, b))).astype(BF)
            for e, a in enumerate((0, 2)):
                for k, b in enumerate((0, 2, 1)):
                    we[e, k * 128 : (k + 1) * 128, :] = tap(a, b).astype(BF)

    south = jnp.where(pair == 0, 0.0, 1.0)
    north = jnp.where(pair == pairs - 1, 0.0, 1.0)
    x0 = x_ref[jnp.maximum(2 * pair - 1, 0)].astype(F32) * south
    x1 = x_ref[2 * pair].astype(F32)
    x2 = x_ref[2 * pair + 1].astype(F32)
    x3 = x_ref[jnp.minimum(2 * pair + 2, 2 * pairs - 1)].astype(F32) * north
    for p, t in enumerate((x0 - x2, x1 + x2, x2 - x1, x3 - x1)):
        tf[p, 8 : 8 + lon, :] = t
        tf[p, 7:8, :] = t[lon - 1 : lon]
        tf[p, 8 + lon : 9 + lon, :] = t[0:1]

    def sides(p):
        return [tf[p, 7 : 7 + lon, :].astype(BF), tf[p, 9 : 9 + lon, :].astype(BF)]

    own = [x_ref[2 * pair], x_ref[2 * pair + 1]]
    m1 = dot(jnp.concatenate(sides(1), axis=1), wm[0])
    m2 = dot(jnp.concatenate(sides(2), axis=1), wm[1])
    out_ref[2 * pair] = (dot(jnp.concatenate(sides(0) + own, axis=1), wy[0]) + (m1 + m2)).astype(BF)
    out_ref[2 * pair + 1] = (dot(jnp.concatenate(sides(3) + own, axis=1), wy[1]) + (m1 - m2)).astype(BF)


def partials(where, xv, inner_weight, first, count, earlier=None):
    rows, lon, channels = xv.shape
    depth, hidden = inner_weight.shape[1:]
    out_shape = [pltpu.VMEM((rows, lon, hidden), BF)]
    in_specs = [held()]
    if earlier is None:
        in_specs.append(pl.BlockSpec((1, depth, hidden), lambda i, s: (s[0], 0, 0), pipeline_mode=pl.Buffered(1)))
        operands = [xv, inner_weight]
        out_shape += [
            pltpu.VMEM((2, 4 * channels, hidden), BF),
            pltpu.VMEM((2, 2 * channels, hidden), BF),
            pltpu.VMEM((2, 3 * channels, hidden), BF),
        ]
        aliases = {}
    else:
        part, wy, wm = earlier
        in_specs += [held()] * 3
        operands = [xv, wy, wm, part]
        aliases = {4: 0}
    return pl.pallas_call(
        functools.partial(partial_kernel, first, rows // 2, lon),
        grid_spec=pltpu.PrefetchScalarGridSpec(
            num_scalar_prefetch=1,
            grid=(count,),
            in_specs=in_specs,
            out_specs=[held()] * len(out_shape),
            scratch_shapes=[pltpu.VMEM((4, lon + 16, channels), F32)],
        ),
        out_shape=out_shape,
        input_output_aliases=aliases,
        compiler_params=limits(28),
        cost_estimate=pl.CostEstimate(
            flops=count * 2 * lon * 6 * channels * hidden * 2,
            bytes_accessed=count * 2 * lon * (hidden + 2 * channels) * 2,
            transcendentals=0,
        ),
        name="own_rows",
    )(where, *operands)


def finish_kernel(
    rows, lon, group, fluxes, where, table, weights, x_ref, part_ref, low_ref, high_ref, mid_ref, taps_ref,
    f_ref, o_ref, wet_ref, out_ref, halo, window, we, spread, wett, wetf,
):
    r = pl.program_id(0)
    parity = r % 2

    @pl.when(r == 0)
    def _():
        we[:, 0:384, :] = taps_ref[...]
        for e, side in enumerate((low_ref, high_ref)):
            v = side[0:lon, :].astype(F32)
            halo[e, 8 : 8 + lon, :] = v
            halo[e, 7:8, :] = v[lon - 1 : lon]
            halo[e, 8 + lon : 9 + lon, :] = v[0:1]
        packs = [
            low_ref[lon : lon + group, :].astype(F32),
            mid_ref[...].astype(F32),
            high_ref[lon : lon + group, :].astype(F32),
        ]
        for g in range(GROUPS):
            size = min(group, lon - g * group)
            owner = lane((group, 128)) // (rows * fluxes)
            total = jnp.zeros((group, 128), F32)
            for w, pack in enumerate(packs):
                shift = (rows * fluxes * (w - g)) % 128
                moved = pltpu.roll(pack, shift, 1) if shift else pack
                total = jnp.where(owner == w, moved, total)
            window[g * group : g * group + size, :] = total[0:size].astype(BF)
        at = sublane((128, spread.shape[1])) % fluxes
        total = jnp.zeros(spread.shape, F32)
        for f in range(fluxes):
            total = jnp.where(at == f, f_ref[0, f : f + 1, :].astype(F32) * 0.5, total)
        spread[...] = total
        wetf[...] = jnp.zeros_like(wetf)
        wetf[0:rows, 0:lon] = jnp.where(where[0] == 1, wet_ref[...].astype(F32), 1.0)
        for c in range(wetf.shape[1] // 128):
            wett[c * 128 : (c + 1) * 128, :] = wetf[:, c * 128 : (c + 1) * 128].T

    slot = sublane(spread.shape) // fluxes
    share = jnp.zeros(spread.shape, F32)
    row = where[1] * rows + r
    for m in range(table.shape[0]):
        local = table[m, where[0], row] - (where[1] - 1) * rows
        share += jnp.where(slot == local, weights[m, where[0], row], 0.0)
    we[parity, 384:512, :] = (share * spread[...]).astype(BF)

    def close(total):
        total = total + part_ref[r].astype(F32)
        act = (total + total * jnp.tanh(total)).astype(BF)
        value = x_ref[r].astype(F32) + dot(act, o_ref[0])
        keep = jnp.broadcast_to(wett[0:lon, 0:1], value.shape)
        out_ref[0] = jnp.where(keep > 0.5, value, 0.0).astype(BF)
        wett[...] = pltpu.roll(wett[...], 127, 1)

    edge = jnp.logical_or(r == 0, r == rows - 1)

    @pl.when(edge)
    def _():
        lhs = [halo[parity, k : k + lon, :].astype(BF) for k in (7, 9, 8)] + [window[...]]
        close(dot(jnp.concatenate(lhs, axis=1), we[parity]))

    @pl.when(jnp.logical_not(edge))
    def _():
        near = x_ref[jnp.clip(r - 1 + 2 * parity, 0, rows - 1)]
        close(dot(jnp.concatenate([near, window[...]], axis=1), we[parity, 256:512, :]))


def finish(where, xv, part, low, high, mid, taps, forcing_in, outer_weight, wet_mask, table, weights):
    rows, lon, channels = xv.shape
    hidden = part.shape[2]
    fluxes = forcing_in.shape[1]
    group = mid.shape[0]
    scalars = pl.BlockSpec(memory_space=pltpu.SMEM)
    return pl.pallas_call(
        functools.partial(finish_kernel, rows, lon, group, fluxes),
        grid_spec=pltpu.PrefetchScalarGridSpec(
            num_scalar_prefetch=1,
            grid=(rows,),
            in_specs=[scalars, scalars] + [held()] * 6 + [
                pl.BlockSpec((1, fluxes, hidden), lambda r, s: (s[0], 0, 0)),
                pl.BlockSpec((1, hidden, channels), lambda r, s: (s[0], 0, 0)),
                pl.BlockSpec((rows, lon), lambda r, s: (s[1], 0)),
            ],
            out_specs=pl.BlockSpec((1, lon, channels), lambda r, s: (r, 0, 0)),
            scratch_shapes=[
                pltpu.VMEM((2, lon + 16, channels), F32),
                pltpu.VMEM((lon, 128), BF),
                pltpu.VMEM((2, 512, hidden), BF),
                pltpu.VMEM((128, hidden), F32),
                pltpu.VMEM((GROUPS * group, 128), F32),
                pltpu.VMEM((128, GROUPS * group), F32),
            ],
        ),
        out_shape=jax.ShapeDtypeStruct((rows, lon, channels), BF),
        compiler_params=limits(28),
        name="finish_rows",
    )(
        where, jnp.transpose(table, (2, 0, 1)), jnp.transpose(weights, (2, 0, 1)), xv, part, low, high, mid,
        taps, forcing_in, outer_weight, wet_mask,
    )


def shards(state, inner_weight, outer_weight, surface_proj, forcing_in, margin_rows, margin_weights, wet_mask):
    count = lax.axis_size("lat")
    half = count // 2
    quarter = half // 2
    lon = state.shape[1]
    group = -(-lon // (GROUPS * 128)) * 128
    moved = (lax.axis_index("lat") + quarter) % count
    where = jnp.where(lax.iota(jnp.int32, 2) == 0, moved // half, moved % half)

    def component(i):
        return ((i + quarter) % count) // half

    def beside(block, distance):
        route = [(i, (i + distance) % count) for i in range(count)]
        route = [(i, j) for i, j in route if component(i) == component(j)]
        return lax.ppermute(block, "lat", route)

    pack, xv, up, down = surfaces(where, state, surface_proj, wet_mask, group)
    mid = lax.ppermute(pack, "lat", [(i, (i + half) % count) for i in range(count)])
    part, wy, wm, taps = partials(where, xv, inner_weight, 0, FIRST_PAIRS)
    mid, part = lax.optimization_barrier((mid, part))
    up = lax.dynamic_update_slice(up, mid, (lon, 0))
    down = lax.dynamic_update_slice(down, mid, (lon, 0))
    low = beside(up, 1)
    high = beside(down, -1)
    (part,) = partials(
        where, xv, inner_weight, FIRST_PAIRS, state.shape[0] // 2 - FIRST_PAIRS, (part, wy, wm)
    )
    return finish(
        where, xv, part, low, high, mid, taps, forcing_in, outer_weight, wet_mask, margin_rows, margin_weights
    )


def solution(mesh):
    placed = (P(("ens", "lat"), None, None), P(), P(), P(), P(), P(), P(), P())
    return jax.shard_map(
        shards, mesh=mesh, in_specs=placed, out_specs=P(("ens", "lat"), None, None), check_vma=False
    )
```

time: 55.2 us -> 47 us (0.85)
  Pallas kernels: 38.3 us -> 30.6 us
  waiting for transfers between devices: 0.01 us -> 4.78 us
  local copies, waits for them, and re-layouts: 3.91 us -> 0.75 us
  starting transfers between devices: 12.4 us -> 10.6 us
    pallas_call x2, Pallas kernels: 19.4 us -> 12.1 us  [partials(): pl.pallas_call(functools.partial(partial_kernel, first, rows // 2, lon),...]
    ppermute x2, waiting for transfers between devices: 0.01 us -> 4.78 us  [beside(): return lax.ppermute(block, 'lat', route)]
    unnamed x17 -> x14, local copies, waits for them, and re-layouts: 3.88 us -> 0.72 us
    pallas_call x1, Pallas kernels: 15.9 us -> 13.2 us  [finish(): pl.pallas_call(functools.partial(finish_kernel, rows, lon, group, fluxes)...]
    pallas_call x1, Pallas kernels: 3 us -> 5.25 us  [surfaces(): pl.pallas_call(functools.partial(surface_kernel, rows, lon, group, fluxes...]
    ppermute x2, starting transfers between devices: 8.26 us -> 6.49 us  [beside(): return lax.ppermute(block, 'lat', route)]
  transfers between devices with their start and end apart: 3 -> 3, of which waited for: 0 -> 1; matrix products, arithmetic and copies ran while one was open for 0% -> 0% of each run, Pallas kernels for 35% -> 26%
where the time goes in v2:
time: 47 us; the launch traced here: 46.8 us
  Pallas kernels  30.6 us (65%)
  starting transfers between devices  10.6 us (23%)
  waiting for transfers between devices  4.78 us (10%)
  local copies, waits for them, and re-layouts  0.75 us (2%)
    pallas_call x1, Pallas kernels, finish(): pl.pallas_call(functools.partial(finish_kernel, rows, lon, group, fluxes)...  13.2 us
    pallas_call x2, Pallas kernels, partials(): pl.pallas_call(functools.partial(partial_kernel, first, rows // 2, lon),...  12.1 us
    ppermute x2, starting transfers between devices, beside(): return lax.ppermute(block, 'lat', route)  6.49 us
    pallas_call x1, Pallas kernels, surfaces(): pl.pallas_call(functools.partial(surface_kernel, rows, lon, group, fluxes...  5.25 us
    ppermute x2, waiting for transfers between devices, beside(): return lax.ppermute(block, 'lat', route)  4.78 us
    ppermute x1, starting transfers between devices, shards(): lax.ppermute(pack, 'lat', [(i, (i + half) % count) for i in range(count)])  4.09 us
  transfers between devices with their start and end apart: 3, of which 1 were waited for; matrix products, arithmetic and copies ran while one was open for 0% of the time, Pallas kernels for 26%

profile of v2, /device:TPU:0, one launch (start us, length us, event | category | flops | bytes accessed | tf_op | source)
XLA Modules:
  0.0 46.8 jit_solution(7319334312269810995)
XLA Ops:
  0.0 0.0 copy-start.5
  0.0 0.7 %copy-done.5 = bf16[2,128,4]{1,2,0:T(4,128)(2,1)S(1)} copy-done((bf16[2,128,4]{1,2,0:T(4,128)(2,1)S(1)}, bf16[2,128,4]{1,2,0:T(4,128)(2,1)}, u32[]{:S(2)}) %copy-start.5) | copy-done | bytes 2072
  0.7 0.0 copy-start.6
  0.7 5.2 %surface_fields.1 = (bf16[384,128]{1,0:T(8,128)(2,1)S(1)}, bf16[8,1440,128]{2,1,0:T(8,128)(2,1)S(1)}, bf16[1824,128]{1,0:T(8,128)(2,1)S(1)}, bf16[1824,128]{1,0:T(8,128)(2,1)S(1)}) custom-call(s32[2]{0:T(128)S(1)} %compare_select_fusion.where.refs_0_, bf16[8,1440,128]{2,1,0:T(8,128)(2,1)} %x_ref.1, bf16[2,4,128]{2,1,0:T(4,128)(2,1)S(1)} %bitcast.5, ...), custom_call_target="tpu_custom_call" | custom-call | tf_op jit(solution)/shard_map/surface_fields/pallas_call | solution.py:84
  5.9 4.1 %collective-permute-start = (bf16[384,128]{1,0:T(8,128)(2,1)S(1)}, bf16[384,128]{1,0:T(8,128)(2,1)S(1)}, u32[]{:S(2)}, u32[]{:S(2)}) collective-permute-start(bf16[384,128]{1,0:T(8,128)(2,1)S(1)} %get-tuple-element.18), channel_id=1, source_target_pairs={{0,8},{1,9},{2,10},{3,11},{4,12},{5,13},{6,14},{7,15},{8,0},{9,1},... | collective-permute-start | bytes 294920 | tf_op jit(solution)/shard_map/ppermute | solution.py:325
  10.0 0.0 copy-done.6
  10.0 6.3 %own_rows.2 = (bf16[8,1440,512]{2,1,0:T(8,128)(2,1)S(1)}, bf16[2,512,512]{2,1,0:T(8,128)(2,1)S(1)}, bf16[2,256,512]{2,1,0:T(8,128)(2,1)S(1)}, bf16[2,384,512]{2,1,0:T(8,128)(2,1)S(1)}) custom-call(s32[2]{0:T(128)S(1)} %compare_select_fusion.where.refs_0_, bf16[8,1440,128]{2,1,0:T(8,128)(2,1)S(1)} %get-tuple-element.15.refs_1_.x_ref, ...), custom_call_target="tpu_custom_call" | custom-call | flops 4529848320 | bytes 8847360 | tf_op jit(solution)/shard_map/own_rows/pallas_call | solution.py:183
  16.4 0.0 collective-permute-done.mid_ref
  16.4 4.6 %collective-permute-start.2 = (bf16[1824,128]{1,0:T(8,128)(2,1)S(1)}, bf16[1824,128]{1,0:T(8,128)(2,1)S(1)}, u32[]{:S(2)}, u32[]{:S(2)}) collective-permute-start(bf16[1824,128]{1,0:T(8,128)(2,1)S(1)} %get-tuple-element.25), channel_id=1, source_target_pairs={{0,15},{1,0},{2,1},{3,2},{5,4},{6,5},{7,6},{8,7},{9,8},{10,9},{11,... | collective-permute-start | bytes 1400840 | tf_op jit(solution)/shard_map/ppermute | solution.py:322
  21.0 1.9 %collective-permute-start.1 = (bf16[1824,128]{1,0:T(8,128)(2,1)S(1)}, bf16[1824,128]{1,0:T(8,128)(2,1)S(1)}, u32[]{:S(2)}, u32[]{:S(2)}) collective-permute-start(bf16[1824,128]{1,0:T(8,128)(2,1)S(1)} %get-tuple-element.26), channel_id=1, source_target_pairs={{0,1},{1,2},{2,3},{4,5},{5,6},{6,7},{7,8},{8,9},{9,10},{10,11},{12... | collective-permute-start | bytes 1400840 | tf_op jit(solution)/shard_map/ppermute | solution.py:322
  22.9 0.0 copy-start
  23.0 0.0 copy-start.1
  23.0 0.0 copy-start.2
  23.0 0.0 copy-start.3
  23.0 0.0 copy-start.4
  23.0 5.8 %own_rows.3.part_ref = bf16[8,1440,512]{2,1,0:T(8,128)(2,1)S(1)} custom-call(s32[2]{0:T(128)S(1)} %compare_select_fusion.where.refs_0_, bf16[8,1440,128]{2,1,0:T(8,128)(2,1)S(1)} %get-tuple-element.15.refs_1_.x_ref, bf16[2,512,512]{2,1,0:T(8,128)(2,1)S(1)} %get-tuple-element.16.refs_2_, ...), custom_call_target="tpu_custom_call", output_to_operand_aliasing={{}: (4, {})} | custom-call | flops 4529848320 | bytes 8847360 | tf_op jit(solution)/shard_map/own_rows/pallas_call | solution.py:183
  28.8 0.0 collective-permute-done.2.high_ref
  28.8 4.8 %collective-permute-done.1.low_ref = bf16[1824,128]{1,0:T(8,128)(2,1)S(1)} collective-permute-done((bf16[1824,128]{1,0:T(8,128)(2,1)S(1)}, bf16[1824,128]{1,0:T(8,128)(2,1)S(1)}, u32[]{:S(2)}, u32[]{:S(2)}) %collective-permute-start.1) | collective-permute-done | bytes 466976 | tf_op jit(solution)/shard_map/ppermute | solution.py:322
  33.6 0.0 copy-done
  33.6 0.0 copy-done.1
  33.6 0.0 copy-done.2
  33.6 0.0 copy-done.3
  33.6 0.0 copy-done.4
  33.6 13.2 %finish_rows.1 = bf16[8,1440,128]{2,1,0:T(8,128)(2,1)} custom-call(s32[2]{0:T(128)S(1)} %compare_select_fusion.where.refs_0_, s32[3,2,64]{2,1,0:T(2,128)S(1)} %bitcast.3, f32[3,2,64]{2,1,0:T(2,128)S(1)} %bitcast.4, bf16[8,1440,128]{2,1,0:T(8,128)(2,1)S(1)} %get-tuple-element.15.refs_1_.x_ref, bf16[8,1440,512]{2,1,0:T(8,128)(2,1)S(1)} %own_rows.3.part_ref, ...), custom_call_target="tpu_custom_call" | custom-call | tf_op jit(solution)/shard_map/finish_rows/pallas_call | solution.py:278
  (2 shorter events, 0.0 us)
Async XLA Ops:
  0.0 0.7 %copy-start.5 = (bf16[2,128,4]{1,2,0:T(4,128)(2,1)S(1)}, bf16[2,128,4]{1,2,0:T(4,128)(2,1)}, u32[]{:S(2)}) copy-start(bf16[2,128,4]{1,2,0:T(4,128)(2,1)} %param.11) | copy-start | bytes 6148
  0.7 9.4 %copy-start.6 = (bf16[2,1152,512]{2,1,0:T(8,128)(2,1)S(1)}, bf16[2,1152,512]{2,1,0:T(8,128)(2,1)}, u32[]{:S(2)}) copy-start(bf16[2,1152,512]{2,1,0:T(8,128)(2,1)} %refs_2_.1) | copy-start | bytes 7077892
  5.9 10.4 %collective-permute-start = (bf16[384,128]{1,0:T(8,128)(2,1)S(1)}, bf16[384,128]{1,0:T(8,128)(2,1)S(1)}, u32[]{:S(2)}, u32[]{:S(2)}) collective-permute-start(bf16[384,128]{1,0:T(8,128)(2,1)S(1)} %get-tuple-element.18), channel_id=1, source_target_pairs={{0,8},{1,9},{2,10},{3,11},{4,12},{5,13},{6,14},{7,15},{8,0},{9,1},... | collective-permute-start | bytes 294920 | tf_op jit(solution)/shard_map/ppermute | solution.py:325
  16.4 12.4 %collective-permute-start.2 = (bf16[1824,128]{1,0:T(8,128)(2,1)S(1)}, bf16[1824,128]{1,0:T(8,128)(2,1)S(1)}, u32[]{:S(2)}, u32[]{:S(2)}) collective-permute-start(bf16[1824,128]{1,0:T(8,128)(2,1)S(1)} %get-tuple-element.25), channel_id=1, source_target_pairs={{0,15},{1,0},{2,1},{3,2},{5,4},{6,5},{7,6},{8,7},{9,8},{10,9},{11,... | collective-permute-start | bytes 1400840 | tf_op jit(solution)/shard_map/ppermute | solution.py:322
  21.0 12.6 %collective-permute-start.1 = (bf16[1824,128]{1,0:T(8,128)(2,1)S(1)}, bf16[1824,128]{1,0:T(8,128)(2,1)S(1)}, u32[]{:S(2)}, u32[]{:S(2)}) collective-permute-start(bf16[1824,128]{1,0:T(8,128)(2,1)S(1)} %get-tuple-element.26), channel_id=1, source_target_pairs={{0,1},{1,2},{2,3},{4,5},{5,6},{6,7},{7,8},{8,9},{9,10},{10,11},{12... | collective-permute-start | bytes 1400840 | tf_op jit(solution)/shard_map/ppermute | solution.py:322
  22.9 10.7 %copy-start = (s32[64,1440]{1,0:T(8,128)S(1)}, s32[64,1440]{1,0:T(8,128)}, u32[]{:S(2)}) copy-start(s32[64,1440]{1,0:T(8,128)} %wet_ref.3) | copy-start | bytes 1105924
  23.0 10.6 %copy-start.1 = (bf16[2,512,128]{2,1,0:T(8,128)(2,1)S(1)}, bf16[2,512,128]{2,1,0:T(8,128)(2,1)}, u32[]{:S(2)}) copy-start(bf16[2,512,128]{2,1,0:T(8,128)(2,1)} %o_ref.1) | copy-start | bytes 786436
  23.0 10.6 %copy-start.2 = (bf16[2,4,512]{2,1,0:T(4,128)(2,1)S(1)}, bf16[2,4,512]{2,1,0:T(4,128)(2,1)}, u32[]{:S(2)}) copy-start(bf16[2,4,512]{2,1,0:T(4,128)(2,1)} %f_ref.1) | copy-start | bytes 24580
  23.0 10.6 %copy-start.3 = (s32[2,64,3]{1,0,2:T(2,128)S(1)}, s32[2,64,3]{1,0,2:T(2,128)}, u32[]{:S(2)}) copy-start(s32[2,64,3]{1,0,2:T(2,128)} %param.13) | copy-start | bytes 4612
  23.0 10.6 %copy-start.4 = (f32[2,64,3]{1,0,2:T(2,128)S(1)}, f32[2,64,3]{1,0,2:T(2,128)}, u32[]{:S(2)}) copy-start(f32[2,64,3]{1,0,2:T(2,128)} %param.14) | copy-start | bytes 4612

commit v3 on v2

--- a/solution.py
+++ b/solution.py
@@ -10,7 +10,6 @@
 BF = jnp.bfloat16
 F32 = jnp.float32
 GROUPS = 4
-FIRST_PAIRS = 2
 
 
 def dot(a, b):
@@ -46,7 +45,7 @@
     @pl.when(step == 0)
     def _():
         acc[...] = jnp.zeros_like(acc)
-        down_ref[0:lon, :] = x_ref[0]
+        down_ref[...] = x_ref[0]
 
     owner = lane((channels, 128)) // fluxes
     for g in range(GROUPS):
@@ -60,7 +59,7 @@
 
     @pl.when(step == pl.num_programs(0) - 1)
     def _():
-        up_ref[0:lon, :] = x_ref[1]
+        up_ref[...] = x_ref[1]
         wetf[...] = jnp.zeros_like(wetf)
         wetf[:, 0:lon] = wet_ref[...].astype(F32)
         mask = jnp.zeros_like(acc)
@@ -72,6 +71,10 @@
             )
         mask = jnp.where(where[0] == 1, mask, jnp.ones_like(mask))
         out_ref[...] = (acc[...] * mask).astype(BF)
+
+
+def in_hbm(x):
+    return pltpu.with_memory_space_constraint(x, pltpu.HBM)
 
 
 def held():
@@ -100,45 +103,35 @@
         out_shape=[
             pltpu.VMEM((group, 128), BF),
             pltpu.VMEM((rows, lon, channels), BF),
-            pltpu.VMEM((lon + group, channels), BF),
-            pltpu.VMEM((lon + group, channels), BF),
+            pltpu.VMEM((lon, channels), BF),
+            pltpu.VMEM((lon, channels), BF),
         ],
         compiler_params=limits(16),
         name="surface_fields",
     )(
-        where,
-        pltpu.with_memory_space_constraint(state, pltpu.HBM),
-        jnp.swapaxes(surface_proj, 1, 2),
-        pltpu.with_memory_space_constraint(wet_mask, pltpu.HBM),
-    )
-
-
-def partial_kernel(first, pairs, lon, *refs):
-    if first == 0:
-        where, x_ref, w_ref, out_ref, wy, wm, we, tf = refs
-    else:
-        where, x_ref, wy, wm, _, out_ref, tf = refs
-    step = pl.program_id(0)
-    pair = step + first
-
-    if first == 0:
-
-        def tap(a, b):
-            return w_ref[0, pl.ds((a * 3 + b) * 128, 128), :].astype(F32) * 0.5
-
-        @pl.when(step == 0)
-        def _():
-            for k, (a, b) in enumerate(((0, 0), (0, 2), (1, 1), (2, 1))):
-                wy[0, k * 128 : (k + 1) * 128, :] = tap(a, b).astype(BF)
-            for k, (a, b) in enumerate(((2, 0), (2, 2), (0, 1), (1, 1))):
-                wy[1, k * 128 : (k + 1) * 128, :] = tap(a, b).astype(BF)
-            for k, b in enumerate((0, 2)):
-                ends = tap(0, b) + tap(2, b)
-                wm[0, k * 128 : (k + 1) * 128, :] = (0.5 * (ends + tap(1, b))).astype(BF)
-                wm[1, k * 128 : (k + 1) * 128, :] = (0.5 * (ends - tap(1, b))).astype(BF)
-            for e, a in enumerate((0, 2)):
-                for k, b in enumerate((0, 2, 1)):
-                    we[e, k * 128 : (k + 1) * 128, :] = tap(a, b).astype(BF)
+        where, in_hbm(state), in_hbm(jnp.swapaxes(surface_proj, 1, 2)), in_hbm(wet_mask)
+    )
+
+
+def partial_kernel(pairs, lon, where, x_ref, w_ref, out_ref, we, wy, wm, tf):
+    pair = pl.program_id(0)
+
+    def tap(a, b):
+        return w_ref[0, pl.ds((a * 3 + b) * 128, 128), :].astype(F32) * 0.5
+
+    @pl.when(pair == 0)
+    def _():
+        for k, (a, b) in enumerate(((0, 0), (0, 2), (1, 1), (2, 1))):
+            wy[0, k * 128 : (k + 1) * 128, :] = tap(a, b).astype(BF)
+        for k, (a, b) in enumerate(((2, 0), (2, 2), (0, 1), (1, 1))):
+            wy[1, k * 128 : (k + 1) * 128, :] = tap(a, b).astype(BF)
+        for k, b in enumerate((0, 2)):
+            ends = tap(0, b) + tap(2, b)
+            wm[0, k * 128 : (k + 1) * 128, :] = (0.5 * (ends + tap(1, b))).astype(BF)
+            wm[1, k * 128 : (k + 1) * 128, :] = (0.5 * (ends - tap(1, b))).astype(BF)
+        for e, a in enumerate((0, 2)):
+            for k, b in enumerate((0, 2, 1)):
+                we[e, k * 128 : (k + 1) * 128, :] = tap(a, b).astype(BF)
 
     south = jnp.where(pair == 0, 0.0, 1.0)
     north = jnp.where(pair == pairs - 1, 0.0, 1.0)
@@ -161,49 +154,44 @@
     out_ref[2 * pair + 1] = (dot(jnp.concatenate(sides(3) + own, axis=1), wy[1]) + (m1 - m2)).astype(BF)
 
 
-def partials(where, xv, inner_weight, first, count, earlier=None):
+def partials(where, xv, inner_weight):
     rows, lon, channels = xv.shape
     depth, hidden = inner_weight.shape[1:]
-    out_shape = [pltpu.VMEM((rows, lon, hidden), BF)]
-    in_specs = [held()]
-    if earlier is None:
-        in_specs.append(pl.BlockSpec((1, depth, hidden), lambda i, s: (s[0], 0, 0), pipeline_mode=pl.Buffered(1)))
-        operands = [xv, inner_weight]
-        out_shape += [
-            pltpu.VMEM((2, 4 * channels, hidden), BF),
-            pltpu.VMEM((2, 2 * channels, hidden), BF),
-            pltpu.VMEM((2, 3 * channels, hidden), BF),
-        ]
-        aliases = {}
-    else:
-        part, wy, wm = earlier
-        in_specs += [held()] * 3
-        operands = [xv, wy, wm, part]
-        aliases = {4: 0}
     return pl.pallas_call(
-        functools.partial(partial_kernel, first, rows // 2, lon),
+        functools.partial(partial_kernel, rows // 2, lon),
         grid_spec=pltpu.PrefetchScalarGridSpec(
             num_scalar_prefetch=1,
-            grid=(count,),
-            in_specs=in_specs,
-            out_specs=[held()] * len(out_shape),
-            scratch_shapes=[pltpu.VMEM((4, lon + 16, channels), F32)],
+            grid=(rows // 2,),
+            in_specs=[
+                held(),
+                pl.BlockSpec(
+                    (1, depth, hidden), lambda i, s: (s[0], 0, 0), pipeline_mode=pl.Buffered(1)
+                ),
+            ],
+            out_specs=[held()] * 2,
+            scratch_shapes=[
+                pltpu.VMEM((2, 4 * channels, hidden), BF),
+                pltpu.VMEM((2, 2 * channels, hidden), BF),
+                pltpu.VMEM((4, lon + 16, channels), F32),
+            ],
         ),
-        out_shape=out_shape,
-        input_output_aliases=aliases,
+        out_shape=[
+            pltpu.VMEM((rows, lon, hidden), BF),
+            pltpu.VMEM((2, 3 * channels, hidden), BF),
+        ],
         compiler_params=limits(28),
         cost_estimate=pl.CostEstimate(
-            flops=count * 2 * lon * 6 * channels * hidden * 2,
-            bytes_accessed=count * 2 * lon * (hidden + 2 * channels) * 2,
+            flops=rows * lon * 6 * channels * hidden * 2,
+            bytes_accessed=rows * lon * (hidden + 2 * channels) * 2,
             transcendentals=0,
         ),
         name="own_rows",
-    )(where, *operands)
+    )(where, xv, inner_weight)
 
 
 def finish_kernel(
-    rows, lon, group, fluxes, where, table, weights, x_ref, part_ref, low_ref, high_ref, mid_ref, taps_ref,
-    f_ref, o_ref, wet_ref, out_ref, halo, window, we, spread, wett, wetf,
+    rows, lon, group, fluxes, where, table, weights, x_ref, part_ref, taps_ref, low_ref, high_ref, wl_ref,
+    wm_ref, wh_ref, f_ref, o_ref, wet_ref, out_ref, halo, window, we, spread, wett, wetf,
 ):
     r = pl.program_id(0)
     parity = r % 2
@@ -212,15 +200,11 @@
     def _():
         we[:, 0:384, :] = taps_ref[...]
         for e, side in enumerate((low_ref, high_ref)):
-            v = side[0:lon, :].astype(F32)
+            v = side[...].astype(F32)
             halo[e, 8 : 8 + lon, :] = v
             halo[e, 7:8, :] = v[lon - 1 : lon]
             halo[e, 8 + lon : 9 + lon, :] = v[0:1]
-        packs = [
-            low_ref[lon : lon + group, :].astype(F32),
-            mid_ref[...].astype(F32),
-            high_ref[lon : lon + group, :].astype(F32),
-        ]
+        packs = [ref[...].astype(F32) for ref in (wl_ref, wm_ref, wh_ref)]
         for g in range(GROUPS):
             size = min(group, lon - g * group)
             owner = lane((group, 128)) // (rows * fluxes)
@@ -269,18 +253,18 @@
         close(dot(jnp.concatenate([near, window[...]], axis=1), we[parity, 256:512, :]))
 
 
-def finish(where, xv, part, low, high, mid, taps, forcing_in, outer_weight, wet_mask, table, weights):
+def finish(where, xv, part, taps, beside, packs, forcing_in, outer_weight, wet_mask, table, weights):
     rows, lon, channels = xv.shape
     hidden = part.shape[2]
     fluxes = forcing_in.shape[1]
-    group = mid.shape[0]
+    group = packs[0].shape[0]
     scalars = pl.BlockSpec(memory_space=pltpu.SMEM)
     return pl.pallas_call(
         functools.partial(finish_kernel, rows, lon, group, fluxes),
         grid_spec=pltpu.PrefetchScalarGridSpec(
             num_scalar_prefetch=1,
             grid=(rows,),
-            in_specs=[scalars, scalars] + [held()] * 6 + [
+            in_specs=[scalars, scalars] + [held()] * 8 + [
                 pl.BlockSpec((1, fluxes, hidden), lambda r, s: (s[0], 0, 0)),
                 pl.BlockSpec((1, hidden, channels), lambda r, s: (s[0], 0, 0)),
                 pl.BlockSpec((rows, lon), lambda r, s: (s[1], 0)),
@@ -299,8 +283,8 @@
         compiler_params=limits(28),
         name="finish_rows",
     )(
-        where, jnp.transpose(table, (2, 0, 1)), jnp.transpose(weights, (2, 0, 1)), xv, part, low, high, mid,
-        taps, forcing_in, outer_weight, wet_mask,
+        where, jnp.transpose(table, (2, 0, 1)), jnp.transpose(weights, (2, 0, 1)), xv, part, taps,
+        *beside, *packs, forcing_in, outer_weight, wet_mask,
     )
 
 
@@ -322,18 +306,16 @@
         return lax.ppermute(block, "lat", route)
 
     pack, xv, up, down = surfaces(where, state, surface_proj, wet_mask, group)
-    mid = lax.ppermute(pack, "lat", [(i, (i + half) % count) for i in range(count)])
-    part, wy, wm, taps = partials(where, xv, inner_weight, 0, FIRST_PAIRS)
-    mid, part = lax.optimization_barrier((mid, part))
-    up = lax.dynamic_update_slice(up, mid, (lon, 0))
-    down = lax.dynamic_update_slice(down, mid, (lon, 0))
+    packs = []
+    for offset in (1, 0, -1):
+        route = [(i, (i + half + offset) % count) for i in range(count)]
+        packs.append(lax.ppermute(pack, "lat", route))
     low = beside(up, 1)
     high = beside(down, -1)
-    (part,) = partials(
-        where, xv, inner_weight, FIRST_PAIRS, state.shape[0] // 2 - FIRST_PAIRS, (part, wy, wm)
-    )
+    inner_weight, xv = lax.optimization_barrier((inner_weight, xv))
+    part, taps = partials(where, xv, inner_weight)
     return finish(
-        where, xv, part, low, high, mid, taps, forcing_in, outer_weight, wet_mask, margin_rows, margin_weights
+        where, xv, part, taps, (low, high), packs, forcing_in, outer_weight, wet_mask, margin_rows, margin_weights
     )
 
 

time: 47 us -> 45 us (0.957)
  waiting for transfers between devices: 4.78 us -> 0.01 us
  starting transfers between devices: 10.6 us -> 14.7 us
  local copies, waits for them, and re-layouts: 0.75 us -> 0.04 us
  Pallas kernels: 30.6 us -> 29.9 us
    ppermute x2, waiting for transfers between devices: 4.78 us -> 0.01 us  [beside(): return lax.ppermute(block, 'lat', route)]
    ppermute x1 -> x3, starting transfers between devices: 4.09 us -> 6.45 us  [shards(): packs.append(lax.ppermute(pack, 'lat', route))]
    ppermute x2, starting transfers between devices: 6.49 us -> 8.25 us  [beside(): return lax.ppermute(block, 'lat', route)]
    pallas_call x2 -> x1, Pallas kernels: 12.1 us -> 11.4 us  [partials(): pl.pallas_call(functools.partial(partial_kernel, rows // 2, lon), grid_sp...]
    unnamed x14 -> x12, local copies, waits for them, and re-layouts: 0.72 us -> 0.04 us
  transfers between devices with their start and end apart: 3 -> 5, of which waited for: 1 -> 0; matrix products, arithmetic and copies ran while one was open for 0% -> 0% of each run, Pallas kernels for 26% -> 26%
where the time goes in v3:
time: 45 us; the launch traced here: 44.8 us
  Pallas kernels  29.9 us (66%)
  starting transfers between devices  14.7 us (33%)
    pallas_call x1, Pallas kernels, finish(): pl.pallas_call(functools.partial(finish_kernel, rows, lon, group, fluxes)...  13.2 us
    pallas_call x1, Pallas kernels, partials(): pl.pallas_call(functools.partial(partial_kernel, rows // 2, lon), grid_sp...  11.4 us
    ppermute x2, starting transfers between devices, beside(): return lax.ppermute(block, 'lat', route)  8.25 us
    ppermute x3, starting transfers between devices, shards(): packs.append(lax.ppermute(pack, 'lat', route))  6.45 us
    pallas_call x1, Pallas kernels, surfaces(): pl.pallas_call(functools.partial(surface_kernel, rows, lon, group, fluxes...  5.26 us
  transfers between devices with their start and end apart: 5, of which 0 were waited for; matrix products, arithmetic and copies ran while one was open for 0% of the time, Pallas kernels for 26%

profile of v3, /device:TPU:0, one launch (start us, length us, event | category | flops | bytes accessed | tf_op | source)
XLA Modules:
  0.0 44.8 jit_solution(7529329897368656414)
XLA Ops:
  0.0 0.0 copy-start.5
  0.0 5.3 %surface_fields.1 = (bf16[384,128]{1,0:T(8,128)(2,1)S(1)}, bf16[8,1440,128]{2,1,0:T(8,128)(2,1)S(1)}, bf16[1440,128]{1,0:T(8,128)(2,1)S(1)}, bf16[1440,128]{1,0:T(8,128)(2,1)S(1)}) custom-call(s32[2]{0:T(128)S(1)} %compare_select_fusion.where, bf16[8,1440,128]{2,1,0:T(8,128)(2,1)} %x_ref.1, bf16[2,4,128]{2,1,0:T(4,128)(2,1)} %bitcast.5, s32[64,1440]{1,0:T(8,128)} %wet_ref.3), custom_call_target="tpu_custom_call" | custom-call | tf_op jit(solution)/shard_map/surface_fields/pallas_call | solution.py:87
  5.3 3.5 %collective-permute-start.4 = (bf16[384,128]{1,0:T(8,128)(2,1)S(1)}, bf16[384,128]{1,0:T(8,128)(2,1)S(1)}, u32[]{:S(2)}, u32[]{:S(2)}) collective-permute-start(bf16[384,128]{1,0:T(8,128)(2,1)S(1)} %get-tuple-element.20), channel_id=1, source_target_pairs={{0,7},{1,8},{2,9},{3,10},{4,11},{5,12},{6,13},{7,14},{8,15},{9,0},... | collective-permute-start | bytes 294920 | tf_op jit(solution)/shard_map/ppermute | solution.py:312
  8.7 2.6 %collective-permute-start.3 = (bf16[384,128]{1,0:T(8,128)(2,1)S(1)}, bf16[384,128]{1,0:T(8,128)(2,1)S(1)}, u32[]{:S(2)}, u32[]{:S(2)}) collective-permute-start(bf16[384,128]{1,0:T(8,128)(2,1)S(1)} %get-tuple-element.20), channel_id=1, source_target_pairs={{0,8},{1,9},{2,10},{3,11},{4,12},{5,13},{6,14},{7,15},{8,0},{9,1},... | collective-permute-start | bytes 294920 | tf_op jit(solution)/shard_map/ppermute | solution.py:312
  11.3 0.4 collective-permute-start.2
  11.7 2.9 %collective-permute-start = (bf16[1440,128]{1,0:T(8,128)(2,1)S(1)}, bf16[1440,128]{1,0:T(8,128)(2,1)S(1)}, u32[]{:S(2)}, u32[]{:S(2)}) collective-permute-start(bf16[1440,128]{1,0:T(8,128)(2,1)S(1)} %get-tuple-element.18), channel_id=1, source_target_pairs={{0,1},{1,2},{2,3},{4,5},{5,6},{6,7},{7,8},{8,9},{9,10},{10,11},{12... | collective-permute-start | bytes 1105928 | tf_op jit(solution)/shard_map/ppermute | solution.py:306
  14.6 5.3 %collective-permute-start.1 = (bf16[1440,128]{1,0:T(8,128)(2,1)S(1)}, bf16[1440,128]{1,0:T(8,128)(2,1)S(1)}, u32[]{:S(2)}, u32[]{:S(2)}) collective-permute-start(bf16[1440,128]{1,0:T(8,128)(2,1)S(1)} %get-tuple-element.19), channel_id=1, source_target_pairs={{0,15},{1,0},{2,1},{3,2},{5,4},{6,5},{7,6},{8,7},{9,8},{10,9},{11,... | collective-permute-start | bytes 1105928 | tf_op jit(solution)/shard_map/ppermute | solution.py:306
  20.0 0.0 copy-done.5
  20.0 0.0 copy-start
  20.0 0.0 copy-start.1
  20.0 0.0 copy-start.2
  20.0 0.0 copy-start.3
  20.0 0.0 copy-start.4
  20.1 11.4 %own_rows.1 = (bf16[8,1440,512]{2,1,0:T(8,128)(2,1)S(1)}, bf16[2,384,512]{2,1,0:T(8,128)(2,1)S(1)}) custom-call(s32[2]{0:T(128)S(1)} %compare_select_fusion.where, bf16[8,1440,128]{2,1,0:T(8,128)(2,1)S(1)} %get-tuple-element.14.x_ref, bf16[2,1152,512]{2,1,0:T(8,128)(2,1)S(1)} %copy-done.5), custom_call_target="tpu_custom_call" | custom-call | flops 9059696640 | bytes 17694720 | tf_op jit(solution)/shard_map/own_rows/pallas_call | solution.py:160
  31.5 0.0 collective-permute-done.4.wh_ref
  31.5 0.0 collective-permute-done.3.wm_ref
  31.5 0.0 collective-permute-done.2.wl_ref
  31.5 0.0 collective-permute-done.low_ref
  31.6 0.0 collective-permute-done.1.high_ref
  31.6 0.0 copy-done
  31.6 0.0 copy-done.1
  31.6 0.0 copy-done.2
  31.6 0.0 copy-done.3
  31.6 0.0 copy-done.4
  31.6 13.2 %finish_rows.1 = bf16[8,1440,128]{2,1,0:T(8,128)(2,1)} custom-call(s32[2]{0:T(128)S(1)} %compare_select_fusion.where, s32[3,2,64]{2,1,0:T(2,128)S(1)} %bitcast.3, f32[3,2,64]{2,1,0:T(2,128)S(1)} %bitcast.4, bf16[8,1440,128]{2,1,0:T(8,128)(2,1)S(1)} %get-tuple-element.14.x_ref, bf16[8,1440,512]{2,1,0:T(8,128)(2,1)S(1)} %get-tuple-element.16.part_ref, ...), custom_call_target="tpu_custom_call" | custom-call | tf_op jit(solution)/shard_map/finish_rows/pallas_call | solution.py:262
  (1 shorter events, 0.0 us)
Async XLA Ops:
  0.0 20.0 %copy-start.5 = (bf16[2,1152,512]{2,1,0:T(8,128)(2,1)S(1)}, bf16[2,1152,512]{2,1,0:T(8,128)(2,1)}, u32[]{:S(2)}) copy-start(bf16[2,1152,512]{2,1,0:T(8,128)(2,1)} %w_ref) | copy-start | bytes 7077892
  5.3 26.2 %collective-permute-start.4 = (bf16[384,128]{1,0:T(8,128)(2,1)S(1)}, bf16[384,128]{1,0:T(8,128)(2,1)S(1)}, u32[]{:S(2)}, u32[]{:S(2)}) collective-permute-start(bf16[384,128]{1,0:T(8,128)(2,1)S(1)} %get-tuple-element.20), channel_id=1, source_target_pairs={{0,7},{1,8},{2,9},{3,10},{4,11},{5,12},{6,13},{7,14},{8,15},{9,0},... | collective-permute-start | bytes 294920 | tf_op jit(solution)/shard_map/ppermute | solution.py:312
  8.7 22.8 %collective-permute-start.3 = (bf16[384,128]{1,0:T(8,128)(2,1)S(1)}, bf16[384,128]{1,0:T(8,128)(2,1)S(1)}, u32[]{:S(2)}, u32[]{:S(2)}) collective-permute-start(bf16[384,128]{1,0:T(8,128)(2,1)S(1)} %get-tuple-element.20), channel_id=1, source_target_pairs={{0,8},{1,9},{2,10},{3,11},{4,12},{5,13},{6,14},{7,15},{8,0},{9,1},... | collective-permute-start | bytes 294920 | tf_op jit(solution)/shard_map/ppermute | solution.py:312
  11.3 20.2 %collective-permute-start.2 = (bf16[384,128]{1,0:T(8,128)(2,1)S(1)}, bf16[384,128]{1,0:T(8,128)(2,1)S(1)}, u32[]{:S(2)}, u32[]{:S(2)}) collective-permute-start(bf16[384,128]{1,0:T(8,128)(2,1)S(1)} %get-tuple-element.20), channel_id=1, source_target_pairs={{0,9},{1,10},{2,11},{3,12},{4,13},{5,14},{6,15},{7,0},{8,1},{9,2},... | collective-permute-start | bytes 294920 | tf_op jit(solution)/shard_map/ppermute | solution.py:312
  11.7 19.8 %collective-permute-start = (bf16[1440,128]{1,0:T(8,128)(2,1)S(1)}, bf16[1440,128]{1,0:T(8,128)(2,1)S(1)}, u32[]{:S(2)}, u32[]{:S(2)}) collective-permute-start(bf16[1440,128]{1,0:T(8,128)(2,1)S(1)} %get-tuple-element.18), channel_id=1, source_target_pairs={{0,1},{1,2},{2,3},{4,5},{5,6},{6,7},{7,8},{8,9},{9,10},{10,11},{12... | collective-permute-start | bytes 1105928 | tf_op jit(solution)/shard_map/ppermute | solution.py:306
  14.6 16.9 %collective-permute-start.1 = (bf16[1440,128]{1,0:T(8,128)(2,1)S(1)}, bf16[1440,128]{1,0:T(8,128)(2,1)S(1)}, u32[]{:S(2)}, u32[]{:S(2)}) collective-permute-start(bf16[1440,128]{1,0:T(8,128)(2,1)S(1)} %get-tuple-element.19), channel_id=1, source_target_pairs={{0,15},{1,0},{2,1},{3,2},{5,4},{6,5},{7,6},{8,7},{9,8},{10,9},{11,... | collective-permute-start | bytes 1105928 | tf_op jit(solution)/shard_map/ppermute | solution.py:306
  20.0 11.6 %copy-start = (s32[64,1440]{1,0:T(8,128)S(1)}, s32[64,1440]{1,0:T(8,128)}, u32[]{:S(2)}) copy-start(s32[64,1440]{1,0:T(8,128)} %wet_ref.3) | copy-start | bytes 1105924
  20.0 11.6 %copy-start.1 = (bf16[2,512,128]{2,1,0:T(8,128)(2,1)S(1)}, bf16[2,512,128]{2,1,0:T(8,128)(2,1)}, u32[]{:S(2)}) copy-start(bf16[2,512,128]{2,1,0:T(8,128)(2,1)} %o_ref.1) | copy-start | bytes 786436
  20.0 11.6 %copy-start.2 = (bf16[2,4,512]{2,1,0:T(4,128)(2,1)S(1)}, bf16[2,4,512]{2,1,0:T(4,128)(2,1)}, u32[]{:S(2)}) copy-start(bf16[2,4,512]{2,1,0:T(4,128)(2,1)} %f_ref.1) | copy-start | bytes 24580
  20.0 11.6 %copy-start.3 = (s32[2,64,3]{1,0,2:T(2,128)S(1)}, s32[2,64,3]{1,0,2:T(2,128)}, u32[]{:S(2)}) copy-start(s32[2,64,3]{1,0,2:T(2,128)} %param.13) | copy-start | bytes 4612
  20.0 11.6 %copy-start.4 = (f32[2,64,3]{1,0,2:T(2,128)S(1)}, f32[2,64,3]{1,0,2:T(2,128)}, u32[]{:S(2)}) copy-start(f32[2,64,3]{1,0,2:T(2,128)} %param.14) | copy-start | bytes 4612

commit v4 on v3

v4 whole, which is shorter than its diff:
```python
import functools

import jax
import jax.numpy as jnp
from jax import lax
from jax.experimental import pallas as pl
from jax.experimental.pallas import tpu as pltpu
from jax.sharding import PartitionSpec as P

BF = jnp.bfloat16
F32 = jnp.float32
ACT = BF
GROUPS = 4


def dot(a, b):
    return jnp.dot(a, b, preferred_element_type=F32)


def lane(shape):
    return lax.broadcasted_iota(jnp.int32, shape, len(shape) - 1)


def sublane(shape):
    return lax.broadcasted_iota(jnp.int32, shape, len(shape) - 2)


def limits(mib):
    return pltpu.CompilerParams(
        dimension_semantics=("arbitrary",), vmem_limit_bytes=mib << 20
    )


def surface_kernel(
    rows, lon, group, fluxes, where, x_ref, proj_ref, wet_ref, out_ref, xv_ref, pair_ref, chip_ref, mask_ref,
    proj, wets, sems
):
    def load(k):
        both = pl.ds(2 * k, 2)
        copy = pltpu.make_async_copy(x_ref.at[both], xv_ref.at[both], sems.at[k])
        copy.start()
        return copy

    loads = [load(0)]
    small = [
        pltpu.make_async_copy(proj_ref.at[where[0]], proj, sems.at[rows // 2]),
        pltpu.make_async_copy(
            wet_ref.at[pl.ds(pl.multiple_of(where[1] * rows, rows), rows)], wets, sems.at[rows // 2 + 1]
        ),
    ]
    for copy in small:
        copy.start()
    loads.append(load(1))
    for copy in small:
        copy.wait()
    even = where[1] % 2 == 0
    channels = x_ref.shape[2]
    pick = (lane((rows, 128)) // fluxes == sublane((rows, 128))).astype(BF)
    wet = jnp.where(where[0] == 1, wets[...].astype(F32), 1.0).astype(BF)
    mask = lax.dot_general(wet, pick, (((0,), (0,)), ((), ())), preferred_element_type=F32)
    mask_ref[...] = mask.astype(BF)
    spread = (lane((fluxes, 128)) % fluxes == sublane((fluxes, 128))).astype(BF)
    tiled = lax.dot_general(
        proj[...], spread, (((0,), (0,)), ((), ())), preferred_element_type=F32
    ).astype(BF)
    owner = lane((channels, 128)) // fluxes
    total = None
    for k in range(rows // 2):
        halves = [jnp.where(owner == 2 * k + e, tiled, jnp.zeros_like(tiled)) for e in (0, 1)]
        loads[k].wait()
        if k + 2 < rows // 2:
            loads.append(load(k + 2))
        both = jnp.concatenate([xv_ref[2 * k], xv_ref[2 * k + 1]], axis=1)
        fields = dot(both, jnp.concatenate(halves, axis=0))
        total = fields if total is None else total + fields
    total = total * mask
    packed = jnp.zeros((group, 128), F32)
    for g in range(GROUPS):
        size = min(group, lon - g * group)
        part = total[g * group : g * group + size]
        if size < group:
            part = jnp.concatenate([part, jnp.zeros((group - size, 128), F32)], axis=0)
        packed += pltpu.roll(part, rows * fluxes * g, 1) if g else part
    packed = packed.astype(BF)
    out_ref[...] = packed
    pair_ref[0:lon, :] = xv_ref[jnp.where(even, rows - 1, 0)]
    pair_ref[lon : lon + group, :] = packed
    chip_ref[...] = xv_ref[jnp.where(even, 0, rows - 1)]


def in_hbm(x):
    return pltpu.with_memory_space_constraint(x, pltpu.HBM)


def held():
    return pl.BlockSpec(memory_space=pltpu.VMEM)


def surfaces(where, state, surface_proj, wet_mask, group):
    rows, lon, channels = state.shape
    fluxes = surface_proj.shape[2]
    return pl.pallas_call(
        functools.partial(surface_kernel, rows, lon, group, fluxes),
        grid_spec=pltpu.PrefetchScalarGridSpec(
            num_scalar_prefetch=1,
            grid=(1,),
            in_specs=[
                pl.BlockSpec(memory_space=pltpu.HBM),
                pl.BlockSpec(memory_space=pltpu.HBM),
                pl.BlockSpec(memory_space=pltpu.HBM),
            ],
            out_specs=[held()] * 5,
            scratch_shapes=[
                pltpu.VMEM((fluxes, channels), BF),
                pltpu.VMEM((rows, lon), jnp.int32),
                pltpu.SemaphoreType.DMA((rows // 2 + 2,)),
            ],
        ),
        out_shape=[
            pltpu.VMEM((group, 128), BF),
            pltpu.VMEM((rows, lon, channels), BF),
            pltpu.VMEM((lon + group, channels), BF),
            pltpu.VMEM((lon, channels), BF),
            pltpu.VMEM((lon, 128), BF),
        ],
        compiler_params=limits(16),
        name="surface_fields",
    )(
        where, in_hbm(state), in_hbm(jnp.swapaxes(surface_proj, 1, 2)), in_hbm(wet_mask)
    )


def partial_kernel(pairs, lon, where, x_ref, w_ref, out_ref, we, wy, wm, tf):
    def tap(a, b):
        return w_ref[0, (a * 3 + b) * 128 : (a * 3 + b + 1) * 128, :].astype(F32) * 0.5

    for k, (a, b) in enumerate(((0, 0), (0, 2), (1, 1), (2, 1))):
        wy[0, k * 128 : (k + 1) * 128, :] = tap(a, b).astype(BF)
    for k, (a, b) in enumerate(((2, 0), (2, 2), (0, 1), (1, 1))):
        wy[1, k * 128 : (k + 1) * 128, :] = tap(a, b).astype(BF)
    for k, b in enumerate((0, 2)):
        ends = tap(0, b) + tap(2, b)
        wm[0, k * 128 : (k + 1) * 128, :] = (0.5 * (ends + tap(1, b))).astype(BF)
        wm[1, k * 128 : (k + 1) * 128, :] = (0.5 * (ends - tap(1, b))).astype(BF)
    for e, a in enumerate((0, 2)):
        for k, b in enumerate((0, 2, 1)):
            we[e, k * 128 : (k + 1) * 128, :] = tap(a, b).astype(BF)

    for pair in range(pairs):
        slot = pair % tf.shape[0]
        own = [x_ref[2 * pair], x_ref[2 * pair + 1]]
        x1, x2 = own[0].astype(F32), own[1].astype(F32)
        low = x_ref[2 * pair - 1].astype(F32) - x2 if pair else -x2
        high = x_ref[2 * pair + 2].astype(F32) - x1 if pair < pairs - 1 else -x1
        for p, t in enumerate((low, x1 + x2, x2 - x1, high)):
            tf[slot, p, 8 : 8 + lon, :] = t
            tf[slot, p, 7:8, :] = t[lon - 1 : lon]
            tf[slot, p, 8 + lon : 9 + lon, :] = t[0:1]

        def sides(p):
            return [tf[slot, p, 7 : 7 + lon, :].astype(BF), tf[slot, p, 9 : 9 + lon, :].astype(BF)]

        m1 = dot(jnp.concatenate(sides(1), axis=1), wm[0])
        m2 = dot(jnp.concatenate(sides(2), axis=1), wm[1])
        out_ref[2 * pair] = (dot(jnp.concatenate(sides(0) + own, axis=1), wy[0]) + (m1 + m2)).astype(BF)
        out_ref[2 * pair + 1] = (dot(jnp.concatenate(sides(3) + own, axis=1), wy[1]) + (m1 - m2)).astype(BF)


def partials(where, xv, inner_weight):
    rows, lon, channels = xv.shape
    depth, hidden = inner_weight.shape[1:]
    return pl.pallas_call(
        functools.partial(partial_kernel, rows // 2, lon),
        grid_spec=pltpu.PrefetchScalarGridSpec(
            num_scalar_prefetch=1,
            grid=(1,),
            in_specs=[
                held(),
                pl.BlockSpec(
                    (1, depth, hidden), lambda i, s: (s[0], 0, 0), pipeline_mode=pl.Buffered(1)
                ),
            ],
            out_specs=[held()] * 2,
            scratch_shapes=[
                pltpu.VMEM((2, 4 * channels, hidden), BF),
                pltpu.VMEM((2, 2 * channels, hidden), BF),
                pltpu.VMEM((1, 4, lon + 16, channels), F32),
            ],
        ),
        out_shape=[
            pltpu.VMEM((rows, lon, hidden), BF),
            pltpu.VMEM((2, 3 * channels, hidden), BF),
        ],
        compiler_params=limits(34),
        cost_estimate=pl.CostEstimate(
            flops=rows * lon * 6 * channels * hidden * 2,
            bytes_accessed=rows * lon * (hidden + 2 * channels) * 2,
            transcendentals=0,
        ),
        name="own_rows",
    )(where, xv, inner_weight)


def finish_kernel(
    rows, lon, group, fluxes, where, table, weights, x_ref, part_ref, taps_ref, mask_ref, pair_ref, chip_ref,
    near_ref, far_ref, f_ref, o_ref, out_ref, halo, window, we, spread, done, sems,
):
    even = where[1] % 2 == 0
    swap = pair_ref[0:lon, :].astype(F32)
    chip = chip_ref[...].astype(F32)
    for e, v in enumerate((jnp.where(even, chip, swap), jnp.where(even, swap, chip))):
        halo[e, 8 : 8 + lon, :] = v
        halo[e, 7:8, :] = v[lon - 1 : lon]
        halo[e, 8 + lon : 9 + lon, :] = v[0:1]
    center = near_ref[0:group, :].astype(F32)
    other = near_ref[group : 2 * group, :].astype(F32)
    far = far_ref[...].astype(F32)
    packs = [jnp.where(even, far, other), center, jnp.where(even, other, far)]
    for g in range(GROUPS):
        size = min(group, lon - g * group)
        owner = lane((group, 128)) // (rows * fluxes)
        total = jnp.zeros((group, 128), F32)
        for w, pack in enumerate(packs):
            shift = (rows * fluxes * (w - g)) % 128
            moved = pltpu.roll(pack, shift, 1) if shift else pack
            total = jnp.where(owner == w, moved, total)
        window[g * group : g * group + size, :] = total[0:size].astype(BF)
    at = sublane((128, spread.shape[1])) % fluxes
    total = jnp.zeros(spread.shape, F32)
    for f in range(fluxes):
        total = jnp.where(at == f, f_ref[0, f : f + 1, :].astype(F32) * 0.5, total)
    spread[...] = total
    slot = sublane((128, 128)) // fluxes
    copies = []
    for r in range(rows):
        parity = r % 2
        edge = r in (0, rows - 1)
        share = jnp.zeros((128, 128), F32)
        row = where[1] * rows + r
        for m in range(table.shape[0]):
            local = table[m, where[0], row] - (where[1] - 1) * rows
            share += jnp.where(slot == local, weights[m, where[0], row], 0.0)
        share = jnp.concatenate([share] * (spread.shape[1] // 128), axis=1)
        base = 0 if edge else 256
        we[r, base:384, :] = taps_ref[parity, base:384, :]
        we[r, 384:512, :] = (share * spread[...]).astype(BF)
        if edge:
            lhs = [halo[parity, k : k + lon, :].astype(BF) for k in (7, 9, 8)]
        else:
            lhs = [x_ref[r + 1 if parity else r - 1]]
        total = dot(jnp.concatenate(lhs + [window[...]], axis=1), we[r, base:512, :])
        total = (total + part_ref[r].astype(F32)).astype(ACT)
        act = (total + total * jnp.tanh(total)).astype(BF)
        value = x_ref[r].astype(F32) + dot(act, o_ref[0])
        keep = jnp.broadcast_to(mask_ref[:, fluxes * r : fluxes * r + 1], value.shape)
        done[r] = value.astype(BF) * keep
        copy = pltpu.make_async_copy(done.at[r], out_ref.at[r], sems.at[r])
        copy.start()
        copies.append(copy)
    for copy in copies:
        copy.wait()


def finish(where, xv, part, taps, mask, received, forcing_in, outer_weight, table, weights):
    rows, lon, channels = xv.shape
    hidden = part.shape[2]
    fluxes = forcing_in.shape[1]
    group = received[3].shape[0]
    scalars = pl.BlockSpec(memory_space=pltpu.SMEM)
    return pl.pallas_call(
        functools.partial(finish_kernel, rows, lon, group, fluxes),
        grid_spec=pltpu.PrefetchScalarGridSpec(
            num_scalar_prefetch=1,
            grid=(1,),
            in_specs=[scalars, scalars] + [held()] * 8 + [
                pl.BlockSpec((1, fluxes, hidden), lambda r, s: (s[0], 0, 0)),
                pl.BlockSpec((1, hidden, channels), lambda r, s: (s[0], 0, 0)),
            ],
            out_specs=pl.BlockSpec(memory_space=pltpu.HBM),
            scratch_shapes=[
                pltpu.VMEM((2, lon + 16, channels), F32),
                pltpu.VMEM((lon, 128), BF),
                pltpu.VMEM((rows, 512, hidden), BF),
                pltpu.VMEM((128, hidden), F32),
                pltpu.VMEM((rows, lon, channels), BF),
                pltpu.SemaphoreType.DMA((rows,)),
            ],
        ),
        out_shape=jax.ShapeDtypeStruct((rows, lon, channels), BF),
        compiler_params=limits(34),
        name="finish_rows",
    )(
        where, jnp.transpose(table, (2, 0, 1)), jnp.transpose(weights, (2, 0, 1)), xv, part, taps, mask,
        *received, forcing_in, outer_weight,
    )


def shards(state, inner_weight, outer_weight, surface_proj, forcing_in, margin_rows, margin_weights, wet_mask):
    count = lax.axis_size("lat")
    half = count // 2
    quarter = half // 2
    lon = state.shape[1]
    group = -(-lon // (GROUPS * 128)) * 128
    moved = (lax.axis_index("lat") + quarter) % count
    where = jnp.where(lax.iota(jnp.int32, 2) == 0, moved // half, moved % half)

    def component(i):
        return ((i + quarter) % count) // half

    def send(block, target):
        return lax.ppermute(block, "lat", [(i, target(i) % count) for i in range(count)])

    pack, xv, pair, chip, mask = surfaces(where, state, surface_proj, wet_mask, group)
    pair = send(pair, lambda i: i + 1 - 2 * (i % 2))
    links = [(i, (i + (1 if i % 2 else -1)) % count) for i in range(count)]
    chip = lax.ppermute(chip, "lat", [(i, j) for i, j in links if component(i) == component(j)])
    far = send(pack, lambda i: i + half + (1 if i % 2 else -1))
    near = send(jnp.concatenate([pack, pair[lon:]], axis=0), lambda i: i + half)
    part, taps = partials(where, xv, inner_weight)
    return finish(
        where, xv, part, taps, mask, (pair, chip, near, far), forcing_in, outer_weight, margin_rows, margin_weights
    )


def solution(mesh):
    placed = (P(("ens", "lat"), None, None), P(), P(), P(), P(), P(), P(), P())
    return jax.shard_map(
        shards, mesh=mesh, in_specs=placed, out_specs=P(("ens", "lat"), None, None), check_vma=False
    )
```

time: 45 us -> 37 us (0.82)
  starting transfers between devices: 14.7 us -> 8.72 us
  Pallas kernels: 29.9 us -> 25.4 us
  waiting for transfers between devices: 0.01 us -> 2.4 us
    ppermute x5 -> x4, starting transfers between devices: 14.7 us -> 8.72 us  [the longest x3 4.72 us: send(): lax.ppermute(block, 'lat', [(i, target(i) % count) for i in range(count)])]
    pallas_call x1, Pallas kernels: 13.2 us -> 9.64 us  [finish(): pl.pallas_call(functools.partial(finish_kernel, rows, lon, group, fluxes)...]
    ppermute x5 -> x4, waiting for transfers between devices: 0.01 us -> 2.4 us  [the longest x3 2.4 us: send(): lax.ppermute(block, 'lat', [(i, target(i) % count) for i in range(count)])]
    pallas_call x1, Pallas kernels: 5.26 us -> 4.44 us  [surfaces(): pl.pallas_call(functools.partial(surface_kernel, rows, lon, group, fluxes...]
  transfers between devices with their start and end apart: 5 -> 4, of which waited for: 0 -> 1; matrix products, arithmetic and copies ran while one was open for 0% -> 0% of each run, Pallas kernels for 26% -> 31%
where the time goes in v4:
time: 37 us; the launch traced here: 36.8 us
  Pallas kernels  25.4 us (69%)
  starting transfers between devices  8.72 us (24%)
  waiting for transfers between devices  2.4 us (6%)
    pallas_call x1, Pallas kernels, partials(): pl.pallas_call(functools.partial(partial_kernel, rows // 2, lon), grid_sp...  11.3 us
    pallas_call x1, Pallas kernels, finish(): pl.pallas_call(functools.partial(finish_kernel, rows, lon, group, fluxes)...  9.64 us
    ppermute x3, starting transfers between devices, send(): lax.ppermute(block, 'lat', [(i, target(i) % count) for i in range(count)])  4.72 us
    pallas_call x1, Pallas kernels, surfaces(): pl.pallas_call(functools.partial(surface_kernel, rows, lon, group, fluxes...  4.44 us
    ppermute x1, starting transfers between devices, shards(): lax.ppermute(chip, 'lat', [(i, j) for i, j in links if component(i) == co...  4 us
    ppermute x3, waiting for transfers between devices, send(): lax.ppermute(block, 'lat', [(i, target(i) % count) for i in range(count)])  2.4 us
  transfers between devices with their start and end apart: 4, of which 1 were waited for; matrix products, arithmetic and copies ran while one was open for 0% of the time, Pallas kernels for 31%

profile of v4, /device:TPU:0, one launch (start us, length us, event | category | flops | bytes accessed | tf_op | source)
XLA Modules:
  0.0 36.8 jit_solution(12705700687346365454)
XLA Ops:
  0.0 0.0 copy-start.4
  0.0 4.4 %surface_fields.1 = (bf16[384,128]{1,0:T(8,128)(2,1)S(1)}, bf16[8,1440,128]{2,1,0:T(8,128)(2,1)S(1)}, bf16[1824,128]{1,0:T(8,128)(2,1)S(1)}, bf16[1440,128]{1,0:T(8,128)(2,1)S(1)}, bf16[1440,128]{1,0:T(8,128)(2,1)S(1)}) custom-call(s32[2]{0:T(128)S(1)} %compare_select_fusion.where, bf16[8,1440,128]{2,1,0:T(8,128)(2,1)} %x_ref.1, bf16[2,4,128]{2,1,0:T(4,128)(2,1)} %bitcast.5, ...), custom_call_target="tpu_custom_call" | custom-call | tf_op jit(solution)/shard_map/surface_fields/pallas_call | solution.py:102
  4.5 0.5 %collective-permute-start = (bf16[1824,128]{1,0:T(8,128)(2,1)S(1)}, bf16[1824,128]{1,0:T(8,128)(2,1)S(1)}, u32[]{:S(2)}, u32[]{:S(2)}) collective-permute-start(bf16[1824,128]{1,0:T(8,128)(2,1)S(1)} %get-tuple-element.16), channel_id=1, source_target_pairs={{0,1},{1,0},{2,3},{3,2},{4,5},{5,4},{6,7},{7,6},{8,9},{9,8},{10,11... | collective-permute-start | bytes 1400840 | tf_op jit(solution)/shard_map/ppermute | solution.py:311
  5.0 3.6 %collective-permute-start.3 = (bf16[384,128]{1,0:T(8,128)(2,1)S(1)}, bf16[384,128]{1,0:T(8,128)(2,1)S(1)}, u32[]{:S(2)}, u32[]{:S(2)}) collective-permute-start(bf16[384,128]{1,0:T(8,128)(2,1)S(1)} %get-tuple-element.18), channel_id=1, source_target_pairs={{0,7},{1,10},{2,9},{3,12},{4,11},{5,14},{6,13},{7,0},{8,15},{9,2},... | collective-permute-start | bytes 294920 | tf_op jit(solution)/shard_map/ppermute | solution.py:311
  8.6 4.0 %collective-permute-start.1 = (bf16[1440,128]{1,0:T(8,128)(2,1)S(1)}, bf16[1440,128]{1,0:T(8,128)(2,1)S(1)}, u32[]{:S(2)}, u32[]{:S(2)}) collective-permute-start(bf16[1440,128]{1,0:T(8,128)(2,1)S(1)} %get-tuple-element.17), channel_id=1, source_target_pairs={{0,15},{1,2},{2,1},{5,6},{6,5},{7,8},{8,7},{9,10},{10,9},{13,14},{... | collective-permute-start | bytes 1105928 | tf_op jit(solution)/shard_map/ppermute | solution.py:316
  12.6 0.0 collective-permute-done.pair_ref
  12.7 0.6 %collective-permute-start.2 = (bf16[768,128]{1,0:T(8,128)(2,1)S(1)}, bf16[768,128]{1,0:T(8,128)(2,1)S(1)}, u32[]{:S(2)}, u32[]{:S(2)}) collective-permute-start(bf16[768,128]{1,0:T(8,128)(2,1)S(1)} %pad_maximum_fusion), channel_id=1, source_target_pairs={{0,8},{1,9},{2,10},{3,11},{4,12},{5,13},{6,14},{7,15},{8,0},{9,1},... | collective-permute-start | bytes 589832 | tf_op jit(solution)/shard_map/ppermute | solution.py:311
  13.2 0.0 copy-done.4
  13.2 0.0 copy-start
  13.2 0.0 copy-start.1
  13.2 0.0 copy-start.2
  13.2 0.0 copy-start.3
  13.3 11.3 %own_rows.1 = (bf16[8,1440,512]{2,1,0:T(8,128)(2,1)S(1)}, bf16[2,384,512]{2,1,0:T(8,128)(2,1)S(1)}) custom-call(s32[2]{0:T(128)S(1)} %compare_select_fusion.where, bf16[8,1440,128]{2,1,0:T(8,128)(2,1)S(1)} %get-tuple-element.12.x_ref, bf16[2,1152,512]{2,1,0:T(8,128)(2,1)S(1)} %copy-done.4), custom_call_target="tpu_custom_call" | custom-call | flops 9059696640 | bytes 17694720 | tf_op jit(solution)/shard_map/own_rows/pallas_call | solution.py:172
  24.6 0.0 collective-permute-done.3.far_ref
  24.6 0.0 collective-permute-done.1.chip_ref
  24.6 2.4 %collective-permute-done.2.near_ref = bf16[768,128]{1,0:T(8,128)(2,1)S(1)} collective-permute-done((bf16[768,128]{1,0:T(8,128)(2,1)S(1)}, bf16[768,128]{1,0:T(8,128)(2,1)S(1)}, u32[]{:S(2)}, u32[]{:S(2)}) %collective-permute-start.2) | collective-permute-done | bytes 196640 | tf_op jit(solution)/shard_map/ppermute | solution.py:311
  27.0 0.0 copy-done
  27.0 0.0 copy-done.1
  27.0 0.0 copy-done.2
  27.0 0.0 copy-done.3
  27.0 9.6 %finish_rows.1 = bf16[8,1440,128]{2,1,0:T(8,128)(2,1)} custom-call(s32[2]{0:T(128)S(1)} %compare_select_fusion.where, s32[3,2,64]{2,1,0:T(2,128)S(1)} %bitcast.3, f32[3,2,64]{2,1,0:T(2,128)S(1)} %bitcast.4, bf16[8,1440,128]{2,1,0:T(8,128)(2,1)S(1)} %get-tuple-element.12.x_ref, bf16[8,1440,512]{2,1,0:T(8,128)(2,1)S(1)} %get-tuple-element.13.part_ref, ...), custom_call_target="tpu_custom_call" | custom-call | tf_op jit(solution)/shard_map/finish_rows/pallas_call | solution.py:270
  (3 shorter events, 0.0 us)
Async XLA Ops:
  0.0 13.2 %copy-start.4 = (bf16[2,1152,512]{2,1,0:T(8,128)(2,1)S(1)}, bf16[2,1152,512]{2,1,0:T(8,128)(2,1)}, u32[]{:S(2)}) copy-start(bf16[2,1152,512]{2,1,0:T(8,128)(2,1)} %w_ref.1) | copy-start | bytes 7077892
  4.5 8.2 %collective-permute-start = (bf16[1824,128]{1,0:T(8,128)(2,1)S(1)}, bf16[1824,128]{1,0:T(8,128)(2,1)S(1)}, u32[]{:S(2)}, u32[]{:S(2)}) collective-permute-start(bf16[1824,128]{1,0:T(8,128)(2,1)S(1)} %get-tuple-element.16), channel_id=1, source_target_pairs={{0,1},{1,0},{2,3},{3,2},{4,5},{5,4},{6,7},{7,6},{8,9},{9,8},{10,11... | collective-permute-start | bytes 1400840 | tf_op jit(solution)/shard_map/ppermute | solution.py:311
  5.0 19.6 %collective-permute-start.3 = (bf16[384,128]{1,0:T(8,128)(2,1)S(1)}, bf16[384,128]{1,0:T(8,128)(2,1)S(1)}, u32[]{:S(2)}, u32[]{:S(2)}) collective-permute-start(bf16[384,128]{1,0:T(8,128)(2,1)S(1)} %get-tuple-element.18), channel_id=1, source_target_pairs={{0,7},{1,10},{2,9},{3,12},{4,11},{5,14},{6,13},{7,0},{8,15},{9,2},... | collective-permute-start | bytes 294920 | tf_op jit(solution)/shard_map/ppermute | solution.py:311
  8.6 16.0 %collective-permute-start.1 = (bf16[1440,128]{1,0:T(8,128)(2,1)S(1)}, bf16[1440,128]{1,0:T(8,128)(2,1)S(1)}, u32[]{:S(2)}, u32[]{:S(2)}) collective-permute-start(bf16[1440,128]{1,0:T(8,128)(2,1)S(1)} %get-tuple-element.17), channel_id=1, source_target_pairs={{0,15},{1,2},{2,1},{5,6},{6,5},{7,8},{8,7},{9,10},{10,9},{13,14},{... | collective-permute-start | bytes 1105928 | tf_op jit(solution)/shard_map/ppermute | solution.py:316
  12.7 14.3 %collective-permute-start.2 = (bf16[768,128]{1,0:T(8,128)(2,1)S(1)}, bf16[768,128]{1,0:T(8,128)(2,1)S(1)}, u32[]{:S(2)}, u32[]{:S(2)}) collective-permute-start(bf16[768,128]{1,0:T(8,128)(2,1)S(1)} %pad_maximum_fusion), channel_id=1, source_target_pairs={{0,8},{1,9},{2,10},{3,11},{4,12},{5,13},{6,14},{7,15},{8,0},{9,1},... | collective-permute-start | bytes 589832 | tf_op jit(solution)/shard_map/ppermute | solution.py:311
  13.2 13.8 %copy-start = (bf16[2,512,128]{2,1,0:T(8,128)(2,1)S(1)}, bf16[2,512,128]{2,1,0:T(8,128)(2,1)}, u32[]{:S(2)}) copy-start(bf16[2,512,128]{2,1,0:T(8,128)(2,1)} %o_ref.1) | copy-start | bytes 786436
  13.2 13.8 %copy-start.1 = (bf16[2,4,512]{2,1,0:T(4,128)(2,1)S(1)}, bf16[2,4,512]{2,1,0:T(4,128)(2,1)}, u32[]{:S(2)}) copy-start(bf16[2,4,512]{2,1,0:T(4,128)(2,1)} %f_ref.1) | copy-start | bytes 24580
  13.2 13.8 %copy-start.2 = (s32[2,64,3]{1,0,2:T(2,128)S(1)}, s32[2,64,3]{1,0,2:T(2,128)}, u32[]{:S(2)}) copy-start(s32[2,64,3]{1,0,2:T(2,128)} %param.13) | copy-start | bytes 4612
  13.2 13.8 %copy-start.3 = (f32[2,64,3]{1,0,2:T(2,128)S(1)}, f32[2,64,3]{1,0,2:T(2,128)}, u32[]{:S(2)}) copy-start(f32[2,64,3]{1,0,2:T(2,128)} %param.14) | copy-start | bytes 4612

commit v5 on v4

--- a/solution.py
+++ b/solution.py
@@ -71,7 +71,8 @@
         if k + 2 < rows // 2:
             loads.append(load(k + 2))
         both = jnp.concatenate([xv_ref[2 * k], xv_ref[2 * k + 1]], axis=1)
-        fields = dot(both, jnp.concatenate(halves, axis=0))
+        mixed = jnp.concatenate(halves, axis=0)
+        fields = jnp.concatenate([dot(both[: lon // 2], mixed), dot(both[lon // 2 :], mixed)], axis=0)
         total = fields if total is None else total + fields
     total = total * mask
     packed = jnp.zeros((group, 128), F32)
@@ -130,7 +131,7 @@
     )
 
 
-def partial_kernel(pairs, lon, where, x_ref, w_ref, out_ref, we, wy, wm, tf):
+def partial_kernel(pairs, lon, fluxes, where, table, weights, x_ref, w_ref, f_ref, out_ref, we, wy, wm, tf):
     def tap(a, b):
         return w_ref[0, (a * 3 + b) * 128 : (a * 3 + b + 1) * 128, :].astype(F32) * 0.5
 
@@ -142,9 +143,24 @@
         ends = tap(0, b) + tap(2, b)
         wm[0, k * 128 : (k + 1) * 128, :] = (0.5 * (ends + tap(1, b))).astype(BF)
         wm[1, k * 128 : (k + 1) * 128, :] = (0.5 * (ends - tap(1, b))).astype(BF)
-    for e, a in enumerate((0, 2)):
+    rows = 2 * pairs
+    hidden = f_ref.shape[2]
+    at = sublane((128, hidden)) % fluxes
+    spread = jnp.zeros((128, hidden), F32)
+    for f in range(fluxes):
+        spread = jnp.where(at == f, f_ref[0, f : f + 1, :].astype(F32) * 0.5, spread)
+
+    def finishing_weights(r):
         for k, b in enumerate((0, 2, 1)):
-            we[e, k * 128 : (k + 1) * 128, :] = tap(a, b).astype(BF)
+            if k == 2 or r in (0, rows - 1):
+                we[r, k * 128 : (k + 1) * 128, :] = tap(2 * (r % 2), b).astype(BF)
+        share = jnp.zeros((128, 128), F32)
+        row = where[1] * rows + r
+        for m in range(table.shape[0]):
+            local = table[m, where[0], row] - (where[1] - 1) * rows
+            share += jnp.where(sublane((128, 128)) // fluxes == local, weights[m, where[0], row], 0.0)
+        share = jnp.concatenate([share] * (hidden // 128), axis=1)
+        we[r, 384:512, :] = (share * spread).astype(BF)
 
     for pair in range(pairs):
         slot = pair % tf.shape[0]
@@ -163,22 +179,29 @@
         m1 = dot(jnp.concatenate(sides(1), axis=1), wm[0])
         m2 = dot(jnp.concatenate(sides(2), axis=1), wm[1])
         out_ref[2 * pair] = (dot(jnp.concatenate(sides(0) + own, axis=1), wy[0]) + (m1 + m2)).astype(BF)
+        finishing_weights(2 * pair)
+        finishing_weights(2 * pair + 1)
         out_ref[2 * pair + 1] = (dot(jnp.concatenate(sides(3) + own, axis=1), wy[1]) + (m1 - m2)).astype(BF)
 
 
-def partials(where, xv, inner_weight):
+def partials(where, xv, inner_weight, forcing_in, table, weights):
     rows, lon, channels = xv.shape
     depth, hidden = inner_weight.shape[1:]
+    fluxes = forcing_in.shape[1]
+    scalars = pl.BlockSpec(memory_space=pltpu.SMEM)
     return pl.pallas_call(
-        functools.partial(partial_kernel, rows // 2, lon),
+        functools.partial(partial_kernel, rows // 2, lon, fluxes),
         grid_spec=pltpu.PrefetchScalarGridSpec(
             num_scalar_prefetch=1,
             grid=(1,),
             in_specs=[
+                scalars,
+                scalars,
                 held(),
                 pl.BlockSpec(
                     (1, depth, hidden), lambda i, s: (s[0], 0, 0), pipeline_mode=pl.Buffered(1)
                 ),
+                pl.BlockSpec((1, fluxes, hidden), lambda i, s: (s[0], 0, 0)),
             ],
             out_specs=[held()] * 2,
             scratch_shapes=[
@@ -189,29 +212,25 @@
         ),
         out_shape=[
             pltpu.VMEM((rows, lon, hidden), BF),
-            pltpu.VMEM((2, 3 * channels, hidden), BF),
+            pltpu.VMEM((rows, 4 * channels, hidden), BF),
         ],
-        compiler_params=limits(34),
+        compiler_params=limits(24),
         cost_estimate=pl.CostEstimate(
             flops=rows * lon * 6 * channels * hidden * 2,
             bytes_accessed=rows * lon * (hidden + 2 * channels) * 2,
             transcendentals=0,
         ),
         name="own_rows",
-    )(where, xv, inner_weight)
+    )(
+        where, jnp.transpose(table, (2, 0, 1)), jnp.transpose(weights, (2, 0, 1)), xv, inner_weight, forcing_in
+    )
 
 
 def finish_kernel(
-    rows, lon, group, fluxes, where, table, weights, x_ref, part_ref, taps_ref, mask_ref, pair_ref, chip_ref,
-    near_ref, far_ref, f_ref, o_ref, out_ref, halo, window, we, spread, done, sems,
+    rows, lon, group, fluxes, where, x_ref, part_ref, we, mask_ref, pair_ref, chip_ref, near_ref, far_ref,
+    o_ref, out_ref, halo, window, done, sems,
 ):
     even = where[1] % 2 == 0
-    swap = pair_ref[0:lon, :].astype(F32)
-    chip = chip_ref[...].astype(F32)
-    for e, v in enumerate((jnp.where(even, chip, swap), jnp.where(even, swap, chip))):
-        halo[e, 8 : 8 + lon, :] = v
-        halo[e, 7:8, :] = v[lon - 1 : lon]
-        halo[e, 8 + lon : 9 + lon, :] = v[0:1]
     center = near_ref[0:group, :].astype(F32)
     other = near_ref[group : 2 * group, :].astype(F32)
     far = far_ref[...].astype(F32)
@@ -225,25 +244,18 @@
             moved = pltpu.roll(pack, shift, 1) if shift else pack
             total = jnp.where(owner == w, moved, total)
         window[g * group : g * group + size, :] = total[0:size].astype(BF)
-    at = sublane((128, spread.shape[1])) % fluxes
-    total = jnp.zeros(spread.shape, F32)
-    for f in range(fluxes):
-        total = jnp.where(at == f, f_ref[0, f : f + 1, :].astype(F32) * 0.5, total)
-    spread[...] = total
-    slot = sublane((128, 128)) // fluxes
     copies = []
-    for r in range(rows):
+    for r in list(range(1, rows - 1)) + [0, rows - 1]:
         parity = r % 2
         edge = r in (0, rows - 1)
-        share = jnp.zeros((128, 128), F32)
-        row = where[1] * rows + r
-        for m in range(table.shape[0]):
-            local = table[m, where[0], row] - (where[1] - 1) * rows
-            share += jnp.where(slot == local, weights[m, where[0], row], 0.0)
-        share = jnp.concatenate([share] * (spread.shape[1] // 128), axis=1)
         base = 0 if edge else 256
-        we[r, base:384, :] = taps_ref[parity, base:384, :]
-        we[r, 384:512, :] = (share * spread[...]).astype(BF)
+        if r == 0:
+            swap = pair_ref[0:lon, :].astype(F32)
+            chip = chip_ref[...].astype(F32)
+            for e, v in enumerate((jnp.where(even, chip, swap), jnp.where(even, swap, chip))):
+                halo[e, 8 : 8 + lon, :] = v
+                halo[e, 7:8, :] = v[lon - 1 : lon]
+                halo[e, 8 + lon : 9 + lon, :] = v[0:1]
         if edge:
             lhs = [halo[parity, k : k + lon, :].astype(BF) for k in (7, 9, 8)]
         else:
@@ -261,37 +273,31 @@
         copy.wait()
 
 
-def finish(where, xv, part, taps, mask, received, forcing_in, outer_weight, table, weights):
+def finish(where, xv, part, taps, mask, received, outer_weight, fluxes):
     rows, lon, channels = xv.shape
     hidden = part.shape[2]
-    fluxes = forcing_in.shape[1]
     group = received[3].shape[0]
-    scalars = pl.BlockSpec(memory_space=pltpu.SMEM)
     return pl.pallas_call(
         functools.partial(finish_kernel, rows, lon, group, fluxes),
         grid_spec=pltpu.PrefetchScalarGridSpec(
             num_scalar_prefetch=1,
             grid=(1,),
-            in_specs=[scalars, scalars] + [held()] * 8 + [
-                pl.BlockSpec((1, fluxes, hidden), lambda r, s: (s[0], 0, 0)),
+            in_specs=[held()] * 8 + [
                 pl.BlockSpec((1, hidden, channels), lambda r, s: (s[0], 0, 0)),
             ],
             out_specs=pl.BlockSpec(memory_space=pltpu.HBM),
             scratch_shapes=[
                 pltpu.VMEM((2, lon + 16, channels), F32),
                 pltpu.VMEM((lon, 128), BF),
-                pltpu.VMEM((rows, 512, hidden), BF),
-                pltpu.VMEM((128, hidden), F32),
                 pltpu.VMEM((rows, lon, channels), BF),
                 pltpu.SemaphoreType.DMA((rows,)),
             ],
         ),
         out_shape=jax.ShapeDtypeStruct((rows, lon, channels), BF),
-        compiler_params=limits(34),
+        compiler_params=limits(20),
         name="finish_rows",
     )(
-        where, jnp.transpose(table, (2, 0, 1)), jnp.transpose(weights, (2, 0, 1)), xv, part, taps, mask,
-        *received, forcing_in, outer_weight,
+        where, xv, part, taps, mask, *received, outer_weight
     )
 
 
@@ -313,12 +319,14 @@
     pack, xv, pair, chip, mask = surfaces(where, state, surface_proj, wet_mask, group)
     pair = send(pair, lambda i: i + 1 - 2 * (i % 2))
     links = [(i, (i + (1 if i % 2 else -1)) % count) for i in range(count)]
+    far = send(pack, lambda i: i + half + (1 if i % 2 else -1))
+    near = jnp.concatenate([pack, pair[lon:]], axis=0)
+    near, chip = lax.optimization_barrier((near, chip))
+    near = send(near, lambda i: i + half)
     chip = lax.ppermute(chip, "lat", [(i, j) for i, j in links if component(i) == component(j)])
-    far = send(pack, lambda i: i + half + (1 if i % 2 else -1))
-    near = send(jnp.concatenate([pack, pair[lon:]], axis=0), lambda i: i + half)
-    part, taps = partials(where, xv, inner_weight)
+    part, taps = partials(where, xv, inner_weight, forcing_in, margin_rows, margin_weights)
     return finish(
-        where, xv, part, taps, mask, (pair, chip, near, far), forcing_in, outer_weight, margin_rows, margin_weights
+        where, xv, part, taps, mask, (pair, chip, near, far), outer_weight, forcing_in.shape[1]
     )
 
 

time: 37 us -> 35.6 us (0.962)
  waiting for transfers between devices: 2.4 us -> 0.01 us
  starting transfers between devices: 8.72 us -> 9.64 us
    ppermute x3, waiting for transfers between devices: 2.4 us -> 0.01 us  [send(): lax.ppermute(block, 'lat', [(i, target(i) % count) for i in range(count)])]
    ppermute x3, starting transfers between devices: 4.72 us -> 6.81 us  [send(): lax.ppermute(block, 'lat', [(i, target(i) % count) for i in range(count)])]
    ppermute x1, starting transfers between devices: 4 us -> 2.83 us  [shards(): lax.ppermute(chip, 'lat', [(i, j) for i, j in links if component(i) == co...]
    pallas_call x1, Pallas kernels: 11.3 us -> 12.4 us  [partials(): pl.pallas_call(functools.partial(partial_kernel, rows // 2, lon, fluxes),...]
    pallas_call x1, Pallas kernels: 9.64 us -> 9.07 us  [finish(): pl.pallas_call(functools.partial(finish_kernel, rows, lon, group, fluxes)...]
    pallas_call x1, Pallas kernels: 4.44 us -> 3.99 us  [surfaces(): pl.pallas_call(functools.partial(surface_kernel, rows, lon, group, fluxes...]
  transfers between devices with their start and end apart: 4 -> 4, of which waited for: 1 -> 0; matrix products, arithmetic and copies ran while one was open for 0% -> 0% of each run, Pallas kernels for 31% -> 35%
where the time goes in v5:
time: 35.6 us; the launch traced here: 35.5 us
  Pallas kernels  25.5 us (72%)
  starting transfers between devices  9.64 us (27%)
    pallas_call x1, Pallas kernels, partials(): pl.pallas_call(functools.partial(partial_kernel, rows // 2, lon, fluxes),...  12.4 us
    pallas_call x1, Pallas kernels, finish(): pl.pallas_call(functools.partial(finish_kernel, rows, lon, group, fluxes)...  9.07 us
    ppermute x3, starting transfers between devices, send(): lax.ppermute(block, 'lat', [(i, target(i) % count) for i in range(count)])  6.81 us
    pallas_call x1, Pallas kernels, surfaces(): pl.pallas_call(functools.partial(surface_kernel, rows, lon, group, fluxes...  3.99 us
    ppermute x1, starting transfers between devices, shards(): lax.ppermute(chip, 'lat', [(i, j) for i, j in links if component(i) == co...  2.83 us
  transfers between devices with their start and end apart: 4, of which 0 were waited for; matrix products, arithmetic and copies ran while one was open for 0% of the time, Pallas kernels for 35%

profile of v5, /device:TPU:0, one launch (start us, length us, event | category | flops | bytes accessed | tf_op | source)
XLA Modules:
  0.0 35.5 jit_solution(3019370841881312946)
XLA Ops:
  0.0 0.0 copy-start.4
  0.0 0.0 copy-start.3
  0.0 0.0 copy-start.2
  0.0 0.0 copy-start.1
  0.0 4.0 %surface_fields.1 = (bf16[384,128]{1,0:T(8,128)(2,1)S(1)}, bf16[8,1440,128]{2,1,0:T(8,128)(2,1)S(1)}, bf16[1824,128]{1,0:T(8,128)(2,1)S(1)}, bf16[1440,128]{1,0:T(8,128)(2,1)S(1)}, bf16[1440,128]{1,0:T(8,128)(2,1)S(1)}) custom-call(s32[2]{0:T(128)S(1)} %compare_select_fusion.where, bf16[8,1440,128]{2,1,0:T(8,128)(2,1)} %x_ref.1, bf16[2,4,128]{2,1,0:T(4,128)(2,1)} %bitcast.5, ...), custom_call_target="tpu_custom_call" | custom-call | tf_op jit(solution)/shard_map/surface_fields/pallas_call | solution.py:103
  4.0 0.5 %collective-permute-start = (bf16[1824,128]{1,0:T(8,128)(2,1)S(1)}, bf16[1824,128]{1,0:T(8,128)(2,1)S(1)}, u32[]{:S(2)}, u32[]{:S(2)}) collective-permute-start(bf16[1824,128]{1,0:T(8,128)(2,1)S(1)} %get-tuple-element.18), channel_id=1, source_target_pairs={{0,1},{1,0},{2,3},{3,2},{4,5},{5,4},{6,7},{7,6},{8,9},{9,8},{10,11... | collective-permute-start | bytes 1400840 | tf_op jit(solution)/shard_map/ppermute | solution.py:317
  4.5 3.6 %collective-permute-start.3 = (bf16[384,128]{1,0:T(8,128)(2,1)S(1)}, bf16[384,128]{1,0:T(8,128)(2,1)S(1)}, u32[]{:S(2)}, u32[]{:S(2)}) collective-permute-start(bf16[384,128]{1,0:T(8,128)(2,1)S(1)} %get-tuple-element.19), channel_id=1, source_target_pairs={{0,7},{1,10},{2,9},{3,12},{4,11},{5,14},{6,13},{7,0},{8,15},{9,2},... | collective-permute-start | bytes 294920 | tf_op jit(solution)/shard_map/ppermute | solution.py:317
  8.2 0.0 collective-permute-done.pair_ref
  8.2 2.7 %collective-permute-start.2 = (bf16[768,128]{1,0:T(8,128)(2,1)S(1)}, bf16[768,128]{1,0:T(8,128)(2,1)S(1)}, u32[]{:S(2)}, u32[]{:S(2)}) collective-permute-start(bf16[768,128]{1,0:T(8,128)(2,1)S(1)} %pad_maximum_fusion), channel_id=1, source_target_pairs={{0,8},{1,9},{2,10},{3,11},{4,12},{5,13},{6,14},{7,15},{8,0},{9,1},... | collective-permute-start | bytes 589832 | tf_op jit(solution)/shard_map/ppermute | solution.py:317
  10.9 2.8 %collective-permute-start.1 = (bf16[1440,128]{1,0:T(8,128)(2,1)S(1)}, bf16[1440,128]{1,0:T(8,128)(2,1)S(1)}, u32[]{:S(2)}, u32[]{:S(2)}) collective-permute-start(bf16[1440,128]{1,0:T(8,128)(2,1)S(1)} %get-tuple-element.21), channel_id=1, source_target_pairs={{0,15},{1,2},{2,1},{5,6},{6,5},{7,8},{8,7},{9,10},{10,9},{13,14},{... | collective-permute-start | bytes 1105928 | tf_op jit(solution)/shard_map/ppermute | solution.py:326
  13.7 0.0 copy-done.4
  13.7 0.0 copy-done.3
  13.7 0.0 copy-done.2
  13.7 0.0 copy-done.1
  13.7 0.0 copy-start
  13.8 12.4 %own_rows.1 = (bf16[8,1440,512]{2,1,0:T(8,128)(2,1)S(1)}, bf16[8,512,512]{2,1,0:T(8,128)(2,1)S(1)}) custom-call(s32[2]{0:T(128)S(1)} %compare_select_fusion.where, s32[3,2,64]{2,1,0:T(2,128)S(1)} %bitcast.3, f32[3,2,64]{2,1,0:T(2,128)S(1)} %bitcast.4, bf16[8,1440,128]{2,1,0:T(8,128)(2,1)S(1)} %get-tuple-element.14.x_ref, ...), custom_call_target="tpu_custom_call" | custom-call | flops 9059696640 | bytes 17694720 | tf_op jit(solution)/shard_map/own_rows/pallas_call | solution.py:192
  26.2 0.0 collective-permute-done.3.far_ref
  26.2 0.0 collective-permute-done.2.near_ref
  26.2 0.0 collective-permute-done.1.chip_ref
  26.2 0.0 copy-done
  26.2 9.1 %finish_rows.1 = bf16[8,1440,128]{2,1,0:T(8,128)(2,1)} custom-call(s32[2]{0:T(128)S(1)} %compare_select_fusion.where, bf16[8,1440,128]{2,1,0:T(8,128)(2,1)S(1)} %get-tuple-element.14.x_ref, bf16[8,1440,512]{2,1,0:T(8,128)(2,1)S(1)} %get-tuple-element.15.part_ref, bf16[8,512,512]{2,1,0:T(8,128)(2,1)S(1)} %get-tuple-element.16.we, ...), custom_call_target="tpu_custom_call" | custom-call | tf_op jit(solution)/shard_map/finish_rows/pallas_call | solution.py:280
  (3 shorter events, 0.0 us)
Async XLA Ops:
  0.0 13.7 %copy-start.4 = (f32[2,64,3]{1,0,2:T(2,128)S(1)}, f32[2,64,3]{1,0,2:T(2,128)}, u32[]{:S(2)}) copy-start(f32[2,64,3]{1,0,2:T(2,128)} %param.14) | copy-start | bytes 4612
  0.0 13.7 %copy-start.3 = (s32[2,64,3]{1,0,2:T(2,128)S(1)}, s32[2,64,3]{1,0,2:T(2,128)}, u32[]{:S(2)}) copy-start(s32[2,64,3]{1,0,2:T(2,128)} %param.13) | copy-start | bytes 4612
  0.0 13.7 %copy-start.2 = (bf16[2,4,512]{2,1,0:T(4,128)(2,1)S(1)}, bf16[2,4,512]{2,1,0:T(4,128)(2,1)}, u32[]{:S(2)}) copy-start(bf16[2,4,512]{2,1,0:T(4,128)(2,1)} %f_ref.1) | copy-start | bytes 24580
  0.0 13.7 %copy-start.1 = (bf16[2,1152,512]{2,1,0:T(8,128)(2,1)S(1)}, bf16[2,1152,512]{2,1,0:T(8,128)(2,1)}, u32[]{:S(2)}) copy-start(bf16[2,1152,512]{2,1,0:T(8,128)(2,1)} %w_ref.1) | copy-start | bytes 7077892
  4.0 4.2 %collective-permute-start = (bf16[1824,128]{1,0:T(8,128)(2,1)S(1)}, bf16[1824,128]{1,0:T(8,128)(2,1)S(1)}, u32[]{:S(2)}, u32[]{:S(2)}) collective-permute-start(bf16[1824,128]{1,0:T(8,128)(2,1)S(1)} %get-tuple-element.18), channel_id=1, source_target_pairs={{0,1},{1,0},{2,3},{3,2},{4,5},{5,4},{6,7},{7,6},{8,9},{9,8},{10,11... | collective-permute-start | bytes 1400840 | tf_op jit(solution)/shard_map/ppermute | solution.py:317
  4.5 21.7 %collective-permute-start.3 = (bf16[384,128]{1,0:T(8,128)(2,1)S(1)}, bf16[384,128]{1,0:T(8,128)(2,1)S(1)}, u32[]{:S(2)}, u32[]{:S(2)}) collective-permute-start(bf16[384,128]{1,0:T(8,128)(2,1)S(1)} %get-tuple-element.19), channel_id=1, source_target_pairs={{0,7},{1,10},{2,9},{3,12},{4,11},{5,14},{6,13},{7,0},{8,15},{9,2},... | collective-permute-start | bytes 294920 | tf_op jit(solution)/shard_map/ppermute | solution.py:317
  8.2 18.0 %collective-permute-start.2 = (bf16[768,128]{1,0:T(8,128)(2,1)S(1)}, bf16[768,128]{1,0:T(8,128)(2,1)S(1)}, u32[]{:S(2)}, u32[]{:S(2)}) collective-permute-start(bf16[768,128]{1,0:T(8,128)(2,1)S(1)} %pad_maximum_fusion), channel_id=1, source_target_pairs={{0,8},{1,9},{2,10},{3,11},{4,12},{5,13},{6,14},{7,15},{8,0},{9,1},... | collective-permute-start | bytes 589832 | tf_op jit(solution)/shard_map/ppermute | solution.py:317
  10.9 15.4 %collective-permute-start.1 = (bf16[1440,128]{1,0:T(8,128)(2,1)S(1)}, bf16[1440,128]{1,0:T(8,128)(2,1)S(1)}, u32[]{:S(2)}, u32[]{:S(2)}) collective-permute-start(bf16[1440,128]{1,0:T(8,128)(2,1)S(1)} %get-tuple-element.21), channel_id=1, source_target_pairs={{0,15},{1,2},{2,1},{5,6},{6,5},{7,8},{8,7},{9,10},{10,9},{13,14},{... | collective-permute-start | bytes 1105928 | tf_op jit(solution)/shard_map/ppermute | solution.py:326
  13.7 12.5 %copy-start = (bf16[2,512,128]{2,1,0:T(8,128)(2,1)S(1)}, bf16[2,512,128]{2,1,0:T(8,128)(2,1)}, u32[]{:S(2)}) copy-start(bf16[2,512,128]{2,1,0:T(8,128)(2,1)} %o_ref.1) | copy-start | bytes 786436

commit v6 on v5

--- a/solution.py
+++ b/solution.py
@@ -32,8 +32,8 @@
 
 
 def surface_kernel(
-    rows, lon, group, fluxes, where, x_ref, proj_ref, wet_ref, out_ref, xv_ref, pair_ref, chip_ref, mask_ref,
-    proj, wets, sems
+    rows, lon, group, fluxes, where, x_ref, proj_ref, wet_ref, f_ref, table_ref, margin_ref, w_ref, out_ref,
+    xv_ref, pair_ref, chip_ref, mask_ref, force_ref, wv_ref, proj, wets, fmap, table, margin, sems,
 ):
     def load(k):
         both = pl.ds(2 * k, 2)
@@ -47,12 +47,28 @@
         pltpu.make_async_copy(
             wet_ref.at[pl.ds(pl.multiple_of(where[1] * rows, rows), rows)], wets, sems.at[rows // 2 + 1]
         ),
+        pltpu.make_async_copy(f_ref.at[where[0]], fmap, sems.at[rows // 2 + 2]),
+        pltpu.make_async_copy(table_ref, table, sems.at[rows // 2 + 3]),
+        pltpu.make_async_copy(margin_ref, margin, sems.at[rows // 2 + 4]),
     ]
     for copy in small:
         copy.start()
-    loads.append(load(1))
+    loads += [load(k) for k in range(1, rows // 2)]
     for copy in small:
         copy.wait()
+    hidden = fmap.shape[1]
+    at = sublane((128, hidden)) % fluxes
+    spread = jnp.zeros((128, hidden), F32)
+    for f in range(fluxes):
+        spread = jnp.where(at == f, fmap[f : f + 1, :].astype(F32) * 0.5, spread)
+    for r in range(rows):
+        share = jnp.zeros((128, 128), F32)
+        row = where[1] * rows + r
+        for m in range(table.shape[0]):
+            local = table[m, where[0], row] - (where[1] - 1) * rows
+            share += jnp.where(sublane((128, 128)) // fluxes == local, margin[m, where[0], row], 0.0)
+        share = jnp.concatenate([share] * (hidden // 128), axis=1)
+        force_ref[r] = (share * spread).astype(BF)
     even = where[1] % 2 == 0
     channels = x_ref.shape[2]
     pick = (lane((rows, 128)) // fluxes == sublane((rows, 128))).astype(BF)
@@ -68,8 +84,9 @@
     for k in range(rows // 2):
         halves = [jnp.where(owner == 2 * k + e, tiled, jnp.zeros_like(tiled)) for e in (0, 1)]
         loads[k].wait()
-        if k + 2 < rows // 2:
-            loads.append(load(k + 2))
+        if k == 0:
+            inner = pltpu.make_async_copy(w_ref.at[where[0]], wv_ref, sems.at[rows // 2 + 5])
+            inner.start()
         both = jnp.concatenate([xv_ref[2 * k], xv_ref[2 * k + 1]], axis=1)
         mixed = jnp.concatenate(halves, axis=0)
         fields = jnp.concatenate([dot(both[: lon // 2], mixed), dot(both[lon // 2 :], mixed)], axis=0)
@@ -87,6 +104,7 @@
     pair_ref[0:lon, :] = xv_ref[jnp.where(even, rows - 1, 0)]
     pair_ref[lon : lon + group, :] = packed
     chip_ref[...] = xv_ref[jnp.where(even, 0, rows - 1)]
+    inner.wait()
 
 
 def in_hbm(x):
@@ -97,7 +115,8 @@
     return pl.BlockSpec(memory_space=pltpu.VMEM)
 
 
-def surfaces(where, state, surface_proj, wet_mask, group):
+def surfaces(where, state, surface_proj, wet_mask, forcing_in, table, weights, inner_weight, group):
+    depth, hidden = inner_weight.shape[1:]
     rows, lon, channels = state.shape
     fluxes = surface_proj.shape[2]
     return pl.pallas_call(
@@ -105,16 +124,15 @@
         grid_spec=pltpu.PrefetchScalarGridSpec(
             num_scalar_prefetch=1,
             grid=(1,),
-            in_specs=[
-                pl.BlockSpec(memory_space=pltpu.HBM),
-                pl.BlockSpec(memory_space=pltpu.HBM),
-                pl.BlockSpec(memory_space=pltpu.HBM),
-            ],
-            out_specs=[held()] * 5,
+            in_specs=[pl.BlockSpec(memory_space=pltpu.HBM)] * 7,
+            out_specs=[held()] * 7,
             scratch_shapes=[
                 pltpu.VMEM((fluxes, channels), BF),
                 pltpu.VMEM((rows, lon), jnp.int32),
-                pltpu.SemaphoreType.DMA((rows // 2 + 2,)),
+                pltpu.VMEM((fluxes, hidden), BF),
+                pltpu.SMEM(table.shape, jnp.int32),
+                pltpu.SMEM(table.shape, F32),
+                pltpu.SemaphoreType.DMA((rows // 2 + 6,)),
             ],
         ),
         out_shape=[
@@ -123,17 +141,25 @@
             pltpu.VMEM((lon + group, channels), BF),
             pltpu.VMEM((lon, channels), BF),
             pltpu.VMEM((lon, 128), BF),
+            pltpu.VMEM((rows, 128, hidden), BF),
+            pltpu.VMEM((depth, hidden), BF),
         ],
         compiler_params=limits(16),
         name="surface_fields",
     )(
-        where, in_hbm(state), in_hbm(jnp.swapaxes(surface_proj, 1, 2)), in_hbm(wet_mask)
-    )
-
-
-def partial_kernel(pairs, lon, fluxes, where, table, weights, x_ref, w_ref, f_ref, out_ref, we, wy, wm, tf):
+        where,
+        *[
+            in_hbm(x)
+            for x in (
+                state, jnp.swapaxes(surface_proj, 1, 2), wet_mask, forcing_in, table, weights, inner_weight
+            )
+        ],
+    )
+
+
+def partial_kernel(pairs, lon, x_ref, w_ref, out_ref, we, wy, wm, tf):
     def tap(a, b):
-        return w_ref[0, (a * 3 + b) * 128 : (a * 3 + b + 1) * 128, :].astype(F32) * 0.5
+        return w_ref[(a * 3 + b) * 128 : (a * 3 + b + 1) * 128, :].astype(F32) * 0.5
 
     for k, (a, b) in enumerate(((0, 0), (0, 2), (1, 1), (2, 1))):
         wy[0, k * 128 : (k + 1) * 128, :] = tap(a, b).astype(BF)
@@ -143,24 +169,9 @@
         ends = tap(0, b) + tap(2, b)
         wm[0, k * 128 : (k + 1) * 128, :] = (0.5 * (ends + tap(1, b))).astype(BF)
         wm[1, k * 128 : (k + 1) * 128, :] = (0.5 * (ends - tap(1, b))).astype(BF)
-    rows = 2 * pairs
-    hidden = f_ref.shape[2]
-    at = sublane((128, hidden)) % fluxes
-    spread = jnp.zeros((128, hidden), F32)
-    for f in range(fluxes):
-        spread = jnp.where(at == f, f_ref[0, f : f + 1, :].astype(F32) * 0.5, spread)
-
-    def finishing_weights(r):
+    for e, a in enumerate((0, 2)):
         for k, b in enumerate((0, 2, 1)):
-            if k == 2 or r in (0, rows - 1):
-                we[r, k * 128 : (k + 1) * 128, :] = tap(2 * (r % 2), b).astype(BF)
-        share = jnp.zeros((128, 128), F32)
-        row = where[1] * rows + r
-        for m in range(table.shape[0]):
-            local = table[m, where[0], row] - (where[1] - 1) * rows
-            share += jnp.where(sublane((128, 128)) // fluxes == local, weights[m, where[0], row], 0.0)
-        share = jnp.concatenate([share] * (hidden // 128), axis=1)
-        we[r, 384:512, :] = (share * spread).astype(BF)
+            we[e, k * 128 : (k + 1) * 128, :] = tap(a, b).astype(BF)
 
     for pair in range(pairs):
         slot = pair % tf.shape[0]
@@ -179,55 +190,37 @@
         m1 = dot(jnp.concatenate(sides(1), axis=1), wm[0])
         m2 = dot(jnp.concatenate(sides(2), axis=1), wm[1])
         out_ref[2 * pair] = (dot(jnp.concatenate(sides(0) + own, axis=1), wy[0]) + (m1 + m2)).astype(BF)
-        finishing_weights(2 * pair)
-        finishing_weights(2 * pair + 1)
         out_ref[2 * pair + 1] = (dot(jnp.concatenate(sides(3) + own, axis=1), wy[1]) + (m1 - m2)).astype(BF)
 
 
-def partials(where, xv, inner_weight, forcing_in, table, weights):
+def partials(xv, inner):
     rows, lon, channels = xv.shape
-    depth, hidden = inner_weight.shape[1:]
-    fluxes = forcing_in.shape[1]
-    scalars = pl.BlockSpec(memory_space=pltpu.SMEM)
+    hidden = inner.shape[1]
     return pl.pallas_call(
-        functools.partial(partial_kernel, rows // 2, lon, fluxes),
-        grid_spec=pltpu.PrefetchScalarGridSpec(
-            num_scalar_prefetch=1,
-            grid=(1,),
-            in_specs=[
-                scalars,
-                scalars,
-                held(),
-                pl.BlockSpec(
-                    (1, depth, hidden), lambda i, s: (s[0], 0, 0), pipeline_mode=pl.Buffered(1)
-                ),
-                pl.BlockSpec((1, fluxes, hidden), lambda i, s: (s[0], 0, 0)),
-            ],
-            out_specs=[held()] * 2,
-            scratch_shapes=[
-                pltpu.VMEM((2, 4 * channels, hidden), BF),
-                pltpu.VMEM((2, 2 * channels, hidden), BF),
-                pltpu.VMEM((1, 4, lon + 16, channels), F32),
-            ],
-        ),
+        functools.partial(partial_kernel, rows // 2, lon),
+        in_specs=[held()] * 2,
+        out_specs=[held()] * 2,
+        scratch_shapes=[
+            pltpu.VMEM((2, 4 * channels, hidden), BF),
+            pltpu.VMEM((2, 2 * channels, hidden), BF),
+            pltpu.VMEM((1, 4, lon + 16, channels), F32),
+        ],
         out_shape=[
             pltpu.VMEM((rows, lon, hidden), BF),
-            pltpu.VMEM((rows, 4 * channels, hidden), BF),
+            pltpu.VMEM((2, 3 * channels, hidden), BF),
         ],
-        compiler_params=limits(24),
+        compiler_params=pltpu.CompilerParams(vmem_limit_bytes=26 << 20),
         cost_estimate=pl.CostEstimate(
             flops=rows * lon * 6 * channels * hidden * 2,
             bytes_accessed=rows * lon * (hidden + 2 * channels) * 2,
             transcendentals=0,
         ),
         name="own_rows",
-    )(
-        where, jnp.transpose(table, (2, 0, 1)), jnp.transpose(weights, (2, 0, 1)), xv, inner_weight, forcing_in
-    )
+    )(xv, inner)
 
 
 def finish_kernel(
-    rows, lon, group, fluxes, where, x_ref, part_ref, we, mask_ref, pair_ref, chip_ref, near_ref, far_ref,
+    rows, lon, group, fluxes, where, x_ref, part_ref, taps_ref, force_ref, mask_ref, pair_ref, chip_ref, near_ref, far_ref,
     o_ref, out_ref, halo, window, done, sems,
 ):
     even = where[1] % 2 == 0
@@ -260,7 +253,7 @@
             lhs = [halo[parity, k : k + lon, :].astype(BF) for k in (7, 9, 8)]
         else:
             lhs = [x_ref[r + 1 if parity else r - 1]]
-        total = dot(jnp.concatenate(lhs + [window[...]], axis=1), we[r, base:512, :])
+        total = dot(jnp.concatenate(lhs + [window[...]], axis=1), jnp.concatenate([taps_ref[parity, base:, :], force_ref[r]], axis=0))
         total = (total + part_ref[r].astype(F32)).astype(ACT)
         act = (total + total * jnp.tanh(total)).astype(BF)
         value = x_ref[r].astype(F32) + dot(act, o_ref[0])
@@ -273,7 +266,7 @@
         copy.wait()
 
 
-def finish(where, xv, part, taps, mask, received, outer_weight, fluxes):
+def finish(where, xv, part, taps, force, mask, received, outer_weight, fluxes):
     rows, lon, channels = xv.shape
     hidden = part.shape[2]
     group = received[3].shape[0]
@@ -282,7 +275,7 @@
         grid_spec=pltpu.PrefetchScalarGridSpec(
             num_scalar_prefetch=1,
             grid=(1,),
-            in_specs=[held()] * 8 + [
+            in_specs=[held()] * 9 + [
                 pl.BlockSpec((1, hidden, channels), lambda r, s: (s[0], 0, 0)),
             ],
             out_specs=pl.BlockSpec(memory_space=pltpu.HBM),
@@ -297,7 +290,7 @@
         compiler_params=limits(20),
         name="finish_rows",
     )(
-        where, xv, part, taps, mask, *received, outer_weight
+        where, xv, part, taps, force, mask, *received, outer_weight
     )
 
 
@@ -316,7 +309,10 @@
     def send(block, target):
         return lax.ppermute(block, "lat", [(i, target(i) % count) for i in range(count)])
 
-    pack, xv, pair, chip, mask = surfaces(where, state, surface_proj, wet_mask, group)
+    pack, xv, pair, chip, mask, force, inner = surfaces(
+        where, state, surface_proj, wet_mask, forcing_in, jnp.transpose(margin_rows, (2, 0, 1)),
+        jnp.transpose(margin_weights, (2, 0, 1)), inner_weight, group,
+    )
     pair = send(pair, lambda i: i + 1 - 2 * (i % 2))
     links = [(i, (i + (1 if i % 2 else -1)) % count) for i in range(count)]
     far = send(pack, lambda i: i + half + (1 if i % 2 else -1))
@@ -324,10 +320,8 @@
     near, chip = lax.optimization_barrier((near, chip))
     near = send(near, lambda i: i + half)
     chip = lax.ppermute(chip, "lat", [(i, j) for i, j in links if component(i) == component(j)])
-    part, taps = partials(where, xv, inner_weight, forcing_in, margin_rows, margin_weights)
-    return finish(
-        where, xv, part, taps, mask, (pair, chip, near, far), outer_weight, forcing_in.shape[1]
-    )
+    part, taps = partials(xv, inner)
+    return finish(where, xv, part, taps, force, mask, (pair, chip, near, far), outer_weight, forcing_in.shape[1])
 
 
 def solution(mesh):

time: 35.6 us -> 34 us (0.955)
  the two profiles are of different devices: /device:TPU:0 before, /device:TPU:18 now
where the time goes in v6:
time: 34 us; the launch traced here: 33.8 us
  Pallas kernels  23.2 us (68%)
  starting transfers between devices  7.29 us (21%)
  waiting for transfers between devices  3.03 us (9%)
    pallas_call x1, Pallas kernels, partials(): pl.pallas_call(functools.partial(partial_kernel, rows // 2, lon), in_spec...  10.7 us
    pallas_call x1, Pallas kernels, finish(): pl.pallas_call(functools.partial(finish_kernel, rows, lon, group, fluxes)...  8.93 us
    ppermute x1, starting transfers between devices, shards(): lax.ppermute(chip, 'lat', [(i, j) for i, j in links if component(i) == co...  4.18 us
    pallas_call x1, Pallas kernels, surfaces(): pl.pallas_call(functools.partial(surface_kernel, rows, lon, group, fluxes...  3.6 us
    ppermute x3, starting transfers between devices, send(): lax.ppermute(block, 'lat', [(i, target(i) % count) for i in range(count)])  3.11 us
    ppermute x1, waiting for transfers between devices, shards(): lax.ppermute(chip, 'lat', [(i, j) for i, j in links if component(i) == co...  3.02 us
  transfers between devices with their start and end apart: 4, of which 1 were waited for; matrix products, arithmetic and copies ran while one was open for 0% of the time, Pallas kernels for 32%

profile of v6, /device:TPU:18, one launch (start us, length us, event | category | flops | bytes accessed | tf_op | source)
XLA Modules:
  0.0 33.8 jit_solution(6897873472678334379)
XLA Ops:
  0.0 3.6 %surface_fields.1 = (bf16[384,128]{1,0:T(8,128)(2,1)S(1)}, bf16[8,1440,128]{2,1,0:T(8,128)(2,1)S(1)}, bf16[1824,128]{1,0:T(8,128)(2,1)S(1)}, bf16[1440,128]{1,0:...) custom-call(s32[2]{0:T(128)S(1)} %compare_select_fusion.where, ...), custom_call_target="tpu_custom_call" | custom-call | tf_op jit(solution)/shard_map/surface_fields/pallas_call | solution.py:122
  3.6 0.1 collective-permute-start
  3.7 2.6 %collective-permute-start.3 = (bf16[384,128]{1,0:T(8,128)(2,1)S(1)}, bf16[384,128]{1,0:T(8,128)(2,1)S(1)}, u32[]{:S(2)}, u32[]{:S(2)}) collective-permute-start(bf16[384,128]{1,0:T(8,128)(2,1)S(1)} %get-tuple-element.23), channel_id=1, source_target_pairs={{0,7},{1,10},{2,9},{3,12},{4,11},{5,14},{6,13},{7,0},{8,15},{9,2},... | collective-permute-start | bytes 294920 | tf_op jit(solution)/shard_map/ppermute | solution.py:310
  6.3 0.0 collective-permute-done.pair_ref
  6.4 0.4 %collective-permute-start.2 = (bf16[768,128]{1,0:T(8,128)(2,1)S(1)}, bf16[768,128]{1,0:T(8,128)(2,1)S(1)}, u32[]{:S(2)}, u32[]{:S(2)}) collective-permute-start(bf16[768,128]{1,0:T(8,128)(2,1)S(1)} %pad_maximum_fusion), channel_id=1, source_target_pairs={{0,8},{1,9},{2,10},{3,11},{4,12},{5,13},{6,14},{7,15},{8,0},{9,1},... | collective-permute-start | bytes 589832 | tf_op jit(solution)/shard_map/ppermute | solution.py:310
  6.8 4.2 %collective-permute-start.1 = (bf16[1440,128]{1,0:T(8,128)(2,1)S(1)}, bf16[1440,128]{1,0:T(8,128)(2,1)S(1)}, u32[]{:S(2)}, u32[]{:S(2)}) collective-permute-start(bf16[1440,128]{1,0:T(8,128)(2,1)S(1)} %get-tuple-element.25), channel_id=1, source_target_pairs={{0,15},{1,2},{2,1},{5,6},{6,5},{7,8},{8,7},{9,10},{10,9},{13,14},{... | collective-permute-start | bytes 1105928 | tf_op jit(solution)/shard_map/ppermute | solution.py:322
  11.0 0.0 copy-start
  11.0 10.7 %own_rows.1 = (bf16[8,1440,512]{2,1,0:T(8,128)(2,1)S(1)}, bf16[2,384,512]{2,1,0:T(8,128)(2,1)S(1)}) custom-call(bf16[8,1440,128]{2,1,0:T(8,128)(2,1)S(1)} %get-tuple-element.16.x_ref, bf16[1152,512]{1,0:T(8,128)(2,1)S(1)} %get-tuple-element.17.w_ref), custom_call_target="tpu_custom_call" | custom-call | flops 9059696640 | bytes 17694720 | tf_op jit(solution)/shard_map/own_rows/pallas_call | solution.py:199
  21.6 0.0 collective-permute-done.3.far_ref
  21.7 0.0 collective-permute-done.2.near_ref
  21.7 3.0 %collective-permute-done.1.chip_ref = bf16[1440,128]{1,0:T(8,128)(2,1)S(1)} collective-permute-done((bf16[1440,128]{1,0:T(8,128)(2,1)S(1)}, bf16[1440,128]{1,0:T(8,128)(2,1)S(1)}, u32[]{:S(2)}, u32[]{:S(2)}) %collective-permute-start.1) | collective-permute-done | bytes 368672 | tf_op jit(solution)/shard_map/ppermute | solution.py:322
  24.7 0.0 copy-done
  24.7 8.9 %finish_rows.1 = bf16[8,1440,128]{2,1,0:T(8,128)(2,1)} custom-call(s32[2]{0:T(128)S(1)} %compare_select_fusion.where, bf16[8,1440,128]{2,1,0:T(8,128)(2,1)S(1)} %get-tuple-element.16.x_ref, bf16[8,1440,512]{2,1,0:T(8,128)(2,1)S(1)} %get-tuple-element.18.part_ref, bf16[2,384,512]{2,1,0:T(8,128)(2,1)S(1)} %get-tuple-element.19.taps_ref, ...), custom_call_target="tpu_custom_call" | custom-call | tf_op jit(solution)/shard_map/finish_rows/pallas_call | solution.py:273
  (3 shorter events, 0.0 us)
Async XLA Ops:
  3.6 2.7 %collective-permute-start = (bf16[1824,128]{1,0:T(8,128)(2,1)S(1)}, bf16[1824,128]{1,0:T(8,128)(2,1)S(1)}, u32[]{:S(2)}, u32[]{:S(2)}) collective-permute-start(bf16[1824,128]{1,0:T(8,128)(2,1)S(1)} %get-tuple-element.22), channel_id=1, source_target_pairs={{0,1},{1,0},{2,3},{3,2},{4,5},{5,4},{6,7},{7,6},{8,9},{9,8},{10,11... | collective-permute-start | bytes 1400840 | tf_op jit(solution)/shard_map/ppermute | solution.py:310
  3.7 18.0 %collective-permute-start.3 = (bf16[384,128]{1,0:T(8,128)(2,1)S(1)}, bf16[384,128]{1,0:T(8,128)(2,1)S(1)}, u32[]{:S(2)}, u32[]{:S(2)}) collective-permute-start(bf16[384,128]{1,0:T(8,128)(2,1)S(1)} %get-tuple-element.23), channel_id=1, source_target_pairs={{0,7},{1,10},{2,9},{3,12},{4,11},{5,14},{6,13},{7,0},{8,15},{9,2},... | collective-permute-start | bytes 294920 | tf_op jit(solution)/shard_map/ppermute | solution.py:310
  6.4 15.3 %collective-permute-start.2 = (bf16[768,128]{1,0:T(8,128)(2,1)S(1)}, bf16[768,128]{1,0:T(8,128)(2,1)S(1)}, u32[]{:S(2)}, u32[]{:S(2)}) collective-permute-start(bf16[768,128]{1,0:T(8,128)(2,1)S(1)} %pad_maximum_fusion), channel_id=1, source_target_pairs={{0,8},{1,9},{2,10},{3,11},{4,12},{5,13},{6,14},{7,15},{8,0},{9,1},... | collective-permute-start | bytes 589832 | tf_op jit(solution)/shard_map/ppermute | solution.py:310
  6.8 17.9 %collective-permute-start.1 = (bf16[1440,128]{1,0:T(8,128)(2,1)S(1)}, bf16[1440,128]{1,0:T(8,128)(2,1)S(1)}, u32[]{:S(2)}, u32[]{:S(2)}) collective-permute-start(bf16[1440,128]{1,0:T(8,128)(2,1)S(1)} %get-tuple-element.25), channel_id=1, source_target_pairs={{0,15},{1,2},{2,1},{5,6},{6,5},{7,8},{8,7},{9,10},{10,9},{13,14},{... | collective-permute-start | bytes 1105928 | tf_op jit(solution)/shard_map/ppermute | solution.py:322
  11.0 13.7 %copy-start = (bf16[2,512,128]{2,1,0:T(8,128)(2,1)S(1)}, bf16[2,512,128]{2,1,0:T(8,128)(2,1)}, u32[]{:S(2)}) copy-start(bf16[2,512,128]{2,1,0:T(8,128)(2,1)} %o_ref.1) | copy-start | bytes 786436

commit v7 on v6

--- a/solution.py
+++ b/solution.py
@@ -188,9 +188,11 @@
             return [tf[slot, p, 7 : 7 + lon, :].astype(BF), tf[slot, p, 9 : 9 + lon, :].astype(BF)]
 
         m1 = dot(jnp.concatenate(sides(1), axis=1), wm[0])
+        y0 = dot(jnp.concatenate(sides(0) + own, axis=1), wy[0]) + m1
+        y1 = dot(jnp.concatenate(sides(3) + own, axis=1), wy[1]) + m1
         m2 = dot(jnp.concatenate(sides(2), axis=1), wm[1])
-        out_ref[2 * pair] = (dot(jnp.concatenate(sides(0) + own, axis=1), wy[0]) + (m1 + m2)).astype(BF)
-        out_ref[2 * pair + 1] = (dot(jnp.concatenate(sides(3) + own, axis=1), wy[1]) + (m1 - m2)).astype(BF)
+        out_ref[2 * pair] = (y0 + m2).astype(BF)
+        out_ref[2 * pair + 1] = (y1 - m2).astype(BF)
 
 
 def partials(xv, inner):

time: 34 us -> 34 us (level)
  transfers between devices with their start and end apart: 4 -> 4, of which waited for: 1 -> 1; matrix products, arithmetic and copies ran while one was open for 0% -> 0% of each run, Pallas kernels for 32% -> 31%
where the time goes in v7:
time: 34 us; the launch traced here: 33.8 us
  Pallas kernels  22.9 us (67%)
  starting transfers between devices  7.29 us (21%)
  waiting for transfers between devices  3.3 us (10%)
    pallas_call x1, Pallas kernels, partials(): pl.pallas_call(functools.partial(partial_kernel, rows // 2, lon), in_spec...  10.4 us
    pallas_call x1, Pallas kernels, finish(): pl.pallas_call(functools.partial(finish_kernel, rows, lon, group, fluxes)...  8.93 us
    ppermute x1, starting transfers between devices, shards(): lax.ppermute(chip, 'lat', [(i, j) for i, j in links if component(i) == co...  4.18 us
    pallas_call x1, Pallas kernels, surfaces(): pl.pallas_call(functools.partial(surface_kernel, rows, lon, group, fluxes...  3.6 us
    ppermute x1, waiting for transfers between devices, shards(): lax.ppermute(chip, 'lat', [(i, j) for i, j in links if component(i) == co...  3.29 us
    ppermute x3, starting transfers between devices, send(): lax.ppermute(block, 'lat', [(i, target(i) % count) for i in range(count)])  3.11 us
  transfers between devices with their start and end apart: 4, of which 1 were waited for; matrix products, arithmetic and copies ran while one was open for 0% of the time, Pallas kernels for 31%

profile of v7, /device:TPU:18, one launch (start us, length us, event | category | flops | bytes accessed | tf_op | source)
XLA Modules:
  0.0 33.8 jit_solution(7195290281608993719)
XLA Ops:
  0.0 3.6 %surface_fields.1 = (bf16[384,128]{1,0:T(8,128)(2,1)S(1)}, bf16[8,1440,128]{2,1,0:T(8,128)(2,1)S(1)}, bf16[1824,128]{1,0:T(8,128)(2,1)S(1)}, bf16[1440,128]{1,0:...) custom-call(s32[2]{0:T(128)S(1)} %compare_select_fusion.where, ...), custom_call_target="tpu_custom_call" | custom-call | tf_op jit(solution)/shard_map/surface_fields/pallas_call | solution.py:122
  3.6 0.1 collective-permute-start
  3.7 2.6 %collective-permute-start.3 = (bf16[384,128]{1,0:T(8,128)(2,1)S(1)}, bf16[384,128]{1,0:T(8,128)(2,1)S(1)}, u32[]{:S(2)}, u32[]{:S(2)}) collective-permute-start(bf16[384,128]{1,0:T(8,128)(2,1)S(1)} %get-tuple-element.23), channel_id=1, source_target_pairs={{0,7},{1,10},{2,9},{3,12},{4,11},{5,14},{6,13},{7,0},{8,15},{9,2},... | collective-permute-start | bytes 294920 | tf_op jit(solution)/shard_map/ppermute | solution.py:312
  6.3 0.0 collective-permute-done.pair_ref
  6.4 0.4 %collective-permute-start.2 = (bf16[768,128]{1,0:T(8,128)(2,1)S(1)}, bf16[768,128]{1,0:T(8,128)(2,1)S(1)}, u32[]{:S(2)}, u32[]{:S(2)}) collective-permute-start(bf16[768,128]{1,0:T(8,128)(2,1)S(1)} %pad_maximum_fusion), channel_id=1, source_target_pairs={{0,8},{1,9},{2,10},{3,11},{4,12},{5,13},{6,14},{7,15},{8,0},{9,1},... | collective-permute-start | bytes 589832 | tf_op jit(solution)/shard_map/ppermute | solution.py:312
  6.8 4.2 %collective-permute-start.1 = (bf16[1440,128]{1,0:T(8,128)(2,1)S(1)}, bf16[1440,128]{1,0:T(8,128)(2,1)S(1)}, u32[]{:S(2)}, u32[]{:S(2)}) collective-permute-start(bf16[1440,128]{1,0:T(8,128)(2,1)S(1)} %get-tuple-element.25), channel_id=1, source_target_pairs={{0,15},{1,2},{2,1},{5,6},{6,5},{7,8},{8,7},{9,10},{10,9},{13,14},{... | collective-permute-start | bytes 1105928 | tf_op jit(solution)/shard_map/ppermute | solution.py:324
  11.0 0.0 copy-start
  11.0 10.4 %own_rows.1 = (bf16[8,1440,512]{2,1,0:T(8,128)(2,1)S(1)}, bf16[2,384,512]{2,1,0:T(8,128)(2,1)S(1)}) custom-call(bf16[8,1440,128]{2,1,0:T(8,128)(2,1)S(1)} %get-tuple-element.16.x_ref, bf16[1152,512]{1,0:T(8,128)(2,1)S(1)} %get-tuple-element.17.w_ref), custom_call_target="tpu_custom_call" | custom-call | flops 9059696640 | bytes 17694720 | tf_op jit(solution)/shard_map/own_rows/pallas_call | solution.py:201
  21.4 0.0 collective-permute-done.3.far_ref
  21.4 0.0 collective-permute-done.2.near_ref
  21.4 3.3 %collective-permute-done.1.chip_ref = bf16[1440,128]{1,0:T(8,128)(2,1)S(1)} collective-permute-done((bf16[1440,128]{1,0:T(8,128)(2,1)S(1)}, bf16[1440,128]{1,0:T(8,128)(2,1)S(1)}, u32[]{:S(2)}, u32[]{:S(2)}) %collective-permute-start.1) | collective-permute-done | bytes 368672 | tf_op jit(solution)/shard_map/ppermute | solution.py:324
  24.7 0.0 copy-done
  24.7 8.9 %finish_rows.1 = bf16[8,1440,128]{2,1,0:T(8,128)(2,1)} custom-call(s32[2]{0:T(128)S(1)} %compare_select_fusion.where, bf16[8,1440,128]{2,1,0:T(8,128)(2,1)S(1)} %get-tuple-element.16.x_ref, bf16[8,1440,512]{2,1,0:T(8,128)(2,1)S(1)} %get-tuple-element.18.part_ref, bf16[2,384,512]{2,1,0:T(8,128)(2,1)S(1)} %get-tuple-element.19.taps_ref, ...), custom_call_target="tpu_custom_call" | custom-call | tf_op jit(solution)/shard_map/finish_rows/pallas_call | solution.py:275
  (3 shorter events, 0.0 us)
Async XLA Ops:
  3.6 2.7 %collective-permute-start = (bf16[1824,128]{1,0:T(8,128)(2,1)S(1)}, bf16[1824,128]{1,0:T(8,128)(2,1)S(1)}, u32[]{:S(2)}, u32[]{:S(2)}) collective-permute-start(bf16[1824,128]{1,0:T(8,128)(2,1)S(1)} %get-tuple-element.22), channel_id=1, source_target_pairs={{0,1},{1,0},{2,3},{3,2},{4,5},{5,4},{6,7},{7,6},{8,9},{9,8},{10,11... | collective-permute-start | bytes 1400840 | tf_op jit(solution)/shard_map/ppermute | solution.py:312
  3.7 17.7 %collective-permute-start.3 = (bf16[384,128]{1,0:T(8,128)(2,1)S(1)}, bf16[384,128]{1,0:T(8,128)(2,1)S(1)}, u32[]{:S(2)}, u32[]{:S(2)}) collective-permute-start(bf16[384,128]{1,0:T(8,128)(2,1)S(1)} %get-tuple-element.23), channel_id=1, source_target_pairs={{0,7},{1,10},{2,9},{3,12},{4,11},{5,14},{6,13},{7,0},{8,15},{9,2},... | collective-permute-start | bytes 294920 | tf_op jit(solution)/shard_map/ppermute | solution.py:312
  6.4 15.0 %collective-permute-start.2 = (bf16[768,128]{1,0:T(8,128)(2,1)S(1)}, bf16[768,128]{1,0:T(8,128)(2,1)S(1)}, u32[]{:S(2)}, u32[]{:S(2)}) collective-permute-start(bf16[768,128]{1,0:T(8,128)(2,1)S(1)} %pad_maximum_fusion), channel_id=1, source_target_pairs={{0,8},{1,9},{2,10},{3,11},{4,12},{5,13},{6,14},{7,15},{8,0},{9,1},... | collective-permute-start | bytes 589832 | tf_op jit(solution)/shard_map/ppermute | solution.py:312
  6.8 17.9 %collective-permute-start.1 = (bf16[1440,128]{1,0:T(8,128)(2,1)S(1)}, bf16[1440,128]{1,0:T(8,128)(2,1)S(1)}, u32[]{:S(2)}, u32[]{:S(2)}) collective-permute-start(bf16[1440,128]{1,0:T(8,128)(2,1)S(1)} %get-tuple-element.25), channel_id=1, source_target_pairs={{0,15},{1,2},{2,1},{5,6},{6,5},{7,8},{8,7},{9,10},{10,9},{13,14},{... | collective-permute-start | bytes 1105928 | tf_op jit(solution)/shard_map/ppermute | solution.py:324
  11.0 13.7 %copy-start = (bf16[2,512,128]{2,1,0:T(8,128)(2,1)S(1)}, bf16[2,512,128]{2,1,0:T(8,128)(2,1)}, u32[]{:S(2)}) copy-start(bf16[2,512,128]{2,1,0:T(8,128)(2,1)} %o_ref.1) | copy-start | bytes 786436

commit v8 on v6

--- a/solution.py
+++ b/solution.py
@@ -101,8 +101,7 @@
         packed += pltpu.roll(part, rows * fluxes * g, 1) if g else part
     packed = packed.astype(BF)
     out_ref[...] = packed
-    pair_ref[0:lon, :] = xv_ref[jnp.where(even, rows - 1, 0)]
-    pair_ref[lon : lon + group, :] = packed
+    pair_ref[...] = xv_ref[jnp.where(even, rows - 1, 0)]
     chip_ref[...] = xv_ref[jnp.where(even, 0, rows - 1)]
     inner.wait()
 
@@ -138,7 +137,7 @@
         out_shape=[
             pltpu.VMEM((group, 128), BF),
             pltpu.VMEM((rows, lon, channels), BF),
-            pltpu.VMEM((lon + group, channels), BF),
+            pltpu.VMEM((lon, channels), BF),
             pltpu.VMEM((lon, channels), BF),
             pltpu.VMEM((lon, 128), BF),
             pltpu.VMEM((rows, 128, hidden), BF),
@@ -243,7 +242,7 @@
         edge = r in (0, rows - 1)
         base = 0 if edge else 256
         if r == 0:
-            swap = pair_ref[0:lon, :].astype(F32)
+            swap = pair_ref[...].astype(F32)
             chip = chip_ref[...].astype(F32)
             for e, v in enumerate((jnp.where(even, chip, swap), jnp.where(even, swap, chip))):
                 halo[e, 8 : 8 + lon, :] = v
@@ -313,13 +312,14 @@
         where, state, surface_proj, wet_mask, forcing_in, jnp.transpose(margin_rows, (2, 0, 1)),
         jnp.transpose(margin_weights, (2, 0, 1)), inner_weight, group,
     )
-    pair = send(pair, lambda i: i + 1 - 2 * (i % 2))
+    partner = send(pack, lambda i: i + 1 - 2 * (i % 2))
     links = [(i, (i + (1 if i % 2 else -1)) % count) for i in range(count)]
     far = send(pack, lambda i: i + half + (1 if i % 2 else -1))
-    near = jnp.concatenate([pack, pair[lon:]], axis=0)
-    near, chip = lax.optimization_barrier((near, chip))
+    near = jnp.concatenate([pack, partner], axis=0)
+    near, chip, pair = lax.optimization_barrier((near, chip, pair))
     near = send(near, lambda i: i + half)
     chip = lax.ppermute(chip, "lat", [(i, j) for i, j in links if component(i) == component(j)])
+    pair = send(pair, lambda i: i + 1 - 2 * (i % 2))
     part, taps = partials(xv, inner)
     return finish(where, xv, part, taps, force, mask, (pair, chip, near, far), outer_weight, forcing_in.shape[1])
 

time: 34 us -> 34.8 us (1.024)
  the two profiles are of different devices: /device:TPU:18 before, /device:TPU:0 now
where the time goes in v8:
time: 34.8 us; the launch traced here: 34.6 us
  Pallas kernels  23.2 us (67%)
  starting transfers between devices  11.1 us (32%)
    pallas_call x1, Pallas kernels, partials(): pl.pallas_call(functools.partial(partial_kernel, rows // 2, lon), in_spec...  10.7 us
    pallas_call x1, Pallas kernels, finish(): pl.pallas_call(functools.partial(finish_kernel, rows, lon, group, fluxes)...  8.93 us
    ppermute x4, starting transfers between devices, send(): lax.ppermute(block, 'lat', [(i, target(i) % count) for i in range(count)])  6.82 us
    ppermute x1, starting transfers between devices, shards(): lax.ppermute(chip, 'lat', [(i, j) for i, j in links if component(i) == co...  4.31 us
    pallas_call x1, Pallas kernels, surfaces(): pl.pallas_call(functools.partial(surface_kernel, rows, lon, group, fluxes...  3.6 us
  transfers between devices with their start and end apart: 5, of which 0 were waited for; matrix products, arithmetic and copies ran while one was open for 0% of the time, Pallas kernels for 31%

profile of v8, /device:TPU:0, one launch (start us, length us, event | category | flops | bytes accessed | tf_op | source)
XLA Modules:
  0.0 34.6 jit_solution(10587645777034254945)
XLA Ops:
  0.0 3.6 %surface_fields.1 = (bf16[384,128]{1,0:T(8,128)(2,1)S(1)}, bf16[8,1440,128]{2,1,0:T(8,128)(2,1)S(1)}, bf16[1440,128]{1,0:T(8,128)(2,1)S(1)}, bf16[1440,128]{1,0:...) custom-call(s32[2]{0:T(128)S(1)} %compare_select_fusion.where, ...), custom_call_target="tpu_custom_call" | custom-call | tf_op jit(solution)/shard_map/surface_fields/pallas_call | solution.py:121
  3.6 0.5 %collective-permute-start = (bf16[384,128]{1,0:T(8,128)(2,1)S(1)}, bf16[384,128]{1,0:T(8,128)(2,1)S(1)}, u32[]{:S(2)}, u32[]{:S(2)}) collective-permute-start(bf16[384,128]{1,0:T(8,128)(2,1)S(1)} %get-tuple-element.23), channel_id=1, source_target_pairs={{0,1},{1,0},{2,3},{3,2},{4,5},{5,4},{6,7},{7,6},{8,9},{9,8},{10,11... | collective-permute-start | bytes 294920 | tf_op jit(solution)/shard_map/ppermute | solution.py:309
  4.1 3.6 %collective-permute-start.4 = (bf16[384,128]{1,0:T(8,128)(2,1)S(1)}, bf16[384,128]{1,0:T(8,128)(2,1)S(1)}, u32[]{:S(2)}, u32[]{:S(2)}) collective-permute-start(bf16[384,128]{1,0:T(8,128)(2,1)S(1)} %get-tuple-element.23), channel_id=1, source_target_pairs={{0,7},{1,10},{2,9},{3,12},{4,11},{5,14},{6,13},{7,0},{8,15},{9,2},... | collective-permute-start | bytes 294920 | tf_op jit(solution)/shard_map/ppermute | solution.py:309
  7.8 0.0 collective-permute-done
  7.8 2.7 %collective-permute-start.3 = (bf16[768,128]{1,0:T(8,128)(2,1)S(1)}, bf16[768,128]{1,0:T(8,128)(2,1)S(1)}, u32[]{:S(2)}, u32[]{:S(2)}) collective-permute-start(bf16[768,128]{1,0:T(8,128)(2,1)S(1)} %pad_maximum_fusion), channel_id=1, source_target_pairs={{0,8},{1,9},{2,10},{3,11},{4,12},{5,13},{6,14},{7,15},{8,0},{9,1},... | collective-permute-start | bytes 589832 | tf_op jit(solution)/shard_map/ppermute | solution.py:309
  10.4 0.0 collective-permute-start.1
  10.4 4.3 %collective-permute-start.2 = (bf16[1440,128]{1,0:T(8,128)(2,1)S(1)}, bf16[1440,128]{1,0:T(8,128)(2,1)S(1)}, u32[]{:S(2)}, u32[]{:S(2)}) collective-permute-start(bf16[1440,128]{1,0:T(8,128)(2,1)S(1)} %get-tuple-element.27), channel_id=1, source_target_pairs={{0,15},{1,2},{2,1},{5,6},{6,5},{7,8},{8,7},{9,10},{10,9},{13,14},{... | collective-permute-start | bytes 1105928 | tf_op jit(solution)/shard_map/ppermute | solution.py:321
  14.8 0.0 copy-start
  14.8 10.7 %own_rows.1 = (bf16[8,1440,512]{2,1,0:T(8,128)(2,1)S(1)}, bf16[2,384,512]{2,1,0:T(8,128)(2,1)S(1)}) custom-call(bf16[8,1440,128]{2,1,0:T(8,128)(2,1)S(1)} %get-tuple-element.17.x_ref, bf16[1152,512]{1,0:T(8,128)(2,1)S(1)} %get-tuple-element.18.w_ref), custom_call_target="tpu_custom_call" | custom-call | flops 9059696640 | bytes 17694720 | tf_op jit(solution)/shard_map/own_rows/pallas_call | solution.py:198
  25.5 0.0 collective-permute-done.4.far_ref
  25.5 0.0 collective-permute-done.3.near_ref
  25.5 0.0 collective-permute-done.1.pair_ref
  25.5 0.0 collective-permute-done.2.chip_ref
  25.5 0.0 copy-done
  25.5 8.9 %finish_rows.1 = bf16[8,1440,128]{2,1,0:T(8,128)(2,1)} custom-call(s32[2]{0:T(128)S(1)} %compare_select_fusion.where, bf16[8,1440,128]{2,1,0:T(8,128)(2,1)S(1)} %get-tuple-element.17.x_ref, bf16[8,1440,512]{2,1,0:T(8,128)(2,1)S(1)} %get-tuple-element.19.part_ref, bf16[2,384,512]{2,1,0:T(8,128)(2,1)S(1)} %get-tuple-element.20.taps_ref, ...), custom_call_target="tpu_custom_call" | custom-call | tf_op jit(solution)/shard_map/finish_rows/pallas_call | solution.py:272
  (2 shorter events, 0.0 us)
Async XLA Ops:
  3.6 4.2 %collective-permute-start = (bf16[384,128]{1,0:T(8,128)(2,1)S(1)}, bf16[384,128]{1,0:T(8,128)(2,1)S(1)}, u32[]{:S(2)}, u32[]{:S(2)}) collective-permute-start(bf16[384,128]{1,0:T(8,128)(2,1)S(1)} %get-tuple-element.23), channel_id=1, source_target_pairs={{0,1},{1,0},{2,3},{3,2},{4,5},{5,4},{6,7},{7,6},{8,9},{9,8},{10,11... | collective-permute-start | bytes 294920 | tf_op jit(solution)/shard_map/ppermute | solution.py:309
  4.1 21.3 %collective-permute-start.4 = (bf16[384,128]{1,0:T(8,128)(2,1)S(1)}, bf16[384,128]{1,0:T(8,128)(2,1)S(1)}, u32[]{:S(2)}, u32[]{:S(2)}) collective-permute-start(bf16[384,128]{1,0:T(8,128)(2,1)S(1)} %get-tuple-element.23), channel_id=1, source_target_pairs={{0,7},{1,10},{2,9},{3,12},{4,11},{5,14},{6,13},{7,0},{8,15},{9,2},... | collective-permute-start | bytes 294920 | tf_op jit(solution)/shard_map/ppermute | solution.py:309
  7.8 17.7 %collective-permute-start.3 = (bf16[768,128]{1,0:T(8,128)(2,1)S(1)}, bf16[768,128]{1,0:T(8,128)(2,1)S(1)}, u32[]{:S(2)}, u32[]{:S(2)}) collective-permute-start(bf16[768,128]{1,0:T(8,128)(2,1)S(1)} %pad_maximum_fusion), channel_id=1, source_target_pairs={{0,8},{1,9},{2,10},{3,11},{4,12},{5,13},{6,14},{7,15},{8,0},{9,1},... | collective-permute-start | bytes 589832 | tf_op jit(solution)/shard_map/ppermute | solution.py:309
  10.4 15.0 %collective-permute-start.1 = (bf16[1440,128]{1,0:T(8,128)(2,1)S(1)}, bf16[1440,128]{1,0:T(8,128)(2,1)S(1)}, u32[]{:S(2)}, u32[]{:S(2)}) collective-permute-start(bf16[1440,128]{1,0:T(8,128)(2,1)S(1)} %get-tuple-element.26), channel_id=1, source_target_pairs={{0,1},{1,0},{2,3},{3,2},{4,5},{5,4},{6,7},{7,6},{8,9},{9,8},{10,11... | collective-permute-start | bytes 1105928 | tf_op jit(solution)/shard_map/ppermute | solution.py:309
  10.4 15.0 %collective-permute-start.2 = (bf16[1440,128]{1,0:T(8,128)(2,1)S(1)}, bf16[1440,128]{1,0:T(8,128)(2,1)S(1)}, u32[]{:S(2)}, u32[]{:S(2)}) collective-permute-start(bf16[1440,128]{1,0:T(8,128)(2,1)S(1)} %get-tuple-element.27), channel_id=1, source_target_pairs={{0,15},{1,2},{2,1},{5,6},{6,5},{7,8},{8,7},{9,10},{10,9},{13,14},{... | collective-permute-start | bytes 1105928 | tf_op jit(solution)/shard_map/ppermute | solution.py:321
  14.8 10.7 %copy-start = (bf16[2,512,128]{2,1,0:T(8,128)(2,1)S(1)}, bf16[2,512,128]{2,1,0:T(8,128)(2,1)}, u32[]{:S(2)}) copy-start(bf16[2,512,128]{2,1,0:T(8,128)(2,1)} %o_ref.1) | copy-start | bytes 786436
